TPU v7x, 32 devices: a whole 2x2x4 slice. The times are simulated.
32 devices in a mesh: row: 8 (over z, core), col: 4 (over y, x).
Axes of the slice: x: 2, y: 2, z: 4, core: 2. Of those that a mesh axis runs over, the one named last changes fastest.
Arguments:
- inputs: bfloat16 [8192, 2048], P('row', 'col'), may hold values from -6 to 6
- cotangent: bfloat16 [8192, 2048], P('row', 'col'), may hold values from -6 to 6
- lengths: int32 [2, 8], replicated, may hold values from 1 to 512, 2048 in all within a row
- query_key_value_weight: bfloat16 [2048, 3, 2048], P('row', None, 'col'), may hold values from -0.1875 to 0.1875
- out_weight: bfloat16 [2048, 2048], P('col', 'row'), may hold values from -1 to 1
- gate_weight: bfloat16 [2048, 8192], P('row', 'col'), may hold values from -0.125 to 0.125
- up_weight: bfloat16 [2048, 8192], P('row', 'col'), may hold values from -0.125 to 0.125
- down_weight: bfloat16 [8192, 2048], P('col', 'row'), may hold values from -0.09375 to 0.09375
Outputs:
- output: bfloat16 [8192, 2048], P('row', 'col')
- input_grad: float32 [8192, 2048], P('row', 'col')
- qkv_grad: float32 [2048, 3, 2048], P('row', None, 'col')
- out_grad: float32 [2048, 2048], P('col', 'row')
- gate_grad: float32 [2048, 8192], P('row', 'col')
- up_grad: float32 [2048, 8192], P('row', 'col')
- down_grad: float32 [8192, 2048], P('col', 'row')
Inputs may be any that keep to these rules, and one draw needn't show every extreme that they name: `lengths`: row g gives, in order, the tokens of the 8 continuations of group g; each row sums to 2048 and its largest entry is 512.
All inputs are finite; a program needn't handle non-finite values.
Results may differ from a plain program's by a relative error of at most 0.02.
Values may be sent and summed in bfloat16 or wider, within the bound.
A program may use at most 256 MiB of HBM per device.

v0:
```python
import math

import jax
import jax.numpy as jnp
from jax import lax
from jax.sharding import PartitionSpec as P

HEAD = 128
PROMPT = 2048
GROUP_LEN = 4096


rope_base = 10000.0
norm_eps = 1e-05
masked_score = -1e30


def passed_along(shard, axis, by):
    size = lax.axis_size(axis)
    pairs = [(i, i + by) for i in range(size) if 0 <= i + by < size]
    return lax.ppermute(shard, axis, pairs)


def normalize_rows(values):
    centre = values - jnp.mean(values, axis=-1, keepdims=True)
    spread = jnp.mean(centre * centre, axis=-1, keepdims=True)
    inverse = lax.rsqrt(spread + norm_eps)
    return (centre * inverse, inverse)


def normalize_back(grad_rows, sum_grad, sum_cross, unit_rows, inverse, row_width):
    return inverse * (grad_rows - sum_grad / row_width - unit_rows * (sum_cross / row_width))


def spread_cols(values, copies):
    return jnp.broadcast_to(values[:, None], (values.shape[0], copies))


def token_layout(lengths, source_row, groups_count, row_count):
    valid_source = source_row >= 0
    safe_source = jnp.maximum(source_row, 0)
    group_id = jnp.where(valid_source, safe_source % groups_count, -1)
    place_here = safe_source // groups_count
    safe_group = jnp.clip(group_id, 0, lengths.shape[0] - 1)
    row_lengths = lax.dynamic_slice_in_dim(lengths, safe_group, 1, 0)[0]
    local_index = place_here * row_count + jnp.arange(row_count, dtype=jnp.int32)
    after_prompt = local_index - PROMPT
    seg_ends = jnp.cumsum(row_lengths)
    in_prompt = local_index < PROMPT
    counted = jnp.sum((after_prompt[:, None] >= seg_ends[None, :]).astype(jnp.int32), axis=1)
    segment = jnp.where(in_prompt, 0, 1 + counted)
    seg_starts = seg_ends - row_lengths
    picked = (segment - 1)[:, None] == jnp.arange(row_lengths.shape[0], dtype=jnp.int32)[None, :]
    seg_start = jnp.sum(jnp.where(picked, seg_starts[None, :], 0), axis=1)
    position = jnp.where(in_prompt, local_index, PROMPT + after_prompt - seg_start)
    return (group_id, local_index, segment, position)


def rotation_angles(position, head_size):
    half_size = head_size // 2
    frequency = jnp.exp(
        -math.log(rope_base) * (2.0 * jnp.arange(half_size, dtype=jnp.float32) / head_size)
    )
    angles = position.astype(jnp.float32)[:, None] * frequency[None, :]
    return (jnp.cos(angles)[:, None, :], jnp.sin(angles)[:, None, :])


def rotate(values, cosine, sine, inverse_turn):
    half_size = values.shape[-1] // 2
    first_half = values[..., :half_size]
    second_half = values[..., half_size:]
    if inverse_turn:
        sine = -sine
    return jnp.concatenate(
        [first_half * cosine - second_half * sine, second_half * cosine + first_half * sine],
        axis=-1,
    )


def visible_mask(query_meta, key_meta):
    query_group, query_index, query_segment, query_position = query_meta
    key_group, key_index, key_segment, key_position = key_meta
    causal = key_index[None, :] <= query_index[:, None]
    shared = (key_segment[None, :] == 0) | (key_segment[None, :] == query_segment[:, None])
    return (query_group == key_group) & causal & shared


def score_block(queries, key_part, allowed, score_scale):
    raw_scores = (
        jnp.einsum("qhd,khd->hqk", queries, key_part, preferred_element_type=jnp.float32)
        * score_scale
    )
    return jnp.where(allowed[None], raw_scores, masked_score)


def body(
    inputs,
    cotangent,
    lengths,
    query_key_value_weight,
    out_weight,
    gate_weight,
    up_weight,
    down_weight,
):
    tok_rows = inputs.shape[0]
    part_width = inputs.shape[1]
    col_count = lax.axis_size("col")
    col_index = lax.axis_index("col")
    row_index = lax.axis_index("row")
    full_width = float(part_width * col_count)
    group_span = GROUP_LEN // tok_rows
    groups_here = lax.axis_size("row") // group_span
    head_size = HEAD
    heads_here = part_width // head_size
    score_scale = head_size ** (-0.5)
    block_place = row_index // groups_here
    full_inputs, full_cotangent = (
        lax.all_gather(inputs, "col", axis=1, tiled=True),
        lax.all_gather(cotangent, "col", axis=1, tiled=True),
    )
    projection_full_rows, out_full, gate_full, up_full, down_full = (
        lax.all_gather(query_key_value_weight, "row", axis=0, tiled=True),
        lax.all_gather(out_weight, "row", axis=1, tiled=True),
        lax.all_gather(gate_weight, "row", axis=0, tiled=True),
        lax.all_gather(up_weight, "row", axis=0, tiled=True),
        lax.all_gather(down_weight, "row", axis=1, tiled=True),
    )
    unit_one, inverse_one = normalize_rows(full_inputs.astype(jnp.float32))
    first_normed_input = unit_one.astype(jnp.bfloat16)
    raw_projection_output = jnp.einsum(
        "cu,ufk->cfk", first_normed_input, projection_full_rows, preferred_element_type=jnp.float32
    )
    raw_projection_output = raw_projection_output.reshape(tok_rows, 3, heads_here, head_size)
    own_meta = token_layout(lengths, row_index, groups_here, tok_rows)
    cosine, sine = rotation_angles(own_meta[3], head_size)
    queries = rotate(raw_projection_output[:, 0], cosine, sine, False).astype(jnp.bfloat16)
    key_rows = rotate(raw_projection_output[:, 1], cosine, sine, False).astype(jnp.bfloat16)
    value_rows = raw_projection_output[:, 2].astype(jnp.bfloat16)
    pieces = [(key_rows, value_rows)]
    for shift_by in range(1, group_span):
        pieces.append(passed_along((key_rows, value_rows), "row", shift_by * groups_here))
    visibility = [
        visible_mask(
            own_meta,
            token_layout(lengths, row_index - shift_by * groups_here, groups_here, tok_rows),
        )
        for shift_by in range(group_span)
    ]
    live_piece = [shift_by <= block_place for shift_by in range(group_span)]
    first_scores = score_block(queries, pieces[0][0], visibility[0], score_scale)
    top_rows = jnp.max(first_scores, axis=-1, keepdims=True)
    total_rows = jnp.sum(jnp.exp(first_scores - top_rows), axis=-1, keepdims=True)
    for shift_by in range(1, group_span):

        def add_stats(carry, shift_by=shift_by):
            old_top, old_total = carry
            scores = score_block(queries, pieces[shift_by][0], visibility[shift_by], score_scale)
            new_top = jnp.maximum(old_top, jnp.max(scores, axis=-1, keepdims=True))
            new_total = old_total * jnp.exp(old_top - new_top) + jnp.sum(
                jnp.exp(scores - new_top), axis=-1, keepdims=True
            )
            return (new_top, new_total)

        top_rows, total_rows = lax.cond(
            live_piece[shift_by], add_stats, lambda carry: carry, (top_rows, total_rows)
        )
    log_total = top_rows + jnp.log(total_rows)
    attended = jnp.zeros((tok_rows, heads_here, head_size), jnp.float32)
    for shift_by in range(group_span):

        def add_values(total, shift_by=shift_by):
            scores = score_block(queries, pieces[shift_by][0], visibility[shift_by], score_scale)
            probs_low = jnp.exp(scores - log_total).astype(jnp.bfloat16)
            return total + jnp.einsum(
                "hqk,khd->qhd", probs_low, pieces[shift_by][1], preferred_element_type=jnp.float32
            )

        attended = lax.cond(live_piece[shift_by], add_values, lambda total: total, attended)
    attended_flat = attended.reshape(tok_rows, part_width).astype(jnp.bfloat16)
    branch_terms = jnp.dot(attended_flat, out_full, preferred_element_type=jnp.float32)
    branch_full = lax.psum(branch_terms, "col")
    middle_full = full_inputs.astype(jnp.float32) + branch_full
    middle = lax.dynamic_slice_in_dim(middle_full, col_index * part_width, part_width, 1)
    unit_two, inverse_two = normalize_rows(middle_full)
    normed_two = unit_two.astype(jnp.bfloat16)
    gate = jnp.dot(normed_two, gate_full, preferred_element_type=jnp.float32)
    up_proj = jnp.dot(normed_two, up_full, preferred_element_type=jnp.float32)
    sigmoid_gate = jax.nn.sigmoid(gate)
    silu_gate = gate * sigmoid_gate
    hidden = (silu_gate * up_proj).astype(jnp.bfloat16)
    ffn_terms = jnp.dot(hidden, down_full, preferred_element_type=jnp.float32)
    ffn_part = lax.psum_scatter(
        ffn_terms.astype(jnp.bfloat16), "col", scatter_dimension=1, tiled=True
    ).astype(jnp.float32)
    output = (middle + ffn_part).astype(jnp.bfloat16)
    projection_full_rows, out_full, gate_full, up_full, down_full = (
        lax.all_gather(query_key_value_weight, "row", axis=0, tiled=True),
        lax.all_gather(out_weight, "row", axis=1, tiled=True),
        lax.all_gather(gate_weight, "row", axis=0, tiled=True),
        lax.all_gather(up_weight, "row", axis=0, tiled=True),
        lax.all_gather(down_weight, "row", axis=1, tiled=True),
    )
    d_hidden = jnp.einsum(
        "td,fd->tf", full_cotangent, down_full, preferred_element_type=jnp.float32
    )
    down_part = jnp.einsum("tf,td->fd", hidden, full_cotangent, preferred_element_type=jnp.float32)
    d_gate = (d_hidden * up_proj * sigmoid_gate * (1.0 + gate * (1.0 - sigmoid_gate))).astype(
        jnp.bfloat16
    )
    d_up = (d_hidden * silu_gate).astype(jnp.bfloat16)
    gate_part = jnp.einsum("td,tf->df", normed_two, d_gate, preferred_element_type=jnp.float32)
    up_part = jnp.einsum("td,tf->df", normed_two, d_up, preferred_element_type=jnp.float32)
    d_normed_two = jnp.einsum(
        "tf,df->td", d_gate, gate_full, preferred_element_type=jnp.float32
    ) + jnp.einsum("tf,df->td", d_up, up_full, preferred_element_type=jnp.float32)
    grad_two, sum_two, cross_two = (
        lax.psum_scatter(
            d_normed_two.astype(jnp.bfloat16), "col", scatter_dimension=1, tiled=True
        ).astype(jnp.float32),
        lax.psum_scatter(
            spread_cols(jnp.sum(d_normed_two, axis=1), col_count).astype(jnp.bfloat16),
            "col",
            scatter_dimension=1,
            tiled=True,
        ).astype(jnp.float32),
        lax.psum_scatter(
            spread_cols(jnp.sum(d_normed_two * unit_two, axis=1), col_count).astype(jnp.bfloat16),
            "col",
            scatter_dimension=1,
            tiled=True,
        ).astype(jnp.float32),
    )
    unit_two_here = lax.dynamic_slice_in_dim(unit_two, col_index * part_width, part_width, 1)
    d_middle = cotangent.astype(jnp.float32) + normalize_back(
        grad_two, sum_two, cross_two, unit_two_here, inverse_two, full_width
    )
    d_branch = d_middle.astype(jnp.bfloat16)
    d_branch_full = lax.all_gather(d_branch, "col", axis=1, tiled=True)
    out_part = jnp.einsum(
        "tc,td->cd", attended_flat, d_branch_full, preferred_element_type=jnp.float32
    )
    d_attended = jnp.einsum(
        "td,cd->tc", d_branch_full, out_full, preferred_element_type=jnp.float32
    )
    d_attended = d_attended.astype(jnp.bfloat16).reshape(tok_rows, heads_here, head_size)
    delta_rows = jnp.zeros((heads_here, tok_rows, 1), jnp.float32)
    for shift_by in range(group_span):

        def add_delta(total, shift_by=shift_by):
            scores = score_block(queries, pieces[shift_by][0], visibility[shift_by], score_scale)
            probs_full = jnp.exp(scores - log_total)
            d_probs = jnp.einsum(
                "qhd,khd->hqk", d_attended, pieces[shift_by][1], preferred_element_type=jnp.float32
            )
            return total + jnp.sum(probs_full * d_probs, axis=-1, keepdims=True)

        delta_rows = lax.cond(live_piece[shift_by], add_delta, lambda total: total, delta_rows)
    zero_rows = jnp.zeros((tok_rows, heads_here, head_size), jnp.float32)
    d_queries = zero_rows
    for shift_by in range(group_span):

        def piece_grads(query_total, shift_by=shift_by):
            key_part, value_part = pieces[shift_by]
            scores = score_block(queries, key_part, visibility[shift_by], score_scale)
            probs_full = jnp.exp(scores - log_total)
            d_probs = jnp.einsum(
                "qhd,khd->hqk", d_attended, value_part, preferred_element_type=jnp.float32
            )
            d_scores = (probs_full * (d_probs - delta_rows)).astype(jnp.bfloat16)
            query_total = (
                query_total
                + jnp.einsum("hqk,khd->qhd", d_scores, key_part, preferred_element_type=jnp.float32)
                * score_scale
            )
            d_key_part = (
                jnp.einsum("hqk,qhd->khd", d_scores, queries, preferred_element_type=jnp.float32)
                * score_scale
            )
            d_value_part = jnp.einsum(
                "hqk,qhd->khd",
                probs_full.astype(jnp.bfloat16),
                d_attended,
                preferred_element_type=jnp.float32,
            )
            return (query_total, d_key_part, d_value_part)

        d_queries, d_key_part, d_value_part = lax.cond(
            live_piece[shift_by],
            piece_grads,
            lambda query_total: (query_total, zero_rows, zero_rows),
            d_queries,
        )
        if shift_by == 0:
            d_keys = d_key_part
            d_values = d_value_part
        else:
            back_keys, back_values = (
                passed_along(
                    d_key_part.astype(jnp.bfloat16), "row", -shift_by * groups_here
                ).astype(d_key_part.dtype),
                passed_along(
                    d_value_part.astype(jnp.bfloat16), "row", -shift_by * groups_here
                ).astype(d_value_part.dtype),
            )
            d_keys = d_keys + back_keys
            d_values = d_values + back_values
    raw_score_gradient = jnp.stack(
        [rotate(d_queries, cosine, sine, True), rotate(d_keys, cosine, sine, True), d_values],
        axis=1,
    )
    raw_score_gradient = raw_score_gradient.reshape(tok_rows, 3, part_width).astype(jnp.bfloat16)
    projection_part_rows = jnp.einsum(
        "lo,lbw->obw", first_normed_input, raw_score_gradient, preferred_element_type=jnp.float32
    )
    first_normed_gradient = jnp.einsum(
        "xzq,vzq->xv", raw_score_gradient, projection_full_rows, preferred_element_type=jnp.float32
    )
    grad_one, sum_one, cross_one = (
        lax.psum_scatter(
            first_normed_gradient.astype(jnp.bfloat16), "col", scatter_dimension=1, tiled=True
        ).astype(jnp.float32),
        lax.psum_scatter(
            spread_cols(jnp.sum(first_normed_gradient, axis=1), col_count).astype(jnp.bfloat16),
            "col",
            scatter_dimension=1,
            tiled=True,
        ).astype(jnp.float32),
        lax.psum_scatter(
            spread_cols(jnp.sum(first_normed_gradient * unit_one, axis=1), col_count).astype(
                jnp.bfloat16
            ),
            "col",
            scatter_dimension=1,
            tiled=True,
        ).astype(jnp.float32),
    )
    unit_one_here = lax.dynamic_slice_in_dim(unit_one, col_index * part_width, part_width, 1)
    input_grad = d_middle + normalize_back(
        grad_one, sum_one, cross_one, unit_one_here, inverse_one, full_width
    )
    owned_grads = (
        lax.psum_scatter(
            projection_part_rows.astype(jnp.bfloat16), "row", scatter_dimension=0, tiled=True
        ).astype(jnp.float32),
        lax.psum_scatter(
            out_part.astype(jnp.bfloat16), "row", scatter_dimension=1, tiled=True
        ).astype(jnp.float32),
        lax.psum_scatter(
            gate_part.astype(jnp.bfloat16), "row", scatter_dimension=0, tiled=True
        ).astype(jnp.float32),
        lax.psum_scatter(
            up_part.astype(jnp.bfloat16), "row", scatter_dimension=0, tiled=True
        ).astype(jnp.float32),
        lax.psum_scatter(
            down_part.astype(jnp.bfloat16), "row", scatter_dimension=1, tiled=True
        ).astype(jnp.float32),
    )
    return (
        output,
        input_grad,
        owned_grads[0],
        owned_grads[1],
        owned_grads[2],
        owned_grads[3],
        owned_grads[4],
    )


def solution(mesh):
    placed = (
        P("row", "col"),
        P("row", "col"),
        P(),
        P("row", None, "col"),
        P("col", "row"),
        P("row", "col"),
        P("row", "col"),
        P("col", "row"),
    )
    return jax.shard_map(
        body,
        mesh=mesh,
        in_specs=placed,
        out_specs=(
            P("row", "col"),
            P("row", "col"),
            P("row", None, "col"),
            P("col", "row"),
            P("row", "col"),
            P("row", "col"),
            P("col", "row"),
        ),
        check_vma=False,
    )
```

profile of v0, /device:TPU:0, one launch (start us, length us, event | category | flops | bytes accessed | tf_op | source)
XLA Modules:
  0.0 1676.3 jit_solution(3196764701043474098)
XLA Ops:
  16.9 48.2 %all-gather.9.cloned.1.call-done = bf16[1024,2048]{1,0:T(8,128)(2,1)} async-done(((bf16[1024,512]{1,0:T(8,128)(2,1)}), bf16[1024,2048]{1,0:T(8,128)(2,1)}) %all-gather.9.cloned.1.call-update) | async-done | bytes 4194320 | tf_op jit(solution)/shard_map/all_gather | solution.py:119
  71.4 61.1 %all-gather.11.cloned.1.call-done = bf16[2048,3,512]{0,2,1:T(8,128)(2,1)} async-done(((bf16[256,3,512]{0,2,1:T(8,128)(2,1)}), bf16[2048,3,512]{0,2,1:T(8,128)(2,1)}) %all-gather.11.cloned.1.call-update) | async-done | bytes 6291472 | tf_op jit(solution)/shard_map/all_gather | solution.py:123
  207.2 22.5 %collective-permute-done.2 = bf16[1024,4,128]{2,0,1:T(8,128)(2,1)S(1)} collective-permute-done((bf16[1024,4,128]{2,0,1:T(8,128)(2,1)}, bf16[1024,4,128]{2,0,1:T(8,128)(2,1)S(1)}, u32[]{:S(2)}, u32[]{:S(2)}) %collective-permute-start.2) | collective-permute-done | bytes 1048608 | tf_op jit(solution)/shard_map/ppermute | solution.py:21
  252.3 22.4 %collective-permute-done.4 = bf16[1024,4,128]{2,0,1:T(8,128)(2,1)} collective-permute-done((bf16[1024,4,128]{2,0,1:T(8,128)(2,1)}, bf16[1024,4,128]{2,0,1:T(8,128)(2,1)}, u32[]{:S(2)}, u32[]{:S(2)}) %collective-permute-start.4) | collective-permute-done | bytes 1048608 | tf_op jit(solution)/shard_map/ppermute | solution.py:21
  274.7 22.2 %collective-permute-done.5 = bf16[1024,4,128]{2,0,1:T(8,128)(2,1)} collective-permute-done((bf16[1024,4,128]{2,0,1:T(8,128)(2,1)}, bf16[1024,4,128]{2,0,1:T(8,128)(2,1)}, u32[]{:S(2)}, u32[]{:S(2)}) %collective-permute-start.5) | collective-permute-done | bytes 1048608 | tf_op jit(solution)/shard_map/ppermute | solution.py:21
  309.4 234.3 %all-reduce.8.cloned.1.call-done = f32[1024,2048]{1,0:T(8,128)} async-done(((f32[1024,2048]{1,0:T(8,128)}), f32[1024,2048]{1,0:T(8,128)}) %all-reduce.8.cloned.1.call-update) | async-done | bytes 8388624 | tf_op jit(solution)/shard_map/psum | solution.py:182
  558.3 69.7 %all-gather.15.cloned.1.call-done = bf16[2048,2048]{1,0:T(8,128)(2,1)} async-done(((bf16[256,2048]{1,0:T(8,128)(2,1)}), bf16[2048,2048]{1,0:T(8,128)(2,1)}) %all-gather.15.cloned.1.call-update) | async-done | bytes 8388624 | tf_op jit(solution)/shard_map/all_gather | solution.py:125
  642.5 67.6 %all-gather.17.cloned.1.call-done = bf16[2048,2048]{1,0:T(8,128)(2,1)} async-done(((bf16[256,2048]{1,0:T(8,128)(2,1)}), bf16[2048,2048]{1,0:T(8,128)(2,1)}) %all-gather.17.cloned.1.call-update) | async-done | bytes 8388624 | tf_op jit(solution)/shard_map/all_gather | solution.py:126
  724.7 38.6 %all-gather.21.cloned.1.call-done = bf16[1024,2048]{1,0:T(8,128)(2,1)} async-done(((bf16[1024,512]{1,0:T(8,128)(2,1)}), bf16[1024,2048]{1,0:T(8,128)(2,1)}) %all-gather.21.cloned.1.call-update) | async-done | bytes 4194320 | tf_op jit(solution)/shard_map/all_gather | solution.py:120
  763.3 84.2 %all-gather.19.cloned.1.call-done = bf16[2048,2048]{1,0:T(8,128)(2,1)} async-done(((bf16[2048,256]{1,0:T(8,128)(2,1)}), bf16[2048,2048]{1,0:T(8,128)(2,1)}) %all-gather.19.cloned.1.call-update) | async-done | bytes 8388624 | tf_op jit(solution)/shard_map/all_gather | solution.py:127
  847.5 21.9 %multiply_convert_fusion.4 = (bf16[1024,2048]{1,0:T(8,128)(2,1)}, bf16[1024,2048]{1,0:T(8,128)(2,1)}, bf16[1024,2048]{1,0:T(8,128)(2,1)}) fusion(f32[1024,2048]{1,0:T(8,128)} %fusion.97, f32[1024,2048]{1,0:T(8,128)} %fusion.98, bf16[1024,2048]{1,0:T(8,128)(2,1)} %all-gather.21.cloned.1.call-done, bf16[2048,2048]{1,0:T(8,128)(2,1)} %all-gather.19.cloned.1.call-done), kind=kOutput, calls=%fused_computation.96 | convolution fusion | flops 8621391872 | bytes 41943040 | tf_op jit(solution)/shard_map/td,fd->tf/dot_general | solution.py:204
  884.3 16.7 fusion.84
  901.7 16.5 all-reduce.5
  919.4 32.8 %reduce-scatter.11.cloned.1.call-done = bf16[1024,512]{1,0:T(8,128)(2,1)} async-done(((bf16[1024,2048]{1,0:T(8,128)(2,1)}), bf16[1024,512]{1,0:T(8,128)(2,1)}) %reduce-scatter.11.cloned.1.call-update) | async-done | bytes 1048592 | tf_op jit(solution)/shard_map/reduce_scatter | solution.py:218
  1019.9 23.2 %conditional.22 = (f32[4,1024,1]{1,0,2:T(4,128)S(1)}) conditional(s32[]{:T(128)} %convert_element_type.245, () %tuple.137, (pred[1024,1024]{1,0:T(8,128)(4,1)}, bf16[1024,4,128]{2,0,1:T(8,128)(2,1)S(1)}, bf16[1024,4,128]{2,0,1:T(8,128)(2,1)}, f32[4,1024,1]{1,0,2:T(4,128)S(1)}, bf16[1024,4,128]{0,2,1:T(8,128)(2,1)}, ...), branch_computations={%region_42.43_spmd, %region_43.45_spmd} | conditional | flops 2168451072 | bytes 40927240 | solution.py:258
  1045.1 43.7 %conditional.26 = (f32[1024,4,128]{2,0,1:T(8,128)S(1)}, f32[1024,4,128]{2,0,1:T(8,128)}, f32[1024,4,128]{2,0,1:T(8,128)}) conditional(s32[]{:T(128)} %convert_element_type.245, () %tuple.136, (pred[1024,1024]{1,0:T(8,128)(4,1)}, bf16[1024,4,128]{2,0,1:T(8,128)(2,1)S(1)}, bf16[1024,4,128]{2,0,1:T(8,128)(2,1)}, f32[4,1024,1]{1,0,2:T(4,128)S(1)}, ...), branch_computations={%region_54.55_spmd, %region_55.56_spmd} | conditional | flops 5411700736 | bytes 149995712 | solution.py:288
  1110.2 16.2 conditional.29
  1139.4 157.6 %collective-permute-done.8 = bf16[1024,4,128]{2,0,1:T(8,128)(2,1)} collective-permute-done((bf16[1024,4,128]{2,0,1:T(8,128)(2,1)}, bf16[1024,4,128]{2,0,1:T(8,128)(2,1)}, u32[]{:S(2)}, u32[]{:S(2)}) %collective-permute-start.8) | collective-permute-done | bytes 1048608 | tf_op jit(solution)/shard_map/ppermute | solution.py:21
  1309.7 73.0 %collective-permute-done.11 = bf16[1024,4,128]{2,0,1:T(8,128)(2,1)} collective-permute-done((bf16[1024,4,128]{2,0,1:T(8,128)(2,1)}, bf16[1024,4,128]{2,0,1:T(8,128)(2,1)}, u32[]{:S(2)}, u32[]{:S(2)}) %collective-permute-start.11) | collective-permute-done | bytes 1048608 | tf_op jit(solution)/shard_map/ppermute | solution.py:21
  1382.7 50.8 %collective-permute-done.10 = bf16[1024,4,128]{2,0,1:T(8,128)(2,1)} collective-permute-done((bf16[1024,4,128]{2,0,1:T(8,128)(2,1)}, bf16[1024,4,128]{2,0,1:T(8,128)(2,1)}, u32[]{:S(2)}, u32[]{:S(2)}) %collective-permute-start.10) | collective-permute-done | bytes 1048608 | tf_op jit(solution)/shard_map/ppermute | solution.py:21
  1468.3 15.3 all-reduce.4
  1496.9 43.8 %reduce-scatter.17.cloned.1.call-done = bf16[512,256]{1,0:T(8,128)(2,1)} async-done(((bf16[512,2048]{1,0:T(8,128)(2,1)}), bf16[512,256]{1,0:T(8,128)(2,1)}) %reduce-scatter.17.cloned.1.call-update) | async-done | bytes 262160 | tf_op jit(solution)/shard_map/reduce_scatter | solution.py:346
  1542.5 52.5 %reduce-scatter.13.cloned.1.call-done = bf16[1024,512]{1,0:T(8,128)(2,1)} async-done(((bf16[1024,2048]{1,0:T(8,128)(2,1)}), bf16[1024,512]{1,0:T(8,128)(2,1)}) %reduce-scatter.13.cloned.1.call-update) | async-done | bytes 1048592 | tf_op jit(solution)/shard_map/reduce_scatter | solution.py:320
  1599.3 67.8 %reduce-scatter.15.cloned.1.call-done = bf16[256,3,512]{2,0,1:T(8,128)(2,1)} async-done(((bf16[2048,3,512]{2,0,1:T(8,128)(2,1)}), bf16[256,3,512]{2,0,1:T(8,128)(2,1)}) %reduce-scatter.15.cloned.1.call-update) | async-done | bytes 786448 | tf_op jit(solution)/shard_map/reduce_scatter | solution.py:343
  (260 shorter events, 441.0 us)
Async XLA Ops:
  7.9 124.6 %all-gather.11.cloned.1.call-start = ((), (), s32[]{:S(2)}) async-start(), calls=%async_computation.9 | async-start | bytes 7077888 | tf_op jit(solution)/shard_map/all_gather | solution.py:123
  10.3 288.7 %all-gather.13.cloned.1.call-start = ((), (), s32[]{:S(2)}) async-start(), calls=%async_computation.10 | async-start | bytes 2359296 | tf_op jit(solution)/shard_map/all_gather | solution.py:124
  11.0 532.7 %all-reduce.8.cloned.1.call-start = ((), (), s32[]{:S(2)}) async-start(), calls=%async_computation.11 | async-start | bytes 16777216 | tf_op jit(solution)/shard_map/psum | solution.py:182
  180.1 94.6 %collective-permute-start.4 = (bf16[1024,4,128]{2,0,1:T(8,128)(2,1)}, bf16[1024,4,128]{2,0,1:T(8,128)(2,1)}, u32[]{:S(2)}, u32[]{:S(2)}) collective-permute-start(bf16[1024,4,128]{2,0,1:T(8,128)(2,1)} %bitcast.116), channel_id=1, source_target_pairs={{0,16},{4,20},{8,24},{12,28},{1,17},{5,21},{9,25},{13,29},{2,18},{... | collective-permute-start | bytes 3145736 | tf_op jit(solution)/shard_map/ppermute | solution.py:21
  189.5 107.4 %collective-permute-start.5 = (bf16[1024,4,128]{2,0,1:T(8,128)(2,1)}, bf16[1024,4,128]{2,0,1:T(8,128)(2,1)}, u32[]{:S(2)}, u32[]{:S(2)}) collective-permute-start(bf16[1024,4,128]{2,0,1:T(8,128)(2,1)} %bitcast.116), channel_id=1, source_target_pairs={{0,24},{4,28},{1,25},{5,29},{2,26},{6,30},{3,27},{7,31}} | collective-permute-start | bytes 3145736 | tf_op jit(solution)/shard_map/ppermute | solution.py:21
  306.7 321.3 %all-gather.15.cloned.1.call-start = ((), (), s32[]{:S(2)}) async-start(), calls=%async_computation.12 | async-start | bytes 9437184 | tf_op jit(solution)/shard_map/all_gather | solution.py:125
  307.3 402.9 %all-gather.17.cloned.1.call-start = ((), (), s32[]{:S(2)}) async-start(), calls=%async_computation.13 | async-start | bytes 9437184 | tf_op jit(solution)/shard_map/all_gather | solution.py:126
  307.8 455.4 %all-gather.21.cloned.1.call-start = ((), (), s32[]{:S(2)}) async-start(), calls=%async_computation.16 | async-start | bytes 5242880 | tf_op jit(solution)/shard_map/all_gather | solution.py:120
  308.6 538.9 %all-gather.19.cloned.1.call-start = ((), (), s32[]{:S(2)}) async-start(), calls=%async_computation.14 | async-start | bytes 9437184 | tf_op jit(solution)/shard_map/all_gather | solution.py:127
  309.3 642.9 %reduce-scatter.11.cloned.1.call-start = ((), (), s32[]{:S(2)}) async-start(), calls=%async_computation.17 | async-start | bytes 5242880 | tf_op jit(solution)/shard_map/reduce_scatter | solution.py:218
  901.0 111.9 %all-gather.23.cloned.1.call-start = ((), (), s32[]{:S(2)}) async-start(), calls=%async_computation.18 | async-start | bytes 5242880 | tf_op jit(solution)/shard_map/all_gather | solution.py:239
  955.7 509.2 %reduce-scatter.9.cloned.1.call-start = ((), (), s32[]{:S(2)}) async-start(), calls=%async_computation.15 | async-start | bytes 5242880 | tf_op jit(solution)/shard_map/reduce_scatter | solution.py:193
  969.6 515.2 %reduce-scatter.21.cloned.1.call-start = ((), (), s32[]{:S(2)}) async-start(), calls=%async_computation.23 | async-start | bytes 9437184 | tf_op jit(solution)/shard_map/reduce_scatter | solution.py:352
  984.1 503.5 %reduce-scatter.19.cloned.1.call-start = ((), (), s32[]{:S(2)}) async-start(), calls=%async_computation.22 | async-start | bytes 9437184 | tf_op jit(solution)/shard_map/reduce_scatter | solution.py:349
  998.5 495.7 %reduce-scatter.23.cloned.1.call-start = ((), (), s32[]{:S(2)}) async-start(), calls=%async_computation.24 | async-start | bytes 9437184 | tf_op jit(solution)/shard_map/reduce_scatter | solution.py:355
  1012.8 527.9 %reduce-scatter.17.cloned.1.call-start = ((), (), s32[]{:S(2)}) async-start(), calls=%async_computation.21 | async-start | bytes 2359296 | tf_op jit(solution)/shard_map/reduce_scatter | solution.py:346
  1126.4 170.5 %collective-permute-start.8 = (bf16[1024,4,128]{2,0,1:T(8,128)(2,1)}, bf16[1024,4,128]{2,0,1:T(8,128)(2,1)}, u32[]{:S(2)}, u32[]{:S(2)}) collective-permute-start(bf16[1024,4,128]{2,0,1:T(8,128)(2,1)} %get-tuple-element.387), channel_id=1, source_target_pairs={{24,0},{28,4},{25,1},{29,5},{26,2},{30,6},{27,3},{31,7}} | collective-permute-start | bytes 3145736 | tf_op jit(solution)/shard_map/ppermute | solution.py:21
  1127.7 170.5 %collective-permute-start.7 = (bf16[1024,4,128]{2,0,1:T(8,128)(2,1)}, bf16[1024,4,128]{2,0,1:T(8,128)(2,1)}, u32[]{:S(2)}, u32[]{:S(2)}) collective-permute-start(bf16[1024,4,128]{2,0,1:T(8,128)(2,1)} %get-tuple-element.386), channel_id=1, source_target_pairs={{16,0},{20,4},{24,8},{28,12},{17,1},{21,5},{25,9},{29,13},{18,2},{... | collective-permute-start | bytes 3145736 | tf_op jit(solution)/shard_map/ppermute | solution.py:21
  1129.1 169.2 %collective-permute-start.6 = (bf16[1024,4,128]{2,0,1:T(8,128)(2,1)}, bf16[1024,4,128]{2,0,1:T(8,128)(2,1)}, u32[]{:S(2)}, u32[]{:S(2)}) collective-permute-start(bf16[1024,4,128]{2,0,1:T(8,128)(2,1)} %get-tuple-element.385), channel_id=1, source_target_pairs={{8,0},{12,4},{16,8},{20,12},{24,16},{28,20},{9,1},{13,5},{17,9},{2... | collective-permute-start | bytes 3145736 | tf_op jit(solution)/shard_map/ppermute | solution.py:21
  1136.7 458.4 %reduce-scatter.13.cloned.1.call-start = ((), (), s32[]{:S(2)}) async-start(), calls=%async_computation.19 | async-start | bytes 5242880 | tf_op jit(solution)/shard_map/reduce_scatter | solution.py:320
  1136.8 245.9 %collective-permute-start.11 = (bf16[1024,4,128]{2,0,1:T(8,128)(2,1)}, bf16[1024,4,128]{2,0,1:T(8,128)(2,1)}, u32[]{:S(2)}, u32[]{:S(2)}) collective-permute-start(bf16[1024,4,128]{2,0,1:T(8,128)(2,1)} %get-tuple-element.391), channel_id=1, source_target_pairs={{24,0},{28,4},{25,1},{29,5},{26,2},{30,6},{27,3},{31,7}} | collective-permute-start | bytes 3145736 | tf_op jit(solution)/shard_map/ppermute | solution.py:21
  1138.1 295.4 %collective-permute-start.10 = (bf16[1024,4,128]{2,0,1:T(8,128)(2,1)}, bf16[1024,4,128]{2,0,1:T(8,128)(2,1)}, u32[]{:S(2)}, u32[]{:S(2)}) collective-permute-start(bf16[1024,4,128]{2,0,1:T(8,128)(2,1)} %get-tuple-element.390), channel_id=1, source_target_pairs={{16,0},{20,4},{24,8},{28,12},{17,1},{21,5},{25,9},{29,13},{18,2},{... | collective-permute-start | bytes 3145736 | tf_op jit(solution)/shard_map/ppermute | solution.py:21
  1297.0 136.5 %collective-permute-start.9 = (bf16[1024,4,128]{2,0,1:T(8,128)(2,1)}, bf16[1024,4,128]{2,0,1:T(8,128)(2,1)}, u32[]{:S(2)}, u32[]{:S(2)}) collective-permute-start(bf16[1024,4,128]{2,0,1:T(8,128)(2,1)} %get-tuple-element.389), channel_id=1, source_target_pairs={{8,0},{12,4},{16,8},{20,12},{24,16},{28,20},{9,1},{13,5},{17,9},{2... | collective-permute-start | bytes 3145736 | tf_op jit(solution)/shard_map/ppermute | solution.py:21
  1452.4 214.7 %reduce-scatter.15.cloned.1.call-start = ((), (), s32[]{:S(2)}) async-start(), calls=%async_computation.20 | async-start | bytes 7077888 | tf_op jit(solution)/shard_map/reduce_scatter | solution.py:343
  (48 other events, 3025.3 us)
Sparse Core Ops, SparseCore 0:
  9.8 55.2 all-gather.8
  67.3 65.1 all-gather.10
  134.1 30.9 all-gather.12
  306.8 236.8 all-reduce.7
  545.2 82.7 all-gather.14
  629.5 80.5 all-gather.16
  712.1 51.0 all-gather.20
  764.9 82.4 all-gather.18
  901.1 51.0 reduce-scatter.10
  955.8 52.5 all-gather.22
  1011.4 52.6 reduce-scatter.8
  1066.3 89.5 reduce-scatter.20
  1158.3 159.1 reduce-scatter.18
  1319.8 174.3 reduce-scatter.22
  1497.0 43.6 reduce-scatter.16
  1543.9 51.1 reduce-scatter.12
  1597.2 69.7 reduce-scatter.14
where the time goes:
time: 1690 us; the launch traced here: 1680 us
  waiting for transfers between devices  1180 us (70%)
  matrix products  272 us (16%)
  other arithmetic  79.1 us (5%)
  local copies, waits for them, and re-layouts  40.9 us (2%)
  loops' own time  32.3 us (2%)
  blocking collectives  31.8 us (2%)
  starting transfers between devices  23.6 us (1%)
    ppermute x12, waiting for transfers between devices, passed_along(): return lax.ppermute(shard, axis, pairs)  373 us
    psum x1, waiting for transfers between devices, body(): branch_full = lax.psum(branch_terms, 'col')  234 us
    all_gather x1, waiting for transfers between devices, body(): lax.all_gather(down_weight, 'row', axis=1, tiled=True)  84.2 us
    all_gather x1, waiting for transfers between devices, body(): lax.all_gather(gate_weight, 'row', axis=0, tiled=True)  69.7 us
    reduce_scatter x1, waiting for transfers between devices, body(): lax.psum_scatter(projection_part_rows.astype(jnp.bfloat16), 'row', scatte...  67.8 us
    all_gather x1, waiting for transfers between devices, body(): lax.all_gather(up_weight, 'row', axis=0, tiled=True)  67.6 us
    all_gather x1, waiting for transfers between devices, body(): lax.all_gather(query_key_value_weight, 'row', axis=0, tiled=True)  61.1 us
    reduce_scatter x1, waiting for transfers between devices, body(): lax.psum_scatter(first_normed_gradient.astype(jnp.bfloat16), 'col', scatt...  52.5 us
  transfers between devices with their start and end apart: 29, of which 20 were waited for; matrix products, arithmetic and copies ran while one was open for 19% of the time, Pallas kernels for 0%

commit v1 on v0

--- a/solution.py
+++ b/solution.py
@@ -1,8 +1,11 @@
+import functools
 import math
 
 import jax
 import jax.numpy as jnp
 from jax import lax
+from jax.experimental import pallas as pl
+from jax.experimental.pallas import tpu as pltpu
 from jax.sharding import PartitionSpec as P
 
 HEAD = 128
@@ -91,6 +94,425 @@
         * score_scale
     )
     return jnp.where(allowed[None], raw_scores, masked_score)
+
+
+BLOCK = 512
+log2e = 1.4426950408889634
+
+
+def swap_col(shard, by):
+    size = lax.axis_size("col")
+    return lax.ppermute(shard, "col", [(i, i ^ by) for i in range(size)])
+
+
+def swap_place(shard, by, groups_here):
+    size = lax.axis_size("row")
+    pairs = [(i, (i // groups_here ^ by) * groups_here + i % groups_here) for i in range(size)]
+    return lax.ppermute(shard, "row", pairs)
+
+
+def gather_cols(shard, dim):
+    count = lax.axis_size("col")
+    index = lax.axis_index("col")
+    width = shard.shape[dim]
+    shape = list(shard.shape)
+    shape[dim] = width * count
+    full = jnp.zeros(shape, shard.dtype)
+    for by in range(count):
+        piece = shard if by == 0 else swap_col(shard, by)
+        full = lax.dynamic_update_slice_in_dim(full, piece, (index ^ by) * width, dim)
+    return full
+
+
+def scatter_cols(terms, width):
+    count = lax.axis_size("col")
+    index = lax.axis_index("col")
+    total = None
+    for by in range(count):
+        piece = lax.dynamic_slice_in_dim(terms, (index ^ by) * width, width, 1)
+        if by:
+            piece = swap_col(piece.astype(jnp.bfloat16), by)
+        piece = piece.astype(jnp.float32)
+        total = piece if total is None else total + piece
+    return total
+
+
+def sum_cols(values):
+    count = lax.axis_size("col")
+    total = values
+    for by in range(1, count):
+        total = total + swap_col(values, by)
+    return total
+
+
+def turn(values, cosine, sine):
+    return values * cosine + pltpu.roll(values, values.shape[1] // 2, 1) * sine
+
+
+def block_mask(key_block, query_block, start_row):
+    key_index = key_block * BLOCK + lax.broadcasted_iota(jnp.int32, (BLOCK, BLOCK), 0)
+    query_index = query_block * BLOCK + lax.broadcasted_iota(jnp.int32, (BLOCK, BLOCK), 1)
+    return (key_index <= query_index) & (key_index >= start_row)
+
+
+def each_block(block, visit):
+    prompt_blocks = PROMPT // BLOCK
+
+    def whole(j, carry):
+        visit(j, False)
+        return carry
+
+    lax.fori_loop(0, jnp.minimum(block, prompt_blocks), whole, 0)
+
+    @pl.when(block > prompt_blocks)
+    def _():
+        visit(block - 1, True)
+
+    visit(block, True)
+
+
+def attend_kernel(q_ref, k_ref, v_ref, start_ref, o_ref, lse_ref, top_ref, total_ref, sum_ref):
+    block = pl.program_id(1)
+    scale = HEAD**-0.5 * log2e
+    top_ref[...] = jnp.full_like(top_ref, masked_score)
+    total_ref[...] = jnp.zeros_like(total_ref)
+    sum_ref[...] = jnp.zeros_like(sum_ref)
+    queries = q_ref[0]
+    start_row = start_ref[0]
+
+    def visit(j, masked):
+        rows = pl.ds(pl.multiple_of(j * BLOCK, BLOCK), BLOCK)
+        scores = scale * lax.dot_general(
+            k_ref[0, rows, :], queries, (((1,), (1,)), ((), ())), preferred_element_type=jnp.float32
+        )
+        if masked:
+            scores = jnp.where(block_mask(j, block, start_row), scores, masked_score)
+        old_top = top_ref[...]
+        new_top = jnp.maximum(old_top, jnp.max(scores, axis=0, keepdims=True))
+        shrink = jnp.exp2(old_top - new_top)
+        probs = jnp.exp2(scores - new_top)
+        if masked:
+            probs = jnp.where(scores > 0.5 * masked_score, probs, 0.0)
+        total_ref[...] = total_ref[...] * shrink + jnp.sum(probs, axis=0, keepdims=True)
+        sum_ref[...] = sum_ref[...] * shrink + lax.dot_general(
+            v_ref[0, rows, :],
+            probs.astype(jnp.bfloat16),
+            (((0,), (0,)), ((), ())),
+            preferred_element_type=jnp.float32,
+        )
+        top_ref[...] = new_top
+
+    each_block(block, visit)
+    total = total_ref[...]
+    o_ref[0] = (sum_ref[...] / total).T.astype(jnp.bfloat16)
+    lse_ref[0, 0] = top_ref[...] + jnp.log2(total)
+
+
+def attend(queries, keys, values, start_rows):
+    heads, length, size = queries.shape
+    blocks = length // BLOCK
+    whole = pl.BlockSpec((1, length, size), lambda h, i: (h, 0, 0))
+    part = pl.BlockSpec((1, BLOCK, size), lambda h, i: (h, i, 0))
+    return pl.pallas_call(
+        attend_kernel,
+        grid=(heads, blocks),
+        in_specs=[part, whole, whole, pl.BlockSpec((1, 1, BLOCK), lambda h, i: (i, 0, 0))],
+        out_specs=[part, pl.BlockSpec((1, 1, 1, BLOCK), lambda h, i: (h, i, 0, 0))],
+        out_shape=[
+            jax.ShapeDtypeStruct((heads, length, size), jnp.bfloat16),
+            jax.ShapeDtypeStruct((heads, blocks, 1, BLOCK), jnp.float32),
+        ],
+        scratch_shapes=[
+            pltpu.VMEM((1, BLOCK), jnp.float32),
+            pltpu.VMEM((1, BLOCK), jnp.float32),
+            pltpu.VMEM((size, BLOCK), jnp.float32),
+        ],
+        compiler_params=pltpu.CompilerParams(vmem_limit_bytes=32 * 2**20),
+        cost_estimate=pl.CostEstimate(
+            flops=heads * length * length * size * 2, bytes_accessed=heads * length * size * 8,
+            transcendentals=heads * length * length // 2,
+        ),
+        name="attend",
+    )(queries, keys, values, start_rows)
+
+
+def attend_back_kernel(
+    q_ref, k_ref, v_ref, do_ref, o_ref, lse_ref, start_ref, cos_ref, sin_ref,
+    dq_ref, dk_ref, dv_ref, dq_sum, dk_sum, dv_sum,
+):
+    block = pl.program_id(1)
+    scale = HEAD**-0.5
+
+    @pl.when(block == 0)
+    def _():
+        dk_sum[...] = jnp.zeros_like(dk_sum)
+        dv_sum[...] = jnp.zeros_like(dv_sum)
+
+    dq_sum[...] = jnp.zeros_like(dq_sum)
+    queries = q_ref[0]
+    d_out = do_ref[0]
+    lse = lse_ref[0, 0]
+    start_row = start_ref[0]
+    delta = jnp.sum(
+        (d_out.astype(jnp.float32) * o_ref[0].astype(jnp.float32)).T, axis=0, keepdims=True
+    )
+
+    def visit(j, masked):
+        rows = pl.ds(pl.multiple_of(j * BLOCK, BLOCK), BLOCK)
+        key_part = k_ref[0, rows, :]
+        scores = (scale * log2e) * lax.dot_general(
+            key_part, queries, (((1,), (1,)), ((), ())), preferred_element_type=jnp.float32
+        )
+        if masked:
+            scores = jnp.where(block_mask(j, block, start_row), scores, masked_score)
+        probs = jnp.exp2(scores - lse)
+        d_probs = lax.dot_general(
+            v_ref[0, rows, :], d_out, (((1,), (1,)), ((), ())), preferred_element_type=jnp.float32
+        )
+        d_scores = (probs * (d_probs - delta)).astype(jnp.bfloat16)
+        dv_sum[rows, :] += jnp.dot(
+            probs.astype(jnp.bfloat16), d_out, preferred_element_type=jnp.float32
+        )
+        dk_sum[rows, :] += jnp.dot(d_scores, queries, preferred_element_type=jnp.float32)
+        dq_sum[...] += lax.dot_general(
+            key_part, d_scores, (((0,), (0,)), ((), ())), preferred_element_type=jnp.float32
+        )
+
+    each_block(block, visit)
+    here = pl.ds(pl.multiple_of(block * BLOCK, BLOCK), BLOCK)
+    dq_ref[0] = turn(dq_sum[...].T * scale, cos_ref[here, :], sin_ref[here, :]).astype(jnp.bfloat16)
+
+    @pl.when(block == pl.num_programs(1) - 1)
+    def _():
+        def finish(j, carry):
+            rows = pl.ds(pl.multiple_of(j * BLOCK, BLOCK), BLOCK)
+            dk_ref[0, rows, :] = turn(
+                dk_sum[rows, :] * scale, cos_ref[rows, :], sin_ref[rows, :]
+            ).astype(jnp.bfloat16)
+            dv_ref[0, rows, :] = dv_sum[rows, :].astype(jnp.bfloat16)
+            return carry
+
+        lax.fori_loop(0, dk_sum.shape[0] // BLOCK, finish, 0)
+
+
+def attend_back(queries, keys, values, d_out, out, lse, start_rows, cosine, sine):
+    heads, length, size = queries.shape
+    blocks = length // BLOCK
+    whole = pl.BlockSpec((1, length, size), lambda h, i: (h, 0, 0))
+    part = pl.BlockSpec((1, BLOCK, size), lambda h, i: (h, i, 0))
+    table = pl.BlockSpec((length, size), lambda h, i: (0, 0))
+    return pl.pallas_call(
+        attend_back_kernel,
+        grid=(heads, blocks),
+        in_specs=[
+            part, whole, whole, part, part,
+            pl.BlockSpec((1, 1, 1, BLOCK), lambda h, i: (h, i, 0, 0)),
+            pl.BlockSpec((1, 1, BLOCK), lambda h, i: (i, 0, 0)),
+            table, table,
+        ],
+        out_specs=[part, whole, whole],
+        out_shape=[jax.ShapeDtypeStruct((heads, length, size), jnp.bfloat16)] * 3,
+        scratch_shapes=[
+            pltpu.VMEM((size, BLOCK), jnp.float32),
+            pltpu.VMEM((length, size), jnp.float32),
+            pltpu.VMEM((length, size), jnp.float32),
+        ],
+        compiler_params=pltpu.CompilerParams(vmem_limit_bytes=48 * 2**20),
+        cost_estimate=pl.CostEstimate(
+            flops=heads * length * length * size * 5, bytes_accessed=heads * length * size * 16,
+            transcendentals=heads * length * length // 2,
+        ),
+        name="attend_back",
+    )(queries, keys, values, d_out, out, lse, start_rows, cosine, sine)
+
+
+def group_tables(lengths, group):
+    row_lengths = lax.dynamic_slice_in_dim(lengths, group, 1, 0)[0]
+    local_index = jnp.arange(GROUP_LEN, dtype=jnp.int32)
+    seg_ends = jnp.cumsum(row_lengths)
+    seg_starts = seg_ends - row_lengths
+    after_prompt = local_index - PROMPT
+    inside = (after_prompt[:, None] >= seg_starts[None, :]) & (
+        after_prompt[:, None] < seg_ends[None, :]
+    )
+    start = jnp.sum(jnp.where(inside, seg_starts[None, :], 0), axis=1)
+    in_prompt = local_index < PROMPT
+    start_row = jnp.where(in_prompt, 0, PROMPT + start)
+    position = jnp.where(in_prompt, local_index, PROMPT + after_prompt - start)
+    half = HEAD // 2
+    frequency = jnp.exp(
+        -math.log(rope_base) * (2.0 * jnp.arange(half, dtype=jnp.float32) / HEAD)
+    )
+    angles = position.astype(jnp.float32)[:, None] * frequency[None, :]
+    cosine, sine = jnp.cos(angles), jnp.sin(angles)
+    return (
+        start_row.reshape(GROUP_LEN // BLOCK, 1, BLOCK),
+        jnp.concatenate([cosine, cosine], axis=1),
+        jnp.concatenate([sine, -sine], axis=1),
+    )
+
+
+def to_heads(rows, span, place, groups_here):
+    heads, kinds, tokens, size = rows.shape
+    mine = heads // span
+    full = jnp.zeros((mine, kinds, span * tokens, size), rows.dtype)
+    for by in range(span):
+        piece = lax.dynamic_slice_in_dim(rows, (place ^ by) * mine, mine, 0)
+        if by:
+            piece = swap_place(piece, by, groups_here)
+        full = lax.dynamic_update_slice_in_dim(full, piece, (place ^ by) * tokens, 2)
+    return full
+
+
+def to_tokens(rows, span, place, groups_here):
+    mine, kinds, length, size = rows.shape
+    tokens = length // span
+    full = jnp.zeros((mine * span, kinds, tokens, size), rows.dtype)
+    for by in range(span):
+        piece = lax.dynamic_slice_in_dim(rows, (place ^ by) * tokens, tokens, 2)
+        if by:
+            piece = swap_place(piece, by, groups_here)
+        full = lax.dynamic_update_slice_in_dim(full, piece, (place ^ by) * mine, 0)
+    return full
+
+
+def fast_body(
+    inputs,
+    cotangent,
+    lengths,
+    query_key_value_weight,
+    out_weight,
+    gate_weight,
+    up_weight,
+    down_weight,
+):
+    tok_rows, part_width = inputs.shape
+    col_count = lax.axis_size("col")
+    col_index = lax.axis_index("col")
+    row_index = lax.axis_index("row")
+    full_width = float(part_width * col_count)
+    span = GROUP_LEN // tok_rows
+    groups_here = lax.axis_size("row") // span
+    heads_here = part_width // HEAD
+    place = row_index // groups_here
+    group = row_index % groups_here
+
+    def own_cols(values):
+        return lax.dynamic_slice_in_dim(values, col_index * part_width, part_width, 1)
+
+    projection = lax.all_gather(query_key_value_weight, "row", axis=0, tiled=True)
+    out_rows = lax.all_gather(out_weight, "row", axis=1, tiled=True)
+    gate_full = lax.all_gather(gate_weight, "row", axis=0, tiled=True)
+    up_full = lax.all_gather(up_weight, "row", axis=0, tiled=True)
+    down_full = lax.all_gather(down_weight, "row", axis=1, tiled=True)
+
+    full_inputs = gather_cols(inputs, 1)
+    full_cotangent = gather_cols(cotangent, 1)
+    out_full = gather_cols(out_rows, 0)
+
+    start_rows, cosine, sine = group_tables(lengths, group)
+    own_cos = lax.dynamic_slice_in_dim(cosine, place * tok_rows, tok_rows, 0)[:, : HEAD // 2]
+    own_sin = lax.dynamic_slice_in_dim(sine, place * tok_rows, tok_rows, 0)[:, : HEAD // 2]
+
+    unit_one, inverse_one = normalize_rows(full_inputs.astype(jnp.float32))
+    normed_one = unit_one.astype(jnp.bfloat16)
+    raw = jnp.einsum(
+        "cu,ufk->cfk", normed_one, projection, preferred_element_type=jnp.float32
+    ).reshape(tok_rows, 3, heads_here, HEAD)
+    own_cos, own_sin = own_cos[:, None, :], own_sin[:, None, :]
+    sent = jnp.stack(
+        [
+            rotate(raw[:, 0], own_cos, own_sin, False),
+            rotate(raw[:, 1], own_cos, own_sin, False),
+            raw[:, 2],
+        ],
+        axis=0,
+    ).astype(jnp.bfloat16)
+    sent = sent.transpose(2, 0, 1, 3)
+    held = to_heads(sent, span, place, groups_here)
+    queries, keys, values = held[:, 0], held[:, 1], held[:, 2]
+    attended_head, lse = attend(queries, keys, values, start_rows)
+    attended = to_tokens(attended_head[:, None], span, place, groups_here)[:, 0]
+    attended = attended.transpose(1, 0, 2).reshape(tok_rows, part_width)
+    attended_full = gather_cols(attended, 1)
+    middle_full = full_inputs.astype(jnp.float32) + jnp.dot(
+        attended_full, out_full, preferred_element_type=jnp.float32
+    )
+    middle = own_cols(middle_full)
+    unit_two, inverse_two = normalize_rows(middle_full)
+    normed_two = unit_two.astype(jnp.bfloat16)
+
+    gate = jnp.dot(normed_two, gate_full, preferred_element_type=jnp.float32)
+    up_proj = jnp.dot(normed_two, up_full, preferred_element_type=jnp.float32)
+    sigmoid_gate = jax.nn.sigmoid(gate)
+    silu_gate = gate * sigmoid_gate
+    hidden = (silu_gate * up_proj).astype(jnp.bfloat16)
+    d_hidden = jnp.einsum(
+        "td,fd->tf", full_cotangent, down_full, preferred_element_type=jnp.float32
+    )
+    d_gate = (d_hidden * up_proj * sigmoid_gate * (1.0 + gate * (1.0 - sigmoid_gate))).astype(
+        jnp.bfloat16
+    )
+    d_up = (d_hidden * silu_gate).astype(jnp.bfloat16)
+    d_normed_two = jnp.einsum(
+        "tf,df->td", d_gate, gate_full, preferred_element_type=jnp.float32
+    ) + jnp.einsum("tf,df->td", d_up, up_full, preferred_element_type=jnp.float32)
+    grad_two = scatter_cols(d_normed_two, part_width)
+    stats_two = sum_cols(
+        jnp.stack([jnp.sum(d_normed_two, axis=1), jnp.sum(d_normed_two * unit_two, axis=1)])
+    )
+    ffn_terms = jnp.dot(hidden, down_full, preferred_element_type=jnp.float32)
+    output = (middle + scatter_cols(ffn_terms, part_width)).astype(jnp.bfloat16)
+
+    down_part = jnp.einsum("tf,td->fd", hidden, full_cotangent, preferred_element_type=jnp.float32)
+    gate_part = jnp.einsum("td,tf->df", normed_two, d_gate, preferred_element_type=jnp.float32)
+    up_part = jnp.einsum("td,tf->df", normed_two, d_up, preferred_element_type=jnp.float32)
+
+    d_middle = cotangent.astype(jnp.float32) + normalize_back(
+        grad_two, stats_two[0][:, None], stats_two[1][:, None], own_cols(unit_two), inverse_two, full_width
+    )
+    d_branch_full = gather_cols(d_middle.astype(jnp.bfloat16), 1)
+    out_part = jnp.einsum("tc,td->cd", attended, d_branch_full, preferred_element_type=jnp.float32)
+    d_attended = jnp.einsum(
+        "td,cd->tc", d_branch_full, out_rows, preferred_element_type=jnp.float32
+    ).astype(jnp.bfloat16)
+    d_attended = d_attended.reshape(tok_rows, heads_here, HEAD).transpose(1, 0, 2)
+    d_head = to_heads(d_attended[:, None], span, place, groups_here)[:, 0]
+    d_queries, d_keys, d_values = attend_back(
+        queries, keys, values, d_head, attended_head, lse, start_rows, cosine, sine
+    )
+    d_raw = to_tokens(
+        jnp.stack([d_queries, d_keys, d_values], axis=1), span, place, groups_here
+    )
+    d_raw = d_raw.transpose(2, 1, 0, 3).reshape(tok_rows, 3, part_width)
+    projection_part = jnp.einsum(
+        "lo,lbw->obw", normed_one, d_raw, preferred_element_type=jnp.float32
+    )
+    d_normed_one = jnp.einsum(
+        "xzq,vzq->xv", d_raw, projection, preferred_element_type=jnp.float32
+    )
+    grad_one = scatter_cols(d_normed_one, part_width)
+    stats_one = sum_cols(
+        jnp.stack([jnp.sum(d_normed_one, axis=1), jnp.sum(d_normed_one * unit_one, axis=1)])
+    )
+    input_grad = d_middle + normalize_back(
+        grad_one, stats_one[0][:, None], stats_one[1][:, None], own_cols(unit_one), inverse_one, full_width
+    )
+
+    def owned(part, dim):
+        return lax.psum_scatter(
+            part.astype(jnp.bfloat16), "row", scatter_dimension=dim, tiled=True
+        ).astype(jnp.float32)
+
+    return (
+        output,
+        input_grad,
+        owned(projection_part, 0),
+        owned(out_part, 1),
+        owned(gate_part, 0),
+        owned(up_part, 0),
+        owned(down_part, 1),
+    )
 
 
 def body(
@@ -367,6 +789,12 @@
     )
 
 
+def step(inputs, *rest):
+    span = GROUP_LEN // inputs.shape[0]
+    heads_here = inputs.shape[1] // HEAD
+    return (body if heads_here % span else fast_body)(inputs, *rest)
+
+
 def solution(mesh):
     placed = (
         P("row", "col"),
@@ -379,7 +807,7 @@
         P("col", "row"),
     )
     return jax.shard_map(
-        body,
+        step,
         mesh=mesh,
         in_specs=placed,
         out_specs=(

time: 1690 us -> 1180 us (0.70)
  waiting for transfers between devices: 1180 us -> 568 us
  local copies, waits for them, and re-layouts: 40.9 us -> 172 us
  matrix products: 272 us -> 194 us
  starting transfers between devices: 23.6 us -> 96.7 us
  Pallas kernels: 0 us -> 60.3 us
  loops' own time: 32.3 us -> 0 us
  blocking collectives: 31.8 us -> 0 us
  other arithmetic: 79.1 us -> 56.2 us
    all_gather x8 -> x5, waiting for transfers between devices: 370 us -> 7.39 us  [the longest x1 7.36 us: fast_body(): lax.all_gather(query_key_value_weight, 'row', axis=0, tiled=True)]
    psum x1 -> x0, waiting for transfers between devices: 234 us -> none  [body(): branch_full = lax.psum(branch_terms, 'col')]
    dynamic_update_slice x0 -> x35, local copies, waits for them, and re-layouts: none -> 120 us  [the longest x8 87.3 us: to_tokens(): full = lax.dynamic_update_slice_in_dim(full, piece, (place ^ by) * mine, 0)]
    dot_general x24 -> x15, matrix products: 272 us -> 194 us  [the longest x1 21.8 us: fast_body(): jnp.einsum('td,fd->tf', full_cotangent, down_full, preferred_element_type...]
    ppermute x12 -> x42, starting transfers between devices: 22.7 us -> 95.9 us  [the longest x12 62 us: swap_place(): return lax.ppermute(shard, 'row', pairs)]
    pallas_call x0 -> x2, Pallas kernels: none -> 60.3 us  [the longest x1 35.2 us: attend_back(): pl.pallas_call(attend_back_kernel, grid=(heads, blocks), in_specs=[part,...]
    another operation x15 -> x0, loops' own time: 32.3 us -> none  [the longest x4 31.1 us: body(): lax.cond(live_piece[shift_by], piece_grads, lambda query_total: (query_to...]
    unnamed x2 -> x0, blocking collectives: 31.8 us -> none
  transfers between devices with their start and end apart: 29 -> 52, of which waited for: 20 -> 22; matrix products, arithmetic and copies ran while one was open for 19% -> 30% of each run, Pallas kernels for 0% -> 5%
where the time goes in v1:
time: 1180 us; the launch traced here: 1160 us
  waiting for transfers between devices  568 us (48%)
  matrix products  194 us (16%)
  local copies, waits for them, and re-layouts  172 us (15%)
  starting transfers between devices  96.7 us (8%)
  Pallas kernels  60.3 us (5%)
  other arithmetic  56.2 us (5%)
  between operations  15.7 us (1%)
    ppermute x30, waiting for transfers between devices, swap_col(): return lax.ppermute(shard, 'col', [(i, i ^ by) for i in range(size)])  199 us
    reduce_scatter x5, waiting for transfers between devices, owned(): lax.psum_scatter(part.astype(jnp.bfloat16), 'row', scatter_dimension=dim,...  196 us
    ppermute x12, waiting for transfers between devices, swap_place(): return lax.ppermute(shard, 'row', pairs)  164 us
    dynamic_update_slice x8, local copies, waits for them, and re-layouts, to_tokens(): full = lax.dynamic_update_slice_in_dim(full, piece, (place ^ by) * mine, 0)  87.3 us
    ppermute x12, starting transfers between devices, swap_place(): return lax.ppermute(shard, 'row', pairs)  62 us
    pallas_call x1, Pallas kernels, attend_back(): pl.pallas_call(attend_back_kernel, grid=(heads, blocks), in_specs=[part,...  35.2 us
    ppermute x30, starting transfers between devices, swap_col(): return lax.ppermute(shard, 'col', [(i, i ^ by) for i in range(size)])  33.9 us
    dynamic_update_slice x19, local copies, waits for them, and re-layouts, gather_cols(): lax.dynamic_update_slice_in_dim(full, piece, (index ^ by) * width, dim)  27.4 us
  transfers between devices with their start and end apart: 52, of which 22 were waited for; matrix products, arithmetic and copies ran while one was open for 30% of the time, Pallas kernels for 5%

profile of v1, /device:TPU:0, one launch (start us, length us, event | category | flops | bytes accessed | tf_op | source)
XLA Modules:
  0.0 1163.1 jit_solution(8506591289603366266)
XLA Ops:
  41.2 19.8 %collective-permute-done.1 = bf16[1024,512]{1,0:T(8,128)(2,1)} collective-permute-done((bf16[1024,512]{1,0:T(8,128)(2,1)S(1)}, bf16[1024,512]{1,0:T(8,128)(2,1)}, u32[]{:S(2)}, u32[]{:S(2)}) %collective-permute-start.1) | collective-permute-done | bytes 1048608 | tf_op jit(solution)/shard_map/ppermute | solution.py:105
  125.9 49.3 %collective-permute-done.3 = bf16[1,3,1024,128]{3,2,1,0:T(8,128)(2,1)} collective-permute-done((bf16[1,3,1024,128]{3,2,1,0:T(8,128)(2,1)}, bf16[1,3,1024,128]{3,2,1,0:T(8,128)(2,1)}, u32[]{:S(2)}, u32[]{:S(2)}) %collective-permute-start.3) | collective-permute-done | bytes 786464 | tf_op jit(solution)/shard_map/ppermute | solution.py:111
  180.4 24.4 %collective-permute-done.5 = bf16[1,3,1024,128]{3,2,1,0:T(8,128)(2,1)} collective-permute-done((bf16[1,3,1024,128]{3,2,1,0:T(8,128)(2,1)}, bf16[1,3,1024,128]{3,2,1,0:T(8,128)(2,1)}, u32[]{:S(2)}, u32[]{:S(2)}) %collective-permute-start.5) | collective-permute-done | bytes 786464 | tf_op jit(solution)/shard_map/ppermute | solution.py:111
  208.7 25.1 %attend.1 = (bf16[1,4096,128]{2,1,0:T(8,128)(2,1)S(1)}, f32[1,8,1,512]{3,2,1,0:T(1,128)S(1)}) custom-call(bf16[1,4096,128]{2,1,0:T(8,128)(2,1)S(1)} %get-tuple-element.47.q_ref, bf16[1,4096,128]{2,1,0:T(8,128)(2,1)S(1)} %get-tuple-element.46.k_ref, bf16[1,4096,128]{2,1,0:T(8,128)(2,1)S(1)} %get-tuple-element.45.v_ref, ...), custom_call_target="tpu_custom_call" | custom-call | flops 4294967296 | bytes 4194304 | tf_op jit(solution)/shard_map/attend/pallas_call | solution.py:216
  235.5 36.3 %collective-permute-start.6 = (bf16[1,1,1024,128]{3,2,1,0:T(8,128)(2,1)S(1)}, bf16[1,1,1024,128]{3,2,1,0:T(8,128)(2,1)S(1)}, u32[]{:S(2)}, u32[]{:S(2)}) collective-permute-start(bf16[1,1,1024,128]{3,2,1,0:T(8,128)(2,1)S(1)} %get-tuple-element.61), channel_id=1, source_target_pairs={{0,8},{4,12},{8,0},{12,4},{16,24},{20,28},{24,16},{28,20},{1,9},{5... | collective-permute-start | bytes 786440 | tf_op jit(solution)/shard_map/ppermute | solution.py:111
  277.8 17.5 %collective-permute-done.6 = bf16[1,1,1024,128]{3,2,1,0:T(8,128)(2,1)S(1)} collective-permute-done((bf16[1,1,1024,128]{3,2,1,0:T(8,128)(2,1)S(1)}, bf16[1,1,1024,128]{3,2,1,0:T(8,128)(2,1)S(1)}, u32[]{:S(2)}, u32[]{:S(2)}) %collective-permute-start.6) | collective-permute-done | bytes 262176 | tf_op jit(solution)/shard_map/ppermute | solution.py:111
  384.6 21.0 %collective-permute-done.10 = bf16[1024,512]{1,0:T(8,128)(2,1)S(1)} collective-permute-done((bf16[1024,512]{1,0:T(8,128)(2,1)S(1)}, bf16[1024,512]{1,0:T(8,128)(2,1)S(1)}, u32[]{:S(2)}, u32[]{:S(2)}) %collective-permute-start.10) | collective-permute-done | bytes 1048608 | tf_op jit(solution)/shard_map/ppermute | solution.py:105
  425.3 14.6 %fusion.21 = f32[1024,2048]{1,0:T(8,128)} fusion(bf16[1024,2048]{1,0:T(8,128)(2,1)} %get-tuple-element.24, bf16[2048,2048]{1,0:T(8,128)(2,1)} %all-gather.10.cloned.1.call-done), kind=kOutput, calls=%fused_computation.137 | convolution fusion | flops 8589934592 | bytes 20971520 | tf_op jit(solution)/shard_map/dot_general | solution.py:445
  454.5 21.8 %multiply_convert_fusion = (bf16[1024,2048]{1,0:T(8,128)(2,1)}, bf16[1024,2048]{1,0:T(8,128)(2,1)}, bf16[1024,2048]{1,0:T(8,128)(2,1)}) fusion(f32[1024,2048]{1,0:T(8,128)} %fusion.21, f32[1024,2048]{1,0:T(8,128)} %fusion.22, bf16[1024,2048]{1,0:T(8,128)(2,1)} %constant_dynamic-update-slice_fusion.6, bf16[2048,2048]{1,0:T(8,128)(2,1)} %all-gather.14.cloned.1.call-done), kind=kOutput, calls=%fused_computation.8 | convolution fusion | flops 8621391872 | bytes 41943040 | tf_op jit(solution)/shard_map/td,fd->tf/dot_general | solution.py:450
  476.3 14.7 %fusion.24 = f32[1024,2048]{1,0:T(8,128)} fusion(bf16[1024,2048]{1,0:T(8,128)(2,1)} %get-tuple-element.27, bf16[2048,2048]{1,0:T(8,128)(2,1)} %all-gather.10.cloned.1.call-done), kind=kOutput, calls=%fused_computation.140 | convolution fusion | flops 8589934592 | bytes 20971520 | tf_op jit(solution)/shard_map/tf,df->td/dot_general | solution.py:457
  491.0 17.4 %fusion.17 = (f32[1024]{0:T(1024)S(1)}, f32[1024]{0:T(1024)S(1)}, f32[1024,2048]{1,0:T(8,128)}) fusion(f32[1024,2048]{1,0:T(8,128)} %get-tuple-element.25, f32[1024,2048]{1,0:T(8,128)} %fusion.24, bf16[1024,2048]{1,0:T(8,128)(2,1)S(1)} %copy-done.31, bf16[2048,2048]{1,0:T(8,128)(2,1)} %all-gather.12.cloned.1.call-done), kind=kOutput, calls=%fused_computation.133 | convolution fusion | flops 8598321152 | bytes 37756928 | tf_op jit(solution)/shard_map/tf,df->td/dot_general | solution.py:459
  517.3 41.2 %collective-permute-done.24 = f32[2,1024]{1,0:T(2,128)S(1)} collective-permute-done((f32[2,1024]{1,0:T(2,128)S(1)}, f32[2,1024]{1,0:T(2,128)S(1)}, u32[]{:S(2)}, u32[]{:S(2)}) %collective-permute-start.24) | collective-permute-done | bytes 8224 | tf_op jit(solution)/shard_map/ppermute | solution.py:105
  574.5 19.4 %collective-permute-done.27 = bf16[1024,512]{1,0:T(8,128)(2,1)S(1)} collective-permute-done((bf16[1024,512]{1,0:T(8,128)(2,1)S(1)}, bf16[1024,512]{1,0:T(8,128)(2,1)S(1)}, u32[]{:S(2)}, u32[]{:S(2)}) %collective-permute-start.27) | collective-permute-done | bytes 1048608 | tf_op jit(solution)/shard_map/ppermute | solution.py:105
  594.1 19.0 %collective-permute-done.28 = bf16[1024,512]{1,0:T(8,128)(2,1)S(1)} collective-permute-done((bf16[1024,512]{1,0:T(8,128)(2,1)S(1)}, bf16[1024,512]{1,0:T(8,128)(2,1)S(1)}, u32[]{:S(2)}, u32[]{:S(2)}) %collective-permute-start.28) | collective-permute-done | bytes 1048608 | tf_op jit(solution)/shard_map/ppermute | solution.py:105
  630.3 20.9 %collective-permute-done.31 = bf16[1,1,1024,128]{3,2,1,0:T(8,128)(2,1)S(1)} collective-permute-done((bf16[1,1,1024,128]{3,2,1,0:T(8,128)(2,1)S(1)}, bf16[1,1,1024,128]{3,2,1,0:T(8,128)(2,1)S(1)}, u32[]{:S(2)}, u32[]{:S(2)}) %collective-permute-start.31) | collective-permute-done | bytes 262176 | tf_op jit(solution)/shard_map/ppermute | solution.py:111
  652.3 35.2 %attend_back.1 = (bf16[1,4096,128]{2,1,0:T(8,128)(2,1)S(1)}, bf16[1,4096,128]{2,1,0:T(8,128)(2,1)S(1)}, bf16[1,4096,128]{2,1,0:T(8,128)(2,1)S(1)}) custom-call(bf16[1,4096,128]{2,1,0:T(8,128)(2,1)S(1)} %copy-done.5, bf16[1,4096,128]{2,1,0:T(8,128)(2,1)S(1)} %copy-done.3, bf16[1,4096,128]{2,1,0:T(8,128)(2,1)} %copy-done.1, bf16[1,4096,128]{2,1,0:T(8,128)(2,1)} %copy-done.24, ...), custom_call_target="tpu_custom_call" | custom-call | flops 10737418240 | bytes 8388608 | tf_op jit(solution)/shard_map/attend_back/pallas_call | solution.py:304
  700.2 25.1 %collective-permute-done.33 = bf16[1,3,1024,128]{3,2,1,0:T(8,128)(2,1)S(1)} collective-permute-done((bf16[1,3,1024,128]{3,2,1,0:T(8,128)(2,1)S(1)}, bf16[1,3,1024,128]{3,2,1,0:T(8,128)(2,1)S(1)}, u32[]{:S(2)}, u32[]{:S(2)}) %collective-permute-start.33) | collective-permute-done | bytes 786464 | tf_op jit(solution)/shard_map/ppermute | solution.py:111
  725.5 26.2 %collective-permute-done.34 = bf16[1,3,1024,128]{3,2,1,0:T(8,128)(2,1)S(1)} collective-permute-done((bf16[1,3,1024,128]{3,2,1,0:T(8,128)(2,1)S(1)}, bf16[1,3,1024,128]{3,2,1,0:T(8,128)(2,1)S(1)}, u32[]{:S(2)}, u32[]{:S(2)}) %collective-permute-start.34) | collective-permute-done | bytes 786464 | tf_op jit(solution)/shard_map/ppermute | solution.py:111
  756.6 35.8 %dynamic_update_slice.151 = bf16[4,3,1024,128]{3,0,2,1:T(4,128)(2,1)S(1)} dynamic-update-slice(bf16[4,3,1024,128]{3,0,2,1:T(4,128)(2,1)S(1)} %copy.59, bf16[1,3,1024,128]{3,0,2,1:T(2,128)(2,1)} %copy.60, s32[]{:T(128)S(6)} %select_n.75, s32[]{:T(128)} %constant.76.clone.1, s32[]{:T(128)} %constant.76.clone.1, s32[]{:T(128)} %constant.76.clone.1) | dynamic-update-slice | bytes 1572868 | tf_op jit(solution)/shard_map/dynamic_update_slice | solution.py:375
  891.8 22.5 %collective-permute-done.16 = bf16[1024,512]{1,0:T(8,128)(2,1)S(1)} collective-permute-done((bf16[1024,512]{1,0:T(8,128)(2,1)}, bf16[1024,512]{1,0:T(8,128)(2,1)S(1)}, u32[]{:S(2)}, u32[]{:S(2)}) %collective-permute-start.16) | collective-permute-done | bytes 1048608 | tf_op jit(solution)/shard_map/ppermute | solution.py:105
  916.3 23.2 %collective-permute-done.39 = f32[2,1024]{1,0:T(2,128)S(1)} collective-permute-done((f32[2,1024]{1,0:T(2,128)S(1)}, f32[2,1024]{1,0:T(2,128)S(1)}, u32[]{:S(2)}, u32[]{:S(2)}) %collective-permute-start.39) | collective-permute-done | bytes 8224 | tf_op jit(solution)/shard_map/ppermute | solution.py:105
  951.8 20.9 %reduce-scatter.12.cloned.1.call-done = bf16[256,2048]{1,0:T(8,128)(2,1)} async-done(((bf16[2048,2048]{1,0:T(8,128)(2,1)}), bf16[256,2048]{1,0:T(8,128)(2,1)}) %reduce-scatter.12.cloned.1.call-update) | async-done | bytes 1048592 | tf_op jit(solution)/shard_map/reduce_scatter | solution.py:503
  975.5 87.5 %reduce-scatter.10.cloned.1.call-done = bf16[256,2048]{1,0:T(8,128)(2,1)} async-done(((bf16[2048,2048]{1,0:T(8,128)(2,1)}), bf16[256,2048]{1,0:T(8,128)(2,1)}) %reduce-scatter.10.cloned.1.call-update) | async-done | bytes 1048592 | tf_op jit(solution)/shard_map/reduce_scatter | solution.py:503
  1065.8 87.3 %reduce-scatter.14.cloned.1.call-done = bf16[2048,256]{1,0:T(8,128)(2,1)} async-done(((bf16[2048,2048]{1,0:T(8,128)(2,1)}), bf16[2048,256]{1,0:T(8,128)(2,1)}) %reduce-scatter.14.cloned.1.call-update) | async-done | bytes 1048592 | tf_op jit(solution)/shard_map/reduce_scatter | solution.py:503
  (278 shorter events, 421.2 us)
Async XLA Ops:
  7.2 70.9 %all-gather.6.cloned.1.call-start = ((), (), s32[]{:S(2)}) async-start(), calls=%async_computation.5 | async-start | bytes 7077888 | tf_op jit(solution)/shard_map/all_gather | solution.py:403
  9.6 116.3 %all-gather.8.cloned.1.call-start = ((), (), s32[]{:S(2)}) async-start(), calls=%async_computation.6 | async-start | bytes 2359296 | tf_op jit(solution)/shard_map/all_gather | solution.py:404
  10.4 414.9 %all-gather.10.cloned.1.call-start = ((), (), s32[]{:S(2)}) async-start(), calls=%async_computation.7 | async-start | bytes 9437184 | tf_op jit(solution)/shard_map/all_gather | solution.py:405
  11.1 428.8 %all-gather.12.cloned.1.call-start = ((), (), s32[]{:S(2)}) async-start(), calls=%async_computation.8 | async-start | bytes 9437184 | tf_op jit(solution)/shard_map/all_gather | solution.py:406
  11.7 442.9 %all-gather.14.cloned.1.call-start = ((), (), s32[]{:S(2)}) async-start(), calls=%async_computation.9 | async-start | bytes 9437184 | tf_op jit(solution)/shard_map/all_gather | solution.py:407
  16.3 104.0 %collective-permute-start.18 = (bf16[1024,512]{1,0:T(8,128)(2,1)}, bf16[1024,512]{1,0:T(8,128)(2,1)}, u32[]{:S(2)}, u32[]{:S(2)}) collective-permute-start(bf16[1024,512]{1,0:T(8,128)(2,1)} %param.9), channel_id=1, source_target_pairs={{0,1},{1,0},{2,3},{3,2},{4,5},{5,4},{6,7},{7,6},{8,9},{9,8},{10,11... | collective-permute-start | bytes 3145736 | tf_op jit(solution)/shard_map/ppermute | solution.py:105
  18.3 929.2 %reduce-scatter.8.cloned.1.call-start = ((), (), s32[]{:S(2)}) async-start(), calls=%async_computation.11 | async-start | bytes 2359296 | tf_op jit(solution)/shard_map/reduce_scatter | solution.py:503
  109.6 65.7 %collective-permute-start.3 = (bf16[1,3,1024,128]{3,2,1,0:T(8,128)(2,1)}, bf16[1,3,1024,128]{3,2,1,0:T(8,128)(2,1)}, u32[]{:S(2)}, u32[]{:S(2)}) collective-permute-start(bf16[1,3,1024,128]{3,2,1,0:T(8,128)(2,1)} %get-tuple-element.50), channel_id=1, source_target_pairs={{0,8},{4,12},{8,0},{12,4},{16,24},{20,28},{24,16},{28,20},{1,9},{5... | collective-permute-start | bytes 2359304 | tf_op jit(solution)/shard_map/ppermute | solution.py:111
  109.6 68.1 %collective-permute-start.4 = (bf16[1,3,1024,128]{3,2,1,0:T(8,128)(2,1)}, bf16[1,3,1024,128]{3,2,1,0:T(8,128)(2,1)}, u32[]{:S(2)}, u32[]{:S(2)}) collective-permute-start(bf16[1,3,1024,128]{3,2,1,0:T(8,128)(2,1)} %get-tuple-element.49), channel_id=1, source_target_pairs={{0,16},{4,20},{8,24},{12,28},{16,0},{20,4},{24,8},{28,12},{1,17},{... | collective-permute-start | bytes 2359304 | tf_op jit(solution)/shard_map/ppermute | solution.py:111
  111.1 124.5 %collective-permute-start.19 = (bf16[1024,512]{1,0:T(8,128)(2,1)}, bf16[1024,512]{1,0:T(8,128)(2,1)}, u32[]{:S(2)}, u32[]{:S(2)}) collective-permute-start(bf16[1024,512]{1,0:T(8,128)(2,1)} %param.9), channel_id=1, source_target_pairs={{0,2},{1,3},{2,0},{3,1},{4,6},{5,7},{6,4},{7,5},{8,10},{9,11},{10,... | collective-permute-start | bytes 3145736 | tf_op jit(solution)/shard_map/ppermute | solution.py:105
  112.0 92.8 %collective-permute-start.5 = (bf16[1,3,1024,128]{3,2,1,0:T(8,128)(2,1)}, bf16[1,3,1024,128]{3,2,1,0:T(8,128)(2,1)}, u32[]{:S(2)}, u32[]{:S(2)}) collective-permute-start(bf16[1,3,1024,128]{3,2,1,0:T(8,128)(2,1)} %get-tuple-element.48), channel_id=1, source_target_pairs={{0,24},{4,28},{8,16},{12,20},{16,8},{20,12},{24,0},{28,4},{1,25},{... | collective-permute-start | bytes 2359304 | tf_op jit(solution)/shard_map/ppermute | solution.py:111
  120.3 153.9 %collective-permute-start.20 = (bf16[1024,512]{1,0:T(8,128)(2,1)}, bf16[1024,512]{1,0:T(8,128)(2,1)}, u32[]{:S(2)}, u32[]{:S(2)}) collective-permute-start(bf16[1024,512]{1,0:T(8,128)(2,1)} %param.9), channel_id=1, source_target_pairs={{0,3},{1,2},{2,1},{3,0},{4,7},{5,6},{6,5},{7,4},{8,11},{9,10},{10,... | collective-permute-start | bytes 3145736 | tf_op jit(solution)/shard_map/ppermute | solution.py:105
  175.2 183.3 %collective-permute-start.12 = (bf16[512,2048]{1,0:T(8,128)(2,1)}, bf16[512,2048]{1,0:T(8,128)(2,1)}, u32[]{:S(2)}, u32[]{:S(2)}) collective-permute-start(bf16[512,2048]{1,0:T(8,128)(2,1)} %all-gather.8.cloned.1.call-done), channel_id=1, source_target_pairs={{0,1},{1,0},{2,3},{3,2},{4,5},{5,4},{6,7},{7,6},{8,9},{9,8},{10,11... | collective-permute-start | bytes 6291464 | tf_op jit(solution)/shard_map/ppermute | solution.py:105
  177.6 187.4 %collective-permute-start.13 = (bf16[512,2048]{1,0:T(8,128)(2,1)}, bf16[512,2048]{1,0:T(8,128)(2,1)}, u32[]{:S(2)}, u32[]{:S(2)}) collective-permute-start(bf16[512,2048]{1,0:T(8,128)(2,1)} %all-gather.8.cloned.1.call-done), channel_id=1, source_target_pairs={{0,2},{1,3},{2,0},{3,1},{4,6},{5,7},{6,4},{7,5},{8,10},{9,11},{10,... | collective-permute-start | bytes 6291464 | tf_op jit(solution)/shard_map/ppermute | solution.py:105
  204.9 163.4 %collective-permute-start.14 = (bf16[512,2048]{1,0:T(8,128)(2,1)}, bf16[512,2048]{1,0:T(8,128)(2,1)}, u32[]{:S(2)}, u32[]{:S(2)}) collective-permute-start(bf16[512,2048]{1,0:T(8,128)(2,1)} %all-gather.8.cloned.1.call-done), channel_id=1, source_target_pairs={{0,3},{1,2},{2,1},{3,0},{4,7},{5,6},{6,5},{7,4},{8,11},{9,10},{10,... | collective-permute-start | bytes 6291464 | tf_op jit(solution)/shard_map/ppermute | solution.py:105
  235.5 59.8 %collective-permute-start.6 = (bf16[1,1,1024,128]{3,2,1,0:T(8,128)(2,1)S(1)}, bf16[1,1,1024,128]{3,2,1,0:T(8,128)(2,1)S(1)}, u32[]{:S(2)}, u32[]{:S(2)}) collective-permute-start(bf16[1,1,1024,128]{3,2,1,0:T(8,128)(2,1)S(1)} %get-tuple-element.61), channel_id=1, source_target_pairs={{0,8},{4,12},{8,0},{12,4},{16,24},{20,28},{24,16},{28,20},{1,9},{5... | collective-permute-start | bytes 786440 | tf_op jit(solution)/shard_map/ppermute | solution.py:111
  626.0 323.3 %reduce-scatter.6.cloned.1.call-start = ((), (), s32[]{:S(2)}) async-start(), calls=%async_computation.10 | async-start | bytes 7077888 | tf_op jit(solution)/shard_map/reduce_scatter | solution.py:503
  697.8 53.9 %collective-permute-start.34 = (bf16[1,3,1024,128]{3,2,1,0:T(8,128)(2,1)S(1)}, bf16[1,3,1024,128]{3,2,1,0:T(8,128)(2,1)S(1)}, u32[]{:S(2)}, u32[]{:S(2)}) collective-permute-start(bf16[1,3,1024,128]{3,2,1,0:T(8,128)(2,1)S(1)} %get-tuple-element.42), channel_id=1, source_target_pairs={{0,16},{4,20},{8,24},{12,28},{16,0},{20,4},{24,8},{28,12},{1,17},{... | collective-permute-start | bytes 2359304 | tf_op jit(solution)/shard_map/ppermute | solution.py:111
  697.8 56.4 %collective-permute-start.35 = (bf16[1,3,1024,128]{3,2,1,0:T(8,128)(2,1)S(1)}, bf16[1,3,1024,128]{3,2,1,0:T(8,128)(2,1)S(1)}, u32[]{:S(2)}, u32[]{:S(2)}) collective-permute-start(bf16[1,3,1024,128]{3,2,1,0:T(8,128)(2,1)S(1)} %get-tuple-element.41), channel_id=1, source_target_pairs={{0,24},{4,28},{8,16},{12,20},{16,8},{20,12},{24,0},{28,4},{1,25},{... | collective-permute-start | bytes 2359304 | tf_op jit(solution)/shard_map/ppermute | solution.py:111
  808.3 164.4 %reduce-scatter.12.cloned.1.call-start = ((), (), s32[]{:S(2)}) async-start(), calls=%async_computation.13 | async-start | bytes 9437184 | tf_op jit(solution)/shard_map/reduce_scatter | solution.py:503
  822.4 240.6 %reduce-scatter.10.cloned.1.call-start = ((), (), s32[]{:S(2)}) async-start(), calls=%async_computation.12 | async-start | bytes 9437184 | tf_op jit(solution)/shard_map/reduce_scatter | solution.py:503
  836.6 316.5 %reduce-scatter.14.cloned.1.call-start = ((), (), s32[]{:S(2)}) async-start(), calls=%async_computation.14 | async-start | bytes 9437184 | tf_op jit(solution)/shard_map/reduce_scatter | solution.py:503
  883.0 61.0 %collective-permute-start.36 = (bf16[1024,512]{1,0:T(8,128)(2,1)S(1)}, bf16[1024,512]{1,0:T(8,128)(2,1)S(1)}, u32[]{:S(2)}, u32[]{:S(2)}) collective-permute-start(bf16[1024,512]{1,0:T(8,128)(2,1)S(1)} %get-tuple-element.29), channel_id=1, source_target_pairs={{0,1},{1,0},{2,3},{3,2},{4,5},{5,4},{6,7},{7,6},{8,9},{9,8},{10,11... | collective-permute-start | bytes 3145736 | tf_op jit(solution)/shard_map/ppermute | solution.py:105
  883.1 61.0 %collective-permute-start.37 = (bf16[1024,512]{1,0:T(8,128)(2,1)S(1)}, bf16[1024,512]{1,0:T(8,128)(2,1)S(1)}, u32[]{:S(2)}, u32[]{:S(2)}) collective-permute-start(bf16[1024,512]{1,0:T(8,128)(2,1)S(1)} %get-tuple-element.31), channel_id=1, source_target_pairs={{0,2},{1,3},{2,0},{3,1},{4,6},{5,7},{6,4},{7,5},{8,10},{9,11},{10,... | collective-permute-start | bytes 3145736 | tf_op jit(solution)/shard_map/ppermute | solution.py:105
  (60 other events, 1560.8 us)
Sparse Core Ops, SparseCore 0:
  10.2 67.8 all-gather.5
  79.7 29.0 all-gather.7
  110.3 139.6 all-gather.9
  251.5 103.5 all-gather.11
  356.5 80.9 all-gather.13
  626.1 38.5 reduce-scatter.7
  808.4 73.9 reduce-scatter.5
  884.7 87.9 reduce-scatter.11
  975.0 87.9 reduce-scatter.9
  1065.1 87.9 reduce-scatter.13

commit v2 on v0

--- a/solution.py
+++ b/solution.py
@@ -1,8 +1,11 @@
+import functools
 import math
 
 import jax
 import jax.numpy as jnp
 from jax import lax
+from jax.experimental import pallas as pl
+from jax.experimental.pallas import tpu as pltpu
 from jax.sharding import PartitionSpec as P
 
 HEAD = 128
@@ -91,6 +94,1324 @@
         * score_scale
     )
     return jnp.where(allowed[None], raw_scores, masked_score)
+
+
+BLOCK = 512
+log2e = 1.4426950408889634
+
+
+def turn(values, cosine, sine):
+    return values * cosine + pltpu.roll(values, values.shape[1] // 2, 1) * sine
+
+
+def block_mask(key_block, query_block, start_row):
+    key_index = key_block * BLOCK + lax.broadcasted_iota(jnp.int32, (BLOCK, BLOCK), 0)
+    query_index = query_block * BLOCK + lax.broadcasted_iota(jnp.int32, (BLOCK, BLOCK), 1)
+    return (key_index <= query_index) & (key_index >= start_row)
+
+
+def each_block(block, visit):
+    prompt_blocks = PROMPT // BLOCK
+
+    def whole(j, carry):
+        visit(j, False)
+        return carry
+
+    lax.fori_loop(0, jnp.minimum(block, prompt_blocks), whole, 0)
+
+    @pl.when(block > prompt_blocks)
+    def _():
+        visit(block - 1, True)
+
+    visit(block, True)
+
+
+MESH = pl.DeviceIdType.MESH
+
+
+def place_of(place, groups_here):
+    row = lax.axis_index("row")
+    return (place * groups_here + lax.rem(row, groups_here), lax.axis_index("col"))
+
+
+def send(source, target, send_sem, recv_sem, device):
+    return pltpu.make_async_remote_copy(
+        src_ref=source, dst_ref=target, send_sem=send_sem, recv_sem=recv_sem,
+        device_id=device, device_id_type=MESH,
+    )
+
+
+def block_rows(block):
+    return pl.ds(pl.multiple_of(block * BLOCK, BLOCK), BLOCK)
+
+
+def col_device(by):
+    return (lax.axis_index("row"), lax.axis_index("col") ^ by)
+
+
+def greet_cols(count):
+    barrier = pltpu.get_barrier_semaphore()
+    for by in range(1, count):
+        pl.semaphore_signal(barrier, inc=1, device_id=col_device(by), device_id_type=MESH)
+    pl.semaphore_wait(barrier, count - 1)
+
+
+class Gather:
+    def __init__(self, source, slots, sends, recvs, local):
+        me = lax.axis_index("col")
+        a, b = source[0], source[1]
+        self.own = []
+        if local is not None:
+            self.own = [
+                pltpu.make_async_copy(a, slots(me)[0], local.at[0]),
+                pltpu.make_async_copy(b, slots(me)[1], local.at[1]),
+            ]
+
+        def copy(i, what, where, by):
+            return send(what, where, sends.at[i], recvs.at[i], col_device(by))
+
+        self.first = [
+            copy(0, a, slots(me)[0], 1),
+            copy(3, b, slots(me)[1], 2),
+            copy(1, b, slots(me)[1], 1),
+            copy(2, a, slots(me)[0], 2),
+        ]
+        across, along = me ^ 1, me ^ 2
+        self.second = [
+            copy(4, slots(across)[0], slots(across)[0], 2),
+            copy(5, slots(along)[1], slots(along)[1], 1),
+        ]
+
+    def start(self):
+        for one in self.own + self.first:
+            one.start()
+
+    def forward(self):
+        self.first[0].wait_recv()
+        self.second[0].start()
+        self.first[1].wait_recv()
+        self.second[1].start()
+
+    def receive(self):
+        for one in self.first[2:] + self.second:
+            one.wait_recv()
+        for one in self.own:
+            one.wait()
+
+    def finish(self):
+        for one in self.first + self.second:
+            one.wait_send()
+
+
+def halves(ref, start, size):
+    half = size // 2
+    return ref.at[pl.ds(start, half)], ref.at[pl.ds(start + half, half)]
+
+
+def greet_all(me, span, groups_here, count):
+    barrier = pltpu.get_barrier_semaphore()
+    for by in range(1, span):
+        pl.semaphore_signal(
+            barrier, inc=1, device_id=place_of(lax.rem(me + by, span), groups_here), device_id_type=MESH
+        )
+    for by in range(1, count):
+        pl.semaphore_signal(barrier, inc=1, device_id=col_device(by), device_id_type=MESH)
+    pl.semaphore_wait(barrier, span + count - 2)
+
+
+def attend_kernel(
+    groups_here, sent_ref, start_ref, rider_ref, back_ref, held_ref, o_ref, lse_ref, riders_ref,
+    qkv_ref, top_ref, total_ref, sum_ref,
+    in_send, in_recv, out_send, out_recv, keep_sem, own_sem, ride_send, ride_recv, ride_local,
+):
+    span, _, tokens, _ = sent_ref.shape
+    me = lax.axis_index("row") // groups_here
+    blocks = start_ref.shape[0]
+    per_place = tokens // BLOCK
+    scale = HEAD**-0.5 * log2e
+    greet_all(me, span, groups_here, riders_ref.shape[0])
+    depth = rider_ref.shape[0]
+    ride = Gather(
+        halves(rider_ref, 0, depth), lambda c: halves(riders_ref.at[c], 0, depth),
+        ride_send, ride_recv, ride_local,
+    )
+
+    def qkv_copy(by):
+        peer = lax.rem(me + by, span)
+        return send(
+            sent_ref.at[peer], qkv_ref.at[:, pl.ds(pl.multiple_of(me * tokens, tokens), tokens)],
+            in_send.at[by], in_recv.at[by], place_of(peer, groups_here),
+        )
+
+    own_rows = pl.ds(pl.multiple_of(me * tokens, tokens), tokens)
+    own_copy = pltpu.make_async_copy(sent_ref.at[me], qkv_ref.at[:, own_rows], in_recv.at[0])
+    own_copy.start()
+    for by in range(1, span):
+        qkv_copy(by).start()
+    ride.start()
+
+    def out_copy(block):
+        to = block // per_place
+        half = lax.rem(block, per_place)
+        by = lax.rem(to - me + span, span)
+        return send(
+            o_ref.at[block_rows(block)], back_ref.at[me, block_rows(half)],
+            out_send.at[block], out_recv.at[by, half], place_of(to, groups_here),
+        )
+
+    def own_out(block):
+        return pltpu.make_async_copy(
+            o_ref.at[block_rows(block)],
+            back_ref.at[me, block_rows(lax.rem(block, per_place))],
+            own_sem.at[lax.rem(block, per_place)],
+        )
+
+    def keep_copy(place):
+        rows = pl.ds(pl.multiple_of(place * tokens, tokens), tokens)
+        return pltpu.make_async_copy(qkv_ref.at[:, rows], held_ref.at[:, rows], keep_sem.at[place])
+
+    def one_block(block, carry):
+        place = block // per_place
+
+        @pl.when(lax.rem(block, per_place) == 0)
+        def _():
+            @pl.when(place == me)
+            def _():
+                own_copy.wait()
+
+            for by in range(1, span):
+
+                @pl.when(lax.rem(place + by, span) == me)
+                def _():
+                    qkv_copy(by).wait_recv()
+
+            keep_copy(place).start()
+
+        top_ref[...] = jnp.full_like(top_ref, masked_score)
+        total_ref[...] = jnp.zeros_like(total_ref)
+        sum_ref[...] = jnp.zeros_like(sum_ref)
+        queries = qkv_ref[0, block_rows(block), :]
+        start_row = start_ref[block]
+
+        def visit(j, masked):
+            rows = block_rows(j)
+            scores = scale * matmul_nt(qkv_ref[1, rows, :], queries)
+            if masked:
+                scores = jnp.where(block_mask(j, block, start_row), scores, masked_score)
+            old_top = top_ref[...]
+            new_top = jnp.maximum(old_top, jnp.max(scores, axis=0, keepdims=True))
+            shrink = jnp.exp2(old_top - new_top)
+            probs = jnp.exp2(scores - new_top)
+            if masked:
+                probs = jnp.where(scores > 0.5 * masked_score, probs, 0.0)
+            total_ref[...] = total_ref[...] * shrink + jnp.sum(probs, axis=0, keepdims=True)
+            sum_ref[...] = sum_ref[...] * shrink + lax.dot_general(
+                qkv_ref[2, rows, :],
+                probs.astype(jnp.bfloat16),
+                (((0,), (0,)), ((), ())),
+                preferred_element_type=jnp.float32,
+            )
+            top_ref[...] = new_top
+
+        each_block(block, visit)
+        total = total_ref[...]
+        o_ref[block_rows(block), :] = (sum_ref[...] / total).T.astype(jnp.bfloat16)
+        lse_ref[block] = top_ref[...] + jnp.log2(total)
+
+        @pl.when(place == me)
+        def _():
+            own_out(block).start()
+
+        @pl.when(place != me)
+        def _():
+            out_copy(block).start()
+
+        @pl.when(block == blocks // 2)
+        def _():
+            ride.forward()
+
+        return carry
+
+    lax.fori_loop(0, blocks, one_block, 0)
+    ride.receive()
+    ride.finish()
+
+    for by in range(1, span):
+        qkv_copy(by).wait_send()
+
+    def finish(block, carry):
+        place = block // per_place
+
+        @pl.when(place == me)
+        def _():
+            own_out(block).wait()
+
+        @pl.when(place != me)
+        def _():
+            out_copy(block).wait_send()
+
+        return carry
+
+    lax.fori_loop(0, blocks, finish, 0)
+    for by in range(1, span):
+        for half in range(per_place):
+            send(
+                o_ref.at[block_rows(half)], back_ref.at[lax.rem(me - by + span, span), block_rows(half)],
+                out_send.at[half], out_recv.at[by, half], place_of(me, groups_here),
+            ).wait_recv()
+    for place in range(span):
+        keep_copy(place).wait()
+
+
+def attend(sent, start_rows, rider, groups_here, count):
+    span, _, tokens, size = sent.shape
+    blocks = start_rows.shape[0]
+    length = span * tokens
+    hbm = pl.BlockSpec(memory_space=pl.ANY)
+    vmem = pl.BlockSpec(memory_space=pltpu.VMEM)
+    per_place = tokens // BLOCK
+    dma = pltpu.SemaphoreType.DMA
+    return pl.pallas_call(
+        functools.partial(attend_kernel, groups_here),
+        in_specs=[hbm, vmem, hbm],
+        out_specs=[hbm, hbm, vmem, vmem, hbm],
+        out_shape=[
+            jax.ShapeDtypeStruct((span, tokens, size), jnp.bfloat16),
+            jax.ShapeDtypeStruct((3, length, size), jnp.bfloat16),
+            jax.ShapeDtypeStruct((length, size), jnp.bfloat16),
+            jax.ShapeDtypeStruct((blocks, 1, BLOCK), jnp.float32),
+            jax.ShapeDtypeStruct((count, *rider.shape), jnp.bfloat16),
+        ],
+        scratch_shapes=[
+            pltpu.VMEM((3, length, size), jnp.bfloat16),
+            pltpu.VMEM((1, BLOCK), jnp.float32),
+            pltpu.VMEM((1, BLOCK), jnp.float32),
+            pltpu.VMEM((size, BLOCK), jnp.float32),
+            dma((span,)), dma((span,)), dma((blocks,)), dma((span, per_place)), dma((span,)),
+            dma((per_place,)), dma((6,)), dma((6,)), dma((2,)),
+        ],
+        compiler_params=pltpu.CompilerParams(
+            vmem_limit_bytes=32 * 2**20, collective_id=1, has_side_effects=True
+        ),
+        cost_estimate=pl.CostEstimate(
+            flops=length * length * size * 2, bytes_accessed=length * size * 200,
+            transcendentals=length * length // 2,
+        ),
+        name="attend",
+    )(sent, start_rows, rider)
+
+
+def attend_back_kernel(
+    groups_here, d_sent_ref, qkv_ref, o_ref, lse_ref, start_ref, cos_ref, sin_ref, rider_ref,
+    d_raw_ref, riders_ref, do_ref, stage_ref, dq_sum, dk_sum, dv_sum,
+    in_send, in_recv, q_send, q_recv, kv_send, kv_recv, own_sem, ride_send, ride_recv,
+):
+    span, tokens, _ = d_sent_ref.shape
+    me = lax.axis_index("row") // groups_here
+    blocks = start_ref.shape[0]
+    per_place = tokens // BLOCK
+    after = blocks - PROMPT // BLOCK
+    scale = HEAD**-0.5
+    greet_all(me, span, groups_here, rider_ref.shape[0])
+    ride = Scatter(
+        rider_ref, riders_ref, None, None, pl.ds(0, tokens), ride_send, ride_recv
+    )
+    own_rows = pl.ds(pl.multiple_of(me * tokens, tokens), tokens)
+
+    def do_copy(by):
+        peer = lax.rem(me + by, span)
+        return send(
+            d_sent_ref.at[peer], do_ref.at[own_rows], in_send.at[by], in_recv.at[by],
+            place_of(peer, groups_here),
+        )
+
+    own_copy = pltpu.make_async_copy(d_sent_ref.at[me], do_ref.at[own_rows], in_recv.at[0])
+    own_copy.start()
+    for by in range(1, span):
+        do_copy(by).start()
+    ride.start()
+    dk_sum[...] = jnp.zeros_like(dk_sum)
+    dv_sum[...] = jnp.zeros_like(dv_sum)
+
+    def moved(block, which):
+        to = block // per_place
+        half = lax.rem(block, per_place)
+        by = lax.rem(to - me + span, span)
+        kinds = pl.ds(1, 2) if which else pl.ds(0, 1)
+        source = stage_ref.at[kinds, block_rows(block)]
+        target = d_raw_ref.at[me, kinds, block_rows(half)]
+        sends, recvs = (kv_send, kv_recv) if which else (q_send, q_recv)
+        return (
+            to == me,
+            pltpu.make_async_copy(source, target, own_sem.at[which, half]),
+            send(source, target, sends.at[block], recvs.at[by, half], place_of(to, groups_here)),
+        )
+
+    def start_move(block, which):
+        mine, local, remote = moved(block, which)
+
+        @pl.when(mine)
+        def _():
+            local.start()
+
+        @pl.when(jnp.logical_not(mine))
+        def _():
+            remote.start()
+
+    def close(j):
+        rows = block_rows(j)
+        stage_ref[1, rows, :] = turn(
+            dk_sum[rows, :] * scale, cos_ref[rows, :], sin_ref[rows, :]
+        ).astype(jnp.bfloat16)
+        stage_ref[2, rows, :] = dv_sum[rows, :].astype(jnp.bfloat16)
+        start_move(j, 1)
+
+    def one_block(n, carry):
+        block = jnp.where(n < after, blocks - after + n, blocks - 1 - n)
+        place = block // per_place
+
+        @pl.when(lax.rem(n, per_place) == 0)
+        def _():
+            @pl.when(place == me)
+            def _():
+                own_copy.wait()
+
+            for by in range(1, span):
+
+                @pl.when(lax.rem(place + by, span) == me)
+                def _():
+                    do_copy(by).wait_recv()
+
+        dq_sum[...] = jnp.zeros_like(dq_sum)
+        here = block_rows(block)
+        queries = qkv_ref[0, here, :]
+        d_out = do_ref[here, :]
+        lse = lse_ref[block]
+        start_row = start_ref[block]
+        delta = jnp.sum(
+            (d_out.astype(jnp.float32) * o_ref[here, :].astype(jnp.float32)).T, axis=0, keepdims=True
+        )
+
+        def visit(j, masked):
+            rows = block_rows(j)
+            key_part = qkv_ref[1, rows, :]
+            scores = (scale * log2e) * matmul_nt(key_part, queries)
+            if masked:
+                scores = jnp.where(block_mask(j, block, start_row), scores, masked_score)
+            probs = jnp.exp2(scores - lse)
+            d_probs = matmul_nt(qkv_ref[2, rows, :], d_out)
+            d_scores = (probs * (d_probs - delta)).astype(jnp.bfloat16)
+            dv_sum[rows, :] += matmul(probs.astype(jnp.bfloat16), d_out)
+            dk_sum[rows, :] += matmul(d_scores, queries)
+            dq_sum[...] += lax.dot_general(
+                key_part, d_scores, (((0,), (0,)), ((), ())), preferred_element_type=jnp.float32
+            )
+
+        each_block(block, visit)
+        stage_ref[0, here, :] = turn(
+            dq_sum[...].T * scale, cos_ref[here, :], sin_ref[here, :]
+        ).astype(jnp.bfloat16)
+        start_move(block, 0)
+
+        @pl.when((n >= 1) & (n < after))
+        def _():
+            close(block - 1)
+
+        @pl.when(n >= after - 1)
+        def _():
+            close(block)
+
+        return carry
+
+    lax.fori_loop(0, blocks, one_block, 0)
+    ride.receive()
+    ride.finish()
+    for by in range(1, span):
+        do_copy(by).wait_send()
+
+    def finish(block, carry):
+        for which in range(2):
+            mine, local, remote = moved(block, which)
+
+            @pl.when(mine)
+            def _():
+                local.wait()
+
+            @pl.when(jnp.logical_not(mine))
+            def _():
+                remote.wait_send()
+
+        return carry
+
+    lax.fori_loop(0, blocks, finish, 0)
+    for by in range(1, span):
+        source = lax.rem(me - by + span, span)
+        for half in range(per_place):
+            for which in range(2):
+                kinds = pl.ds(1, 2) if which else pl.ds(0, 1)
+                sends, recvs = (kv_send, kv_recv) if which else (q_send, q_recv)
+                send(
+                    stage_ref.at[kinds, block_rows(half)], d_raw_ref.at[source, kinds, block_rows(half)],
+                    sends.at[half], recvs.at[by, half], place_of(me, groups_here),
+                ).wait_recv()
+
+
+def attend_back(d_sent, held, out, lse, start_rows, cosine, sine, rider, groups_here):
+    span, tokens, size = d_sent.shape
+    blocks = start_rows.shape[0]
+    length = span * tokens
+    hbm = pl.BlockSpec(memory_space=pl.ANY)
+    vmem = pl.BlockSpec(memory_space=pltpu.VMEM)
+    per_place = tokens // BLOCK
+    dma = pltpu.SemaphoreType.DMA
+    return pl.pallas_call(
+        functools.partial(attend_back_kernel, groups_here),
+        in_specs=[hbm] + [vmem] * 6 + [hbm],
+        out_specs=[hbm, hbm],
+        out_shape=[
+            jax.ShapeDtypeStruct((span, 3, tokens, size), jnp.bfloat16),
+            jax.ShapeDtypeStruct((rider.shape[0] - 1, *rider.shape[1:]), jnp.bfloat16),
+        ],
+        scratch_shapes=[
+            pltpu.VMEM((length, size), jnp.bfloat16),
+            pltpu.VMEM((3, length, size), jnp.bfloat16),
+            pltpu.VMEM((size, BLOCK), jnp.float32),
+            pltpu.VMEM((length, size), jnp.float32),
+            pltpu.VMEM((length, size), jnp.float32),
+            dma((span,)), dma((span,)), dma((blocks,)), dma((span, per_place)), dma((blocks,)),
+            dma((span, per_place)), dma((2, per_place)), dma((1, rider.shape[0] - 1)),
+            dma((1, rider.shape[0] - 1)),
+        ],
+        compiler_params=pltpu.CompilerParams(
+            vmem_limit_bytes=48 * 2**20, collective_id=2, has_side_effects=True
+        ),
+        cost_estimate=pl.CostEstimate(
+            flops=length * length * size * 5, bytes_accessed=length * size * 200,
+            transcendentals=length * length // 2,
+        ),
+        name="attend_back",
+    )(d_sent, held, out, lse, start_rows, cosine, sine, rider)
+
+
+def matmul(a, b):
+    return jnp.dot(a, b, preferred_element_type=jnp.float32)
+
+
+def matmul_nt(a, b):
+    return lax.dot_general(a, b, (((1,), (1,)), ((), ())), preferred_element_type=jnp.float32)
+
+
+def resident(shape):
+    zeros = (0,) * len(shape)
+    return pl.BlockSpec(shape, lambda *_: zeros, pipeline_mode=pl.Buffered(1))
+
+
+def own_width(ref, width, col):
+    return ref[:, pl.ds(pl.multiple_of(col * width, width), width)]
+
+
+def enter_kernel(
+    inputs_ref, cot_ref, pieces_ref, cots_ref, unit_ref, unit_t_ref, own_ref, inverse_ref,
+    held_ref, rows_ref, sends, recvs, local, keep,
+):
+    count, rows, piece = held_ref.shape
+    col = lax.axis_index("col")
+    greet_cols(count)
+    first = Gather(
+        halves(inputs_ref, 0, rows), lambda c: halves(held_ref.at[c], 0, rows),
+        sends.at[0], recvs.at[0], local.at[0],
+    )
+    second = Gather(
+        halves(cot_ref, 0, rows), lambda c: halves(cots_ref.at[c], 0, rows),
+        sends.at[1], recvs.at[1], local.at[1],
+    )
+    first.start()
+    first.forward()
+    second.start()
+    first.receive()
+    out = pltpu.make_async_copy(held_ref, pieces_ref, keep)
+    out.start()
+
+    def norm(t, carry):
+        here = pl.ds(pl.multiple_of(t * 128, 128), 128)
+        parts = [held_ref[c, here, :].astype(jnp.float32) for c in range(count)]
+        unit, inverse = normalize_rows(jnp.concatenate(parts, axis=1))
+        rows_ref[...] = unit
+        unit = unit.astype(jnp.bfloat16)
+        unit_ref[here, :] = unit
+        unit_t_ref[:, here] = unit.T
+        own_ref[here, :] = own_width(rows_ref, piece, col)
+        inverse_ref[here, :] = jnp.broadcast_to(inverse, (128, 128))
+        return carry
+
+    for t in range(rows // 128):
+        norm(t, 0)
+    second.forward()
+    second.receive()
+    first.finish()
+    second.finish()
+    out.wait()
+
+
+def enter(inputs, cotangent, count):
+    rows, piece = inputs.shape
+    width = count * piece
+    hbm = pl.BlockSpec(memory_space=pl.ANY)
+    vmem = pl.BlockSpec(memory_space=pltpu.VMEM)
+    dma = pltpu.SemaphoreType.DMA
+    shape = jax.ShapeDtypeStruct
+    return pl.pallas_call(
+        enter_kernel,
+        in_specs=[hbm, hbm],
+        out_specs=[hbm, hbm, vmem, vmem, vmem, vmem],
+        out_shape=[
+            shape((count, rows, piece), jnp.bfloat16),
+            shape((count, rows, piece), jnp.bfloat16),
+            shape((rows, width), jnp.bfloat16),
+            shape((width, rows), jnp.bfloat16),
+            shape((rows, piece), jnp.float32),
+            shape((rows, 128), jnp.float32),
+        ],
+        scratch_shapes=[
+            pltpu.VMEM((count, rows, piece), jnp.bfloat16),
+            pltpu.VMEM((128, width), jnp.float32),
+            dma((2, 6)), dma((2, 6)), dma((2, 2)), dma,
+        ],
+        compiler_params=pltpu.CompilerParams(
+            vmem_limit_bytes=40 * 2**20, collective_id=3, has_side_effects=True
+        ),
+        cost_estimate=pl.CostEstimate(
+            flops=10 * rows * width, bytes_accessed=100 * rows * width, transcendentals=0
+        ),
+        name="enter",
+    )(inputs, cotangent)
+
+
+def own_width(ref, width, col):
+    return ref[:, pl.ds(pl.multiple_of(col * width, width), width)]
+
+
+def project_kernel(unit_ref, weight_ref, cos_ref, sin_ref, out_ref):
+    kind = pl.program_id(0)
+    rows, width = unit_ref.shape
+    heads = out_ref.shape[0]
+    weight = weight_ref[:, 0].reshape(width, heads * HEAD)
+    step = min(256, rows)
+    for t in range(0, rows, step):
+        here = pl.ds(t, step)
+        raw = matmul(unit_ref[here, :], weight)
+
+        @pl.when(kind < 2)
+        def _():
+            cosine, sine = cos_ref[here, :], sin_ref[here, :]
+            for h in range(heads):
+                part = turn(raw[:, h * HEAD : (h + 1) * HEAD], cosine, -sine)
+                out_ref[h, 0, here, :] = part.astype(jnp.bfloat16)
+
+        @pl.when(kind == 2)
+        def _():
+            for h in range(heads):
+                out_ref[h, 0, here, :] = raw[:, h * HEAD : (h + 1) * HEAD].astype(jnp.bfloat16)
+
+
+def project(unit, weight, cosine, sine):
+    rows, width = unit.shape
+    owners, _, depth, columns = weight.shape
+    kinds = 3
+    heads = columns // HEAD
+    return pl.pallas_call(
+        project_kernel,
+        grid=(kinds,),
+        in_specs=[
+            resident((rows, width)),
+            pl.BlockSpec((owners, 1, depth, columns), lambda k: (0, k, 0, 0)),
+            resident((rows, HEAD)),
+            resident((rows, HEAD)),
+        ],
+        out_specs=pl.BlockSpec((heads, 1, rows, HEAD), lambda k: (0, k, 0, 0)),
+        out_shape=jax.ShapeDtypeStruct((heads, kinds, rows, HEAD), jnp.bfloat16),
+        compiler_params=pltpu.CompilerParams(vmem_limit_bytes=40 * 2**20),
+        cost_estimate=pl.CostEstimate(
+            flops=2 * rows * width * kinds * columns, bytes_accessed=2 * width * kinds * columns,
+            transcendentals=0,
+        ),
+        name="project",
+    )(unit, weight, cosine, sine)
+
+
+def branch_kernel(
+    back_ref, weight_ref, pieces_ref, unit_ref, unit_t_ref, middle_ref, own_ref, inverse_ref,
+    heads_ref, flat_ref, rows_ref, terms_ref, sends, recvs, local,
+):
+    col = lax.axis_index("col")
+    count, heads, rows, size = heads_ref.shape
+    piece = pieces_ref.shape[2]
+    greet_cols(count)
+    parts = 2
+    span = rows // parts
+
+    def cut(ref, p):
+        half = span // 2
+        return (
+            ref.at[:, pl.ds(p * span, half)],
+            ref.at[:, pl.ds(p * span + half, half)],
+        )
+
+    gathers = [
+        Gather(
+            cut(back_ref, p), lambda c, p=p: cut(heads_ref.at[c], p),
+            sends.at[p], recvs.at[p], local.at[p],
+        )
+        for p in range(parts)
+    ]
+    gathers[0].start()
+    for p in range(parts):
+        gathers[p].forward()
+        if p + 1 < parts:
+            gathers[p + 1].start()
+        gathers[p].receive()
+        for c in range(count):
+            for h in range(heads):
+                at = (c * heads + h) * size
+                flat_ref[:, at : at + size] = heads_ref[c, h, pl.ds(p * span, span), :]
+        terms_ref[...] = matmul_nt(flat_ref[:, :piece], weight_ref[0])
+        for c in range(1, count):
+            terms_ref[...] += matmul_nt(flat_ref[:, c * piece : (c + 1) * piece], weight_ref[c])
+
+        def finish(t, carry):
+            inner = pl.ds(pl.multiple_of(t * 128, 128), 128)
+            here = pl.ds(pl.multiple_of(p * span + t * 128, 128), 128)
+            rest = [pieces_ref[c, here, :].astype(jnp.float32) for c in range(count)]
+            middle = jnp.concatenate(rest, axis=1) + terms_ref[inner, :]
+            rows_ref[...] = middle
+            middle_ref[here, :] = own_width(rows_ref, piece, col)
+            unit, inverse = normalize_rows(middle)
+            rows_ref[...] = unit
+            own_ref[here, :] = own_width(rows_ref, piece, col)
+            inverse_ref[here, :] = jnp.broadcast_to(inverse, (128, 128))
+            unit = unit.astype(jnp.bfloat16)
+            unit_ref[here, :] = unit
+            unit_t_ref[:, here] = unit.T
+            return carry
+
+        for t in range(span // 128):
+            finish(t, 0)
+    for one in gathers:
+        one.finish()
+
+
+def branch(back, weight, pieces):
+    heads, rows, size = back.shape
+    count, _, piece = pieces.shape
+    width = count * piece
+    hbm = pl.BlockSpec(memory_space=pl.ANY)
+    vmem = pl.BlockSpec(memory_space=pltpu.VMEM)
+    dma = pltpu.SemaphoreType.DMA
+    shape = jax.ShapeDtypeStruct
+    return pl.pallas_call(
+        branch_kernel,
+        in_specs=[hbm, vmem, vmem],
+        out_specs=[vmem] * 5,
+        out_shape=[
+            shape((rows, width), jnp.bfloat16),
+            shape((width, rows), jnp.bfloat16),
+            shape((rows, piece), jnp.float32),
+            shape((rows, piece), jnp.float32),
+            shape((rows, 128), jnp.float32),
+        ],
+        scratch_shapes=[
+            pltpu.VMEM((count, heads, rows, size), jnp.bfloat16),
+            pltpu.VMEM((rows // 2, width), jnp.bfloat16),
+            pltpu.VMEM((128, width), jnp.float32),
+            pltpu.VMEM((rows // 2, width), jnp.float32),
+            dma((2, 6)), dma((2, 6)), dma((2, 2)),
+        ],
+        compiler_params=pltpu.CompilerParams(
+            vmem_limit_bytes=56 * 2**20, collective_id=4, has_side_effects=True
+        ),
+        cost_estimate=pl.CostEstimate(
+            flops=2 * rows * width * width, bytes_accessed=40 * width * width, transcendentals=0
+        ),
+        name="branch",
+    )(back, weight, pieces)
+
+
+def project_grad_kernel(unit_t_ref, d_raw_ref, grad_ref, rows_ref):
+    owners, _, depth, _ = grad_ref.shape
+    for h in range(d_raw_ref.shape[0]):
+        rows_ref[:, h * HEAD : (h + 1) * HEAD] = d_raw_ref[h, 0]
+    for owner in range(owners):
+        grad_ref[owner, 0] = matmul(
+            unit_t_ref[owner * depth : (owner + 1) * depth, :], rows_ref[...]
+        ).astype(jnp.bfloat16)
+
+
+def project_grad(unit_t, d_raw, owners):
+    width, rows = unit_t.shape
+    heads, kinds = d_raw.shape[:2]
+    columns, depth = heads * HEAD, width // owners
+    return pl.pallas_call(
+        project_grad_kernel,
+        grid=(kinds,),
+        in_specs=[
+            resident((width, rows)),
+            pl.BlockSpec((heads, 1, rows, HEAD), lambda k: (0, k, 0, 0)),
+        ],
+        out_specs=pl.BlockSpec((owners, 1, depth, columns), lambda k: (0, k, 0, 0)),
+        out_shape=jax.ShapeDtypeStruct((owners, kinds, depth, columns), jnp.bfloat16),
+        scratch_shapes=[pltpu.VMEM((rows, columns), jnp.bfloat16)],
+        compiler_params=pltpu.CompilerParams(vmem_limit_bytes=40 * 2**20),
+        cost_estimate=pl.CostEstimate(
+            flops=2 * rows * width * kinds * columns, bytes_accessed=2 * width * kinds * columns,
+            transcendentals=0,
+        ),
+        name="project_grad",
+    )(unit_t, d_raw)
+
+
+def stats_of(values, unit):
+    rows = values.shape[0]
+    lane = lax.broadcasted_iota(jnp.int32, (rows, 128), 1)
+    both = jnp.where(
+        lane % 8 < 4,
+        jnp.sum(values, axis=1, keepdims=True),
+        jnp.sum(values * unit, axis=1, keepdims=True),
+    )
+    return both.T[:8]
+
+
+def columns_of(stats):
+    back = jnp.concatenate([stats] * 16, axis=0).T
+    return back[:, :1], back[:, 4:5]
+
+
+class Scatter:
+    def __init__(self, pieces, slots, stats, stat_slots, here, sends, recvs):
+        me = lax.axis_index("col")
+        self.copies = []
+        for by in range(1, pieces.shape[0]):
+            device = col_device(by)
+            self.copies.append(
+                send(pieces.at[me ^ by, here], slots.at[by - 1, here],
+                     sends.at[0, by - 1], recvs.at[0, by - 1], device)
+            )
+            if stats is not None:
+                self.copies.append(
+                    send(stats.at[:, here], stat_slots.at[by - 1, :, here],
+                         sends.at[1, by - 1], recvs.at[1, by - 1], device)
+                )
+
+    def start(self):
+        for one in self.copies:
+            one.start()
+
+    def receive(self):
+        for one in self.copies:
+            one.wait_recv()
+
+    def finish(self):
+        for one in self.copies:
+            one.wait_send()
+
+
+def split_rows(sum_ref, unit_ref, pieces_ref, stats_ref, start, size):
+    count, _, width = pieces_ref.shape
+    for t in range(start, start + size, 128):
+        here = pl.ds(t, 128)
+        values = sum_ref[here, :]
+        stats_ref[:, here] = stats_of(values, unit_ref[here, :].astype(jnp.float32))
+        for c in range(count):
+            pieces_ref[c, here, :] = values[:, c * width : (c + 1) * width].astype(jnp.bfloat16)
+
+
+def normed_grad(sum_ref, slots, stats_ref, stat_slots, own_ref, inverse_ref, here, width, col):
+    piece = slots.shape[2]
+    grad = sum_ref[here, pl.ds(pl.multiple_of(col * piece, piece), piece)]
+    stats = stats_ref[:, here]
+    for by in range(slots.shape[0]):
+        grad = grad + slots[by, here, :].astype(jnp.float32)
+        stats = stats + stat_slots[by, :, here]
+    sums, cross = columns_of(stats)
+    return normalize_back(grad, sums, cross, own_ref[here, :], inverse_ref[here, :1], float(width))
+
+
+def leave_kernel(
+    d_raw_ref, weight_ref, unit_ref, own_ref, inverse_ref, d_middle_ref, out_ref,
+    rows_ref, sum_ref, pieces_ref, slots_ref, stats_ref, stat_slots_ref, weights_ref,
+    sends, recvs, load,
+):
+    col = lax.axis_index("col")
+    rows, width = unit_ref.shape
+    heads, kinds = d_raw_ref.shape[:2]
+    columns = heads * HEAD
+    loads = [
+        pltpu.make_async_copy(weight_ref.at[:, k], weights_ref.at[k], load.at[k]) for k in range(kinds)
+    ]
+    for one in loads:
+        one.start()
+    greet_cols(pieces_ref.shape[0])
+    for k in range(kinds):
+        for h in range(heads):
+            rows_ref[k, :, h * HEAD : (h + 1) * HEAD] = d_raw_ref[h, k]
+    for one in loads:
+        one.wait()
+    parts = 2
+    span = rows // parts
+    moves = []
+    for p in range(parts):
+        here = pl.ds(p * span, span)
+        sum_ref[here, :] = matmul_nt(rows_ref[0, here, :], weights_ref[0].reshape(width, columns))
+        for k in range(1, kinds):
+            sum_ref[here, :] += matmul_nt(
+                rows_ref[k, here, :], weights_ref[k].reshape(width, columns)
+            )
+        split_rows(sum_ref, unit_ref, pieces_ref, stats_ref, p * span, span)
+        moves.append(
+            Scatter(pieces_ref, slots_ref, stats_ref, stat_slots_ref, here, sends.at[p], recvs.at[p])
+        )
+        moves[p].start()
+    for p in range(parts):
+        moves[p].receive()
+        for t in range(p * span, (p + 1) * span, 128):
+            here = pl.ds(t, 128)
+            out_ref[here, :] = d_middle_ref[here, :] + normed_grad(
+                sum_ref, slots_ref, stats_ref, stat_slots_ref, own_ref, inverse_ref, here, width, col
+            )
+    for one in moves:
+        one.finish()
+
+
+def leave(d_raw, weight, unit, own, inverse, d_middle, count):
+    rows, width = unit.shape
+    heads, kinds = d_raw.shape[:2]
+    owners, _, depth, columns = weight.shape
+    piece = width // count
+    hbm = pl.BlockSpec(memory_space=pl.ANY)
+    vmem = pl.BlockSpec(memory_space=pltpu.VMEM)
+    dma = pltpu.SemaphoreType.DMA
+    return pl.pallas_call(
+        leave_kernel,
+        in_specs=[vmem, hbm] + [vmem] * 4,
+        out_specs=vmem,
+        out_shape=jax.ShapeDtypeStruct((rows, piece), jnp.float32),
+        scratch_shapes=[
+            pltpu.VMEM((kinds, rows, columns), jnp.bfloat16),
+            pltpu.VMEM((rows, width), jnp.float32),
+            pltpu.VMEM((count, rows, piece), jnp.bfloat16),
+            pltpu.VMEM((count - 1, rows, piece), jnp.bfloat16),
+            pltpu.VMEM((8, rows), jnp.float32),
+            pltpu.VMEM((count - 1, 8, rows), jnp.float32),
+            pltpu.VMEM((kinds, owners, depth, columns), jnp.bfloat16),
+            dma((2, 2, count - 1)), dma((2, 2, count - 1)), dma((kinds,)),
+        ],
+        compiler_params=pltpu.CompilerParams(
+            vmem_limit_bytes=60 * 2**20, collective_id=5, has_side_effects=True
+        ),
+        cost_estimate=pl.CostEstimate(
+            flops=2 * rows * width * kinds * columns, bytes_accessed=100 * rows * width, transcendentals=0
+        ),
+        name="leave",
+    )(d_raw, weight, unit, own, inverse, d_middle)
+
+
+def feed_front(unit_ref, cot_ref, weight_ref, two_ref, act):
+    owners, _, _, depth, cols = weight_ref.shape
+    rows, width = unit_ref.shape
+    count, _, piece = cot_ref.shape
+    gate_weight = weight_ref[:, 0, 0].reshape(width, cols)
+    up_weight = weight_ref[:, 0, 1].reshape(width, cols)
+    down_weight = weight_ref[:, 0, 2].reshape(width, cols)
+    step = min(256, rows)
+    for t in range(0, rows, step):
+        here = pl.ds(t, step)
+        unit = unit_ref[here, :]
+        gate = matmul(unit, gate_weight)
+        up_proj = matmul(unit, up_weight)
+        d_hidden = sum(
+            matmul(cot_ref[c, here, :], down_weight[c * piece : (c + 1) * piece])
+            for c in range(count)
+        )
+        sigmoid_gate = jax.nn.sigmoid(gate)
+        silu_gate = gate * sigmoid_gate
+        act[0, here, :] = (silu_gate * up_proj).astype(jnp.bfloat16)
+        act[1, here, :] = (
+            d_hidden * up_proj * sigmoid_gate * (1.0 + gate * (1.0 - sigmoid_gate))
+        ).astype(jnp.bfloat16)
+        act[2, here, :] = (d_hidden * silu_gate).astype(jnp.bfloat16)
+    for t in range(0, rows, step):
+        here = pl.ds(t, step)
+        two_ref[here, :] += matmul_nt(act[1, here, :], gate_weight) + matmul_nt(
+            act[2, here, :], up_weight
+        )
+
+
+def feed_rear(unit_t_ref, cot_t_ref, down_weight, grad_ref, out_ref, act):
+    owners, _, _, depth, cols = grad_ref.shape
+    if out_ref is not None:
+        rows = out_ref.shape[0]
+        step = min(256, rows)
+        for t in range(0, rows, step):
+            here = pl.ds(t, step)
+            out_ref[here, :] += matmul_nt(act[0, here, :], down_weight)
+    hidden, d_gate, d_up = act[0], act[1], act[2]
+    for owner in range(owners):
+        here = pl.ds(owner * depth, depth)
+        unit_t = unit_t_ref[here, :]
+        grad_ref[owner, 0, 0] = matmul(unit_t, d_gate).astype(jnp.bfloat16)
+        grad_ref[owner, 0, 1] = matmul(unit_t, d_up).astype(jnp.bfloat16)
+        grad_ref[owner, 0, 2] = matmul(cot_t_ref[here, :], hidden).astype(jnp.bfloat16)
+
+
+def feed_all_kernel(
+    unit_ref, unit_t_ref, cot_ref, cot_t_ref, weight_ref, *refs
+):
+    old = refs[:-7]
+    grad_ref, new_two_ref, new_out_ref, two_ref, out_ref, act_ref, sem = refs[-7:]
+    tile = pl.program_id(0)
+
+    @pl.when(tile == 0)
+    def _():
+        if old:
+            loads = [
+                pltpu.make_async_copy(old[0], two_ref, sem.at[0]),
+                pltpu.make_async_copy(old[1], out_ref, sem.at[1]),
+            ]
+            for load in loads:
+                load.start()
+            for load in loads:
+                load.wait()
+        else:
+            two_ref[...] = jnp.zeros_like(two_ref)
+            out_ref[...] = jnp.zeros_like(out_ref)
+
+    feed_front(unit_ref, cot_ref, weight_ref, two_ref, act_ref)
+    final = tile == pl.num_programs(0) - 1
+    copies = [
+        pltpu.make_async_copy(two_ref, new_two_ref, sem.at[0]),
+        pltpu.make_async_copy(out_ref, new_out_ref, sem.at[1]),
+    ]
+
+    @pl.when(final)
+    def _():
+        copies[0].start()
+
+    down_weight = weight_ref[:, 0, 2].reshape(unit_ref.shape[1], weight_ref.shape[4])
+    feed_rear(unit_t_ref, cot_t_ref, down_weight, grad_ref, out_ref, act_ref)
+
+    @pl.when(final)
+    def _():
+        copies[1].start()
+        for copy in copies:
+            copy.wait()
+
+
+def feed_cost(rows, width, owners, tiles, depth, cols, matmuls):
+    return pl.CostEstimate(
+        flops=2 * matmuls * rows * width * tiles * cols,
+        bytes_accessed=12 * owners * tiles * depth * cols,
+        transcendentals=rows * tiles * cols,
+    )
+
+
+def feed_all(unit, unit_t, cot, cot_t, weights, old):
+    rows, width = unit.shape
+    owners, tiles, _, depth, cols = weights.shape
+    block = pl.BlockSpec((owners, 1, 3, depth, cols), lambda i: (0, i, 0, 0, 0))
+    hbm = pl.BlockSpec(memory_space=pl.ANY)
+    return pl.pallas_call(
+        feed_all_kernel,
+        grid=(tiles,),
+        in_specs=[
+            resident((rows, width)), resident((width, rows)), resident(cot.shape),
+            resident((width, rows)), block,
+        ] + [hbm] * len(old),
+        out_specs=[block, hbm, hbm],
+        out_shape=[jax.ShapeDtypeStruct(weights.shape, jnp.bfloat16)]
+        + [jax.ShapeDtypeStruct((rows, width), jnp.float32)] * 2,
+        scratch_shapes=[
+            pltpu.VMEM((rows, width), jnp.float32),
+            pltpu.VMEM((rows, width), jnp.float32),
+            pltpu.VMEM((3, rows, cols), jnp.bfloat16),
+            pltpu.SemaphoreType.DMA((2,)),
+        ],
+        compiler_params=pltpu.CompilerParams(vmem_limit_bytes=62 * 2**20),
+        cost_estimate=feed_cost(rows, width, owners, tiles, depth, cols, 9),
+        name="feed_all",
+    )(unit, unit_t, cot, cot_t, weights, *old)
+
+
+def feed_last_kernel(
+    unit_hbm, unit_t_hbm, cots_hbm, cot_t_hbm, weight_hbm, old_two_hbm, old_out_hbm, own_ref,
+    inverse_ref, out_t_ref, back_ref,
+    grad_ref, ffn_ref, d_middle_ref, d_sent_ref, out_grad_ref,
+    unit_ref, turned_ref, cots_ref, weight_ref, two_ref, sum_ref, act_ref, pieces_ref, slots_ref,
+    stats_ref, stat_slots_ref, d_pieces_ref,
+    load, sends, recvs, g_sends, g_recvs,
+):
+    col = lax.axis_index("col")
+    rows, width = unit_ref.shape
+    count, _, piece = pieces_ref.shape
+    owners, tiles, _, depth, cols = weight_ref.shape
+    heads, _, size = back_ref.shape
+
+    def fetch(i, source, target):
+        copy = pltpu.make_async_copy(source, target, load.at[i])
+        copy.start()
+        return copy
+
+    loads = [
+        fetch(0, unit_hbm, unit_ref), fetch(1, weight_hbm, weight_ref), fetch(2, cots_hbm, cots_ref),
+        fetch(3, old_two_hbm, two_ref), fetch(4, unit_t_hbm, turned_ref.at[0]),
+        fetch(5, cot_t_hbm, turned_ref.at[1]), fetch(6, old_out_hbm.at[: rows // 2], sum_ref),
+    ]
+    greet_cols(count)
+    for i in range(4):
+        loads[i].wait()
+    for tile in range(tiles):
+        feed_front(unit_ref, cots_ref, weight_ref.at[:, tile : tile + 1], two_ref, act_ref.at[tile])
+    parts = 2
+    span = rows // parts
+    moves, gathers = [], []
+    for p in range(parts):
+        split_rows(two_ref, unit_ref, pieces_ref, stats_ref, p * span, span)
+        moves.append(
+            Scatter(pieces_ref, slots_ref, stats_ref, stat_slots_ref, pl.ds(p * span, span),
+                    sends.at[p], recvs.at[p])
+        )
+        moves[p].start()
+        own = d_pieces_ref.at[col]
+        gathers.append(
+            Gather(
+                halves(own, p * span, span),
+                lambda c, p=p: halves(d_pieces_ref.at[c], p * span, span),
+                g_sends.at[p], g_recvs.at[p], None,
+            )
+        )
+    for p in range(2):
+        loads[6 + p].wait()
+        for tile in range(tiles):
+            down_weight = weight_ref[:, tile, 2].reshape(width, cols)
+            sum_ref[...] += matmul_nt(act_ref[tile, 0, pl.ds(p * span, span), :], down_weight)
+        for c in range(count):
+            ffn_ref[c, pl.ds(p * span, span), :] = sum_ref[
+                :, c * piece : (c + 1) * piece
+            ].astype(jnp.bfloat16)
+        if p == 0:
+            loads.append(fetch(7, old_out_hbm.at[rows // 2 :], sum_ref))
+    for i in range(4, 6):
+        loads[i].wait()
+    for tile in range(tiles):
+        feed_rear(
+            turned_ref.at[0], turned_ref.at[1], None, grad_ref.at[:, tile : tile + 1], None,
+            act_ref.at[tile],
+        )
+    own_cot = cots_ref.at[col]
+    for p in range(parts):
+        moves[p].receive()
+        for t in range(p * span, (p + 1) * span, 128):
+            here = pl.ds(t, 128)
+            d_middle = own_cot[here, :].astype(jnp.float32) + normed_grad(
+                two_ref, slots_ref, stats_ref, stat_slots_ref, own_ref, inverse_ref, here, width, col
+            )
+            d_middle_ref[here, :] = d_middle
+            d_pieces_ref[col, here, :] = d_middle.astype(jnp.bfloat16)
+        gathers[p].start()
+    for p in range(parts):
+        gathers[p].forward()
+        gathers[p].receive()
+        here = pl.ds(p * span, span)
+        d_attended = matmul(d_pieces_ref[0, here, :], out_t_ref[:piece, :])
+        for c in range(1, count):
+            d_attended += matmul(
+                d_pieces_ref[c, here, :], out_t_ref[c * piece : (c + 1) * piece, :]
+            )
+        for h in range(heads):
+            d_sent_ref[h, here, :] = d_attended[:, h * size : (h + 1) * size].astype(jnp.bfloat16)
+    per_piece = piece // depth
+    for owner in range(owners):
+        at = (owner % per_piece) * depth
+        d_branch = d_pieces_ref[owner // per_piece, :, at : at + depth]
+        for h in range(heads):
+            out_grad_ref[owner, h * size : (h + 1) * size, :] = lax.dot_general(
+                back_ref[h], d_branch, (((0,), (0,)), ((), ())), preferred_element_type=jnp.float32
+            ).astype(jnp.bfloat16)
+    for one in moves + gathers:
+        one.finish()
+
+
+def feed_last(unit, unit_t, cots, cot_t, weights, old, own, inverse, out_t, back):
+    rows, width = unit.shape
+    count, _, piece = cots.shape
+    owners, tiles, _, depth, cols = weights.shape
+    heads, _, size = back.shape
+    hbm = pl.BlockSpec(memory_space=pl.ANY)
+    vmem = pl.BlockSpec(memory_space=pltpu.VMEM)
+    dma = pltpu.SemaphoreType.DMA
+    shape = jax.ShapeDtypeStruct
+    return pl.pallas_call(
+        feed_last_kernel,
+        in_specs=[hbm] * 7 + [vmem] * 4,
+        out_specs=[vmem] * 5,
+        out_shape=[
+            shape(weights.shape, jnp.bfloat16),
+            shape((count, rows, piece), jnp.bfloat16),
+            shape((rows, piece), jnp.float32),
+            shape((heads, rows, size), jnp.bfloat16),
+            shape((owners, heads * size, depth), jnp.bfloat16),
+        ],
+        scratch_shapes=[
+            pltpu.VMEM((rows, width), jnp.bfloat16),
+            pltpu.VMEM((2, width, rows), jnp.bfloat16),
+            pltpu.VMEM((count, rows, piece), jnp.bfloat16),
+            pltpu.VMEM(weights.shape, jnp.bfloat16),
+            pltpu.VMEM((rows, width), jnp.float32),
+            pltpu.VMEM((rows // 2, width), jnp.float32),
+            pltpu.VMEM((tiles, 3, rows, cols), jnp.bfloat16),
+            pltpu.VMEM((count, rows, piece), jnp.bfloat16),
+            pltpu.VMEM((count - 1, rows, piece), jnp.bfloat16),
+            pltpu.VMEM((8, rows), jnp.float32),
+            pltpu.VMEM((count - 1, 8, rows), jnp.float32),
+            pltpu.VMEM((count, rows, piece), jnp.bfloat16),
+            dma((8,)), dma((2, 2, count - 1)), dma((2, 2, count - 1)), dma((2, 6)), dma((2, 6)),
+        ],
+        compiler_params=pltpu.CompilerParams(
+            vmem_limit_bytes=63 * 2**20 + 2**19, collective_id=6, has_side_effects=True
+        ),
+        cost_estimate=pl.CostEstimate(
+            flops=18 * rows * width * tiles * cols, bytes_accessed=100 * rows * width,
+            transcendentals=rows * cols,
+        ),
+        name="feed_last",
+    )(unit, unit_t, cots, cot_t, weights, *old, own, inverse, out_t, back)
+
+
+def group_tables(lengths, group):
+    row_lengths = lax.dynamic_slice_in_dim(lengths, group, 1, 0)[0]
+    local_index = jnp.arange(GROUP_LEN, dtype=jnp.int32)
+    seg_ends = jnp.cumsum(row_lengths)
+    seg_starts = seg_ends - row_lengths
+    after_prompt = local_index - PROMPT
+    inside = (after_prompt[:, None] >= seg_starts[None, :]) & (
+        after_prompt[:, None] < seg_ends[None, :]
+    )
+    start = jnp.sum(jnp.where(inside, seg_starts[None, :], 0), axis=1)
+    in_prompt = local_index < PROMPT
+    start_row = jnp.where(in_prompt, 0, PROMPT + start)
+    position = jnp.where(in_prompt, local_index, PROMPT + after_prompt - start)
+    half = HEAD // 2
+    frequency = jnp.exp(
+        -math.log(rope_base) * (2.0 * jnp.arange(half, dtype=jnp.float32) / HEAD)
+    )
+    angles = position.astype(jnp.float32)[:, None] * frequency[None, :]
+    cosine, sine = jnp.cos(angles), jnp.sin(angles)
+    return (
+        start_row.reshape(GROUP_LEN // BLOCK, 1, BLOCK),
+        jnp.concatenate([cosine, cosine], axis=1),
+        jnp.concatenate([sine, -sine], axis=1),
+    )
+
+
+def fast_body(
+    inputs,
+    cotangent,
+    lengths,
+    query_key_value_weight,
+    out_weight,
+    gate_weight,
+    up_weight,
+    down_weight,
+):
+    tok_rows, part_width = inputs.shape
+    col_count = lax.axis_size("col")
+    col_index = lax.axis_index("col")
+    row_index = lax.axis_index("row")
+    span = GROUP_LEN // tok_rows
+    groups_here = lax.axis_size("row") // span
+    heads_here = part_width // HEAD
+    place = row_index // groups_here
+    group = row_index % groups_here
+    depth = gate_weight.shape[0]
+    hidden_here = gate_weight.shape[1]
+    tiles = hidden_here // min(256, depth)
+    tile = hidden_here // tiles
+
+    def gather(shard, after=None):
+        if after is not None:
+            shard, after = tied(shard, after)
+        return lax.all_gather(shard, "row"), after
+
+    def tied(value, *others):
+        return lax.optimization_barrier((value, *others))
+
+    mixed = jnp.concatenate([query_key_value_weight.transpose(1, 0, 2), out_weight.T[None]])
+    weights, _ = gather(mixed)
+    packed = jnp.stack([gate_weight, up_weight, down_weight.T]).reshape(3, depth, tiles, tile)
+    packed = packed.transpose(2, 0, 1, 3)
+    last = max(1, tiles // 8)
+    first = tiles // 2
+    start_rows, cosine, sine = lax.optimization_barrier(group_tables(lengths, group))
+    own_cos = lax.dynamic_slice_in_dim(
+        cosine.reshape(span, tok_rows, HEAD), place, 1, 0
+    )[0]
+    own_sin = lax.dynamic_slice_in_dim(sine.reshape(span, tok_rows, HEAD), place, 1, 0)[0]
+
+    early_inputs, own_cos = tied(inputs, own_cos)
+    pieces, cots, normed_one, unit_one_t, unit_one, inverse_one = enter(
+        early_inputs, cotangent, col_count
+    )
+    normed_one, weights = tied(normed_one, weights)
+    feed_one, weights = gather(packed[:first], weights)
+    sent = project(normed_one, weights, own_cos, own_sin)
+    out_rows_t = weights[:, 3].reshape(-1, part_width)
+    back, held, attended_head, lse, out_t = attend(
+        sent, start_rows, out_rows_t, groups_here, col_count
+    )
+    back, feed_one = tied(back, feed_one)
+    feed_two, feed_one = gather(packed[first:-last], feed_one)
+    normed_two, unit_t, middle, unit_two, inverse_two = branch(back, out_t, pieces)
+    cot_t = cots.transpose(0, 2, 1).reshape(-1, tok_rows)
+    rows_two = (normed_two, unit_t, cots, cot_t)
+
+    def owned(part):
+        return lax.psum_scatter(part, "row", scatter_dimension=0, tiled=True)[0]
+
+    grads_one, *sums = feed_all(*rows_two, feed_one, ())
+    sums[0], feed_two = tied(sums[0], feed_two)
+    feed_three, feed_two = gather(packed[-last:], feed_two)
+    grads_two, *sums = feed_all(*rows_two, feed_two, sums)
+    sums[0], grads_one, feed_three = tied(sums[0], grads_one, feed_three)
+    grads_one = owned(grads_one)
+    grads_three, ffn_pieces, d_middle, d_sent, out_part = feed_last(
+        *rows_two, feed_three, sums, unit_two, inverse_two, out_rows_t, back
+    )
+    d_sent, grads_one = tied(d_sent, grads_one)
+    grads_two, grads_one = tied(grads_two, grads_one)
+    grads_two = owned(grads_two)
+    d_raw, ffn_others = attend_back(
+        d_sent, held, attended_head, lse, start_rows, cosine, sine, ffn_pieces, groups_here
+    )
+    projection_part = project_grad(unit_one_t, d_raw, weights.shape[0])
+    projection_part, grads_two = tied(projection_part, grads_two)
+    blocks = out_part.reshape(out_part.shape[0], -1, tile, depth)
+    late = jnp.concatenate(
+        [grads_three.reshape(out_part.shape[0], -1, depth, tile), blocks], axis=1
+    )
+    late, grads_two = tied(late, grads_two)
+    late = owned(late)
+    input_grad = leave(
+        d_raw, weights, normed_one, unit_one, inverse_one, d_middle, col_count
+    )
+    projection_part, late, input_grad = tied(projection_part, late, input_grad)
+    own_grads = owned(projection_part)
+    own_ffn = lax.dynamic_slice_in_dim(ffn_pieces, col_index, 1, 0)[0]
+    output = middle + own_ffn.astype(jnp.float32) + jnp.sum(ffn_others.astype(jnp.float32), axis=0)
+    output = output.astype(jnp.bfloat16)
+    qkv_grad = own_grads.astype(jnp.float32).transpose(1, 0, 2)
+    grads_three = late[: 3 * last].reshape(last, 3, depth, tile)
+    out_grad = late[3 * last :].reshape(part_width, depth).astype(jnp.float32)
+    grads = jnp.concatenate([grads_one, grads_two, grads_three]).astype(jnp.float32)
+    grads = grads.transpose(1, 2, 0, 3).reshape(3, depth, hidden_here)
+    return (output, input_grad, qkv_grad, out_grad, grads[0], grads[1], grads[2].T)
 
 
 def body(
@@ -367,6 +1688,13 @@
     )
 
 
+def step(inputs, *rest):
+    span = GROUP_LEN // inputs.shape[0]
+    heads_here = inputs.shape[1] // HEAD
+    fast = heads_here == span and lax.axis_size("col") == 4
+    return (fast_body if fast else body)(inputs, *rest)
+
+
 def solution(mesh):
     placed = (
         P("row", "col"),
@@ -379,7 +1707,7 @@
         P("col", "row"),
     )
     return jax.shard_map(
-        body,
+        step,
         mesh=mesh,
         in_specs=placed,
         out_specs=(

time: 1690 us -> 969 us (0.57)
  waiting for transfers between devices: 1180 us -> 91.8 us
  Pallas kernels: 0 us -> 758 us
  matrix products: 272 us -> 0 us
  other arithmetic: 79.1 us -> 26.8 us
  loops' own time: 32.3 us -> 0 us
  blocking collectives: 31.8 us -> 0 us
    pallas_call x0 -> x10, Pallas kernels: none -> 758 us  [the longest x1 168 us: attend(): pl.pallas_call(functools.partial(attend_kernel, groups_here), in_specs=[h...]
    ppermute x12 -> x0, waiting for transfers between devices: 373 us -> none  [passed_along(): return lax.ppermute(shard, axis, pairs)]
    all_gather x8 -> x4, waiting for transfers between devices: 370 us -> 12.1 us  [gather(): return (lax.all_gather(shard, 'row'), after)]
    dot_general x24 -> x0, matrix products: 272 us -> none  [the longest x3 24.5 us: score_block(): jnp.einsum('qhd,khd->hqk', queries, key_part, preferred_element_type=jnp....]
    psum x1 -> x0, waiting for transfers between devices: 234 us -> none  [body(): branch_full = lax.psum(branch_terms, 'col')]
    reduce_scatter x8 -> x4, waiting for transfers between devices: 201 us -> 79.6 us  [owned(): return lax.psum_scatter(part, 'row', scatter_dimension=0, tiled=True)[0]]
    another operation x15 -> x0, loops' own time: 32.3 us -> none  [the longest x4 31.1 us: body(): lax.cond(live_piece[shift_by], piece_grads, lambda query_total: (query_to...]
    unnamed x2 -> x0, blocking collectives: 31.8 us -> none
  transfers between devices with their start and end apart: 29 -> 8, of which waited for: 20 -> 4; matrix products, arithmetic and copies ran while one was open for 19% -> 5% of each run, Pallas kernels for 0% -> 79%
where the time goes in v2:
time: 969 us; the launch traced here: 962 us
  Pallas kernels  758 us (78%)
  waiting for transfers between devices  91.8 us (9%)
  local copies, waits for them, and re-layouts  57.5 us (6%)
  other arithmetic  26.8 us (3%)
  between operations  14.8 us (2%)
  starting transfers between devices  13.1 us (1%)
    pallas_call x1, Pallas kernels, attend(): pl.pallas_call(functools.partial(attend_kernel, groups_here), in_specs=[h...  168 us
    pallas_call x1, Pallas kernels, attend_back(): pl.pallas_call(functools.partial(attend_back_kernel, groups_here), in_spe...  166 us
    pallas_call x1, Pallas kernels, feed_last(): pl.pallas_call(feed_last_kernel, in_specs=[hbm] * 7 + [vmem] * 4, out_spe...  111 us
    pallas_call x2, Pallas kernels, feed_all(): pl.pallas_call(feed_all_kernel, grid=(tiles,), in_specs=[resident((rows,...  97.8 us
    reduce_scatter x4, waiting for transfers between devices, owned(): return lax.psum_scatter(part, 'row', scatter_dimension=0, tiled=True)[0]  79.6 us
    pallas_call x1, Pallas kernels, enter(): pl.pallas_call(enter_kernel, in_specs=[hbm, hbm], out_specs=[hbm, hbm, vm...  76.1 us
    pallas_call x1, Pallas kernels, leave(): pl.pallas_call(leave_kernel, in_specs=[vmem, hbm] + [vmem] * 4, out_specs...  64.5 us
    pallas_call x1, Pallas kernels, branch(): pl.pallas_call(branch_kernel, in_specs=[hbm, vmem, vmem], out_specs=[vmem...  54.8 us
  transfers between devices with their start and end apart: 8, of which 4 were waited for; matrix products, arithmetic and copies ran while one was open for 5% of the time, Pallas kernels for 79%

profile of v2, /device:TPU:0, one launch (start us, length us, event | category | flops | bytes accessed | tf_op | source)
XLA Modules:
  0.0 962.3 jit_solution(4781707367634986989)
XLA Ops:
  15.5 7.5 multiply_sine_fusion
  27.6 76.1 %enter.1 = (bf16[4,1024,512]{2,1,0:T(8,128)(2,1)S(1)}, bf16[4,1024,512]{2,1,0:T(8,128)(2,1)S(1)}, bf16[1024,2048]{1,0:T(8,128)(2,1)}, bf16[2048,1024]{1,0:T(8,12...) custom-call(bf16[1024,512]{1,0:T(8,128)(2,1)S(1)} %copy-done.5, bf16[1024,512]{1,0:T(8,128)(2,1)S(1)} %copy-done.6), custom_call_target="tpu_custom_call" | custom-call | flops 20971520 | bytes 209715200 | tf_op jit(solution)/shard_map/enter/pallas_call | solution.py:663
  109.9 2.6 copy.44
  112.5 12.4 %all-gather.13.cloned.1.call-start = ((), (), s32[]{:S(2)}) async-start(), calls=%async_computation.10 | async-start | bytes 10616832 | tf_op jit(solution)/shard_map/all_gather | solution.py:1341
  128.2 12.9 %project.1.sent_ref = bf16[4,3,1024,128]{3,2,1,0:T(8,128)(2,1)S(1)} custom-call(bf16[1024,2048]{1,0:T(8,128)(2,1)S(1)} %copy-done.9, bf16[8,4,256,512]{3,2,1,0:T(8,128)(2,1)} %bitcast.83, f32[1024,128]{1,0:T(8,128)S(1)} %copy-done.8, f32[1024,128]{1,0:T(8,128)S(1)} %dynamic-slice_bitcast_fusion.sin_ref), custom_call_target="tpu_custom_call" | custom-call | flops 6442450944 | bytes 6291456 | tf_op jit(solution)/shard_map/project/pallas_call | solution.py:722
  141.2 168.3 %attend.1 = (bf16[4,1024,128]{2,1,0:T(8,128)(2,1)S(1)}, bf16[3,4096,128]{2,1,0:T(8,128)(2,1)S(1)}, bf16[4096,128]{1,0:T(8,128)(2,1)S(1)}, f32[8,1,512]{2,1,0:T(1,128)S(1)}, bf16[4,2048,512]{2,1,0:T(8,128)(2,1)S(1)}) custom-call(bf16[4,3,1024,128]{3,2,1,0:T(8,128)(2,1)S(1)} %project.1.sent_ref, s32[8,1,512]{2,1,0:T(1,128)S(1)} %compare_select_fusion.start_ref, ...), custom_call_target="tpu_custom_call" | custom-call | flops 4294967296 | bytes 104857600 | tf_op jit(solution)/shard_map/attend/pallas_call | solution.py:374
  310.4 3.3 copy-done.16
  318.0 6.3 copy.45
  324.2 54.8 %branch.1 = (bf16[1024,2048]{1,0:T(8,128)(2,1)}, bf16[2048,1024]{1,0:T(8,128)(2,1)}, f32[1024,512]{1,0:T(8,128)}, f32[1024,512]{1,0:T(8,128)}, f32[1024,128]{1,0:T(8,128)}) custom-call(bf16[4,1024,128]{2,1,0:T(8,128)(2,1)} %copy-done.7, bf16[4,2048,512]{2,1,0:T(8,128)(2,1)} %copy-done.16, bf16[4,1024,512]{2,1,0:T(8,128)(2,1)} %copy-done.11), custom_call_target="tpu_custom_call" | custom-call | flops 8589934592 | bytes 167772160 | tf_op jit(solution)/shard_map/branch/pallas_call | solution.py:811
  379.0 51.5 %feed_all.2 = (bf16[8,4,3,256,256]{4,3,2,1,0:T(8,128)(2,1)}, f32[1024,2048]{1,0:T(8,128)}, f32[1024,2048]{1,0:T(8,128)}) custom-call(bf16[1024,2048]{1,0:T(8,128)(2,1)} %get-tuple-element.82.unit_ref.unit_hbm, bf16[2048,1024]{1,0:T(8,128)(2,1)} %get-tuple-element.83.unit_t_ref.unit_t_hbm, bf16[4,1024,512]{2,1,0:T(8,128)(2,1)} %copy-done, ...), custom_call_target="tpu_custom_call" | custom-call | flops 38654705664 | bytes 25165824 | tf_op jit(solution)/shard_map/feed_all/pallas_call | solution.py:1121
  431.5 46.4 %feed_all.3 = (bf16[8,3,3,256,256]{4,3,2,1,0:T(8,128)(2,1)}, f32[1024,2048]{1,0:T(8,128)}, f32[1024,2048]{1,0:T(8,128)}) custom-call(bf16[1024,2048]{1,0:T(8,128)(2,1)} %get-tuple-element.82.unit_ref.unit_hbm, bf16[2048,1024]{1,0:T(8,128)(2,1)} %get-tuple-element.83.unit_t_ref.unit_t_hbm, bf16[4,1024,512]{2,1,0:T(8,128)(2,1)} %copy-done, ...), custom_call_target="tpu_custom_call" | custom-call | flops 28991029248 | bytes 18874368 | tf_op jit(solution)/shard_map/feed_all/pallas_call | solution.py:1121
  477.9 12.1 %all-gather.15.cloned.1.call-done = bf16[8,3,256,256]{3,2,1,0:T(8,128)(2,1)} async-done(((bf16[1,3,256,256]{3,2,1,0:T(8,128)(2,1)}), bf16[8,3,256,256]{3,2,1,0:T(8,128)(2,1)}) %all-gather.15.cloned.1.call-update) | async-done | bytes 3145744 | tf_op jit(solution)/shard_map/all_gather | solution.py:1341
  490.3 110.6 %feed_last.1 = (bf16[8,1,3,256,256]{4,3,2,1,0:T(8,128)(2,1)}, bf16[4,1024,512]{2,1,0:T(8,128)(2,1)}, f32[1024,512]{1,0:T(8,128)}, bf16[4,1024,128]{2,1,0:T(8,128)(2,1)}, bf16[8,512,256]{2,1,0:T(8,128)(2,1)}) custom-call(bf16[1024,2048]{1,0:T(8,128)(2,1)} %get-tuple-element.82.unit_ref.unit_hbm, bf16[2048,1024]{1,0:T(8,128)(2,1)} %get-tuple-element.83.unit_t_ref.unit_t_hbm, ...), custom_call_target="tpu_custom_call" | custom-call | flops 9663676416 | bytes 209715200 | tf_op jit(solution)/shard_map/feed_last/pallas_call | solution.py:1251
  601.0 26.8 %reduce-scatter.5.cloned.1.call-done = bf16[1,4,3,256,256]{4,3,2,1,0:T(8,128)(2,1)} async-done(((bf16[8,4,3,256,256]{4,3,2,1,0:T(8,128)(2,1)}), bf16[1,4,3,256,256]{4,3,2,1,0:T(8,128)(2,1)}) %reduce-scatter.5.cloned.1.call-update) | async-done | bytes 1572880 | tf_op jit(solution)/shard_map/reduce_scatter | solution.py:1376
  627.9 5.4 pad_maximum_fusion
  634.8 165.6 %attend_back.1 = (bf16[4,3,1024,128]{3,2,1,0:T(8,128)(2,1)}, bf16[3,1024,512]{2,1,0:T(8,128)(2,1)}) custom-call(bf16[4,1024,128]{2,1,0:T(8,128)(2,1)S(1)} %copy-done.13, bf16[3,4096,128]{2,1,0:T(8,128)(2,1)} %copy-done.17, bf16[4096,128]{1,0:T(8,128)(2,1)S(1)} %copy-done.19, f32[8,1,512]{2,1,0:T(1,128)S(1)} %get-tuple-element.107.lse_ref, ...), custom_call_target="tpu_custom_call" | custom-call | flops 10737418240 | bytes 104857600 | tf_op jit(solution)/shard_map/attend_back/pallas_call | solution.py:567
  802.3 7.8 project_grad.1
  810.2 2.7 copy-done.2
  813.1 64.5 %leave.1 = f32[1024,512]{1,0:T(8,128)} custom-call(bf16[4,3,1024,128]{3,2,1,0:T(8,128)(2,1)} %get-tuple-element.110.d_raw_ref, bf16[8,4,256,512]{3,2,1,0:T(8,128)(2,1)} %bitcast.84, bf16[1024,2048]{1,0:T(8,128)(2,1)} %get-tuple-element.70.unit_ref, f32[1024,512]{1,0:T(8,128)} %copy-done.12, f32[1024,128]{1,0:T(8,128)} %copy-done.14, ...), custom_call_target="tpu_custom_call" | custom-call | flops 6442450944 | bytes 209715200 | tf_op jit(solution)/shard_map/leave/pallas_call | solution.py:992
  877.6 3.4 reduce-scatter.9.cloned.1.call-done
  884.5 3.0 fusion.1
  889.3 2.6 fusion.5
  902.1 49.4 %reduce-scatter.11.cloned.1.call-done = bf16[1,3,256,512]{3,2,1,0:T(8,128)(2,1)} async-done(((bf16[8,3,256,512]{3,2,1,0:T(8,128)(2,1)}), bf16[1,3,256,512]{3,2,1,0:T(8,128)(2,1)}) %reduce-scatter.11.cloned.1.call-update) | async-done | bytes 786448 | tf_op jit(solution)/shard_map/reduce_scatter | solution.py:1376
  951.5 2.5 convert_bitcast_fusion.1
  (112 shorter events, 49.3 us)
Async XLA Ops:
  7.2 3.5 copy-start.29
  7.2 3.7 copy-start.26
  7.2 102.7 %all-gather.9.cloned.1.call-start = ((), (), s32[]{:S(2)}) async-start(), calls=%async_computation.8 | async-start | bytes 9437184 | tf_op jit(solution)/shard_map/all_gather | solution.py:1341
  10.6 305.8 %all-gather.11.cloned.1.call-start = ((), (), s32[]{:S(2)}) async-start(), calls=%async_computation.9 | async-start | bytes 14155776 | tf_op jit(solution)/shard_map/all_gather | solution.py:1341
  13.9 9.1 copy-start.20
  23.0 3.4 copy-start.5
  25.5 87.0 %copy-start.3 = (f32[4096,128]{1,0:T(8,128)}, f32[4096,128]{1,0:T(8,128)S(1)}, u32[]{:S(2)}) copy-start(f32[4096,128]{1,0:T(8,128)S(1)} %get-tuple-element.67.cos_ref) | copy-start | bytes 6291460
  112.5 318.0 %all-gather.13.cloned.1.call-start = ((), (), s32[]{:S(2)}) async-start(), calls=%async_computation.10 | async-start | bytes 10616832 | tf_op jit(solution)/shard_map/all_gather | solution.py:1341
  124.9 3.2 copy-start.9
  128.2 12.9 %copy-start.1 = (bf16[8,1,256,512]{3,2,1,0:T(8,128)(2,1)}, bf16[8,1,256,512]{3,2,1,0:T(8,128)(2,1)S(1)}, u32[]{:S(2)}) copy-start(bf16[8,1,256,512]{3,2,1,0:T(8,128)(2,1)S(1)} %slice.31) | copy-start | bytes 6291460
  141.2 175.2 %slice-start = ((bf16[8,3,256,256]{2,3,0,1:T(8,128)(2,1)}), bf16[3,3,256,256]{2,3,0,1:T(8,128)(2,1)S(1)}, s32[]{:S(2)}) async-start(bf16[8,3,256,256]{2,3,0,1:T(8,128)(2,1)} %copy-done.20), calls=%async_computation.12 | async-start | bytes 2359296 | tf_op jit(solution)/shard_map/slice | solution.py:1370
  310.4 3.3 copy-start.16
  317.9 172.1 %all-gather.15.cloned.1.call-start = ((), (), s32[]{:S(2)}) async-start(), calls=%async_computation.11 | async-start | bytes 3538944 | tf_op jit(solution)/shard_map/all_gather | solution.py:1341
  379.0 51.5 %slice-start.1 = ((bf16[8,3,256,256]{2,3,0,1:T(8,128)(2,1)}), bf16[1,3,256,256]{2,3,0,1:T(8,128)(2,1)S(1)}, s32[]{:S(2)}) async-start(bf16[8,3,256,256]{2,3,0,1:T(8,128)(2,1)} %copy-done.20), calls=%async_computation.13 | async-start | bytes 786432 | tf_op jit(solution)/shard_map/slice | solution.py:1380
  431.5 196.3 %reduce-scatter.5.cloned.1.call-start = ((), (), s32[]{:S(2)}) async-start(), calls=%async_computation.4 | async-start | bytes 14155776 | tf_op jit(solution)/shard_map/reduce_scatter | solution.py:1376
  490.1 322.8 %reduce-scatter.7.cloned.1.call-start = ((), (), s32[]{:S(2)}) async-start(), calls=%async_computation.5 | async-start | bytes 10616832 | tf_op jit(solution)/shard_map/reduce_scatter | solution.py:1376
  627.8 253.1 %reduce-scatter.9.cloned.1.call-start = ((), (), s32[]{:S(2)}) async-start(), calls=%async_computation.6 | async-start | bytes 5898240 | tf_op jit(solution)/shard_map/reduce_scatter | solution.py:1376
  627.9 5.5 copy-start.4
  627.9 5.4 copy-start.13
  634.8 165.6 %copy-start.10 = (bf16[2048,1024]{1,0:T(8,128)(2,1)S(1)}, bf16[2048,1024]{1,0:T(8,128)(2,1)}, u32[]{:S(2)}) copy-start(bf16[2048,1024]{1,0:T(8,128)(2,1)} %get-tuple-element.109.unit_t_ref) | copy-start | bytes 12582916
  812.9 138.6 %reduce-scatter.11.cloned.1.call-start = ((), (), s32[]{:S(2)}) async-start(), calls=%async_computation.7 | async-start | bytes 7077888 | tf_op jit(solution)/shard_map/reduce_scatter | solution.py:1376
  884.5 3.0 copy-start.28
  884.5 3.0 copy-start.24
  901.3 52.7 %copy-start.23 = (f32[1024,512]{1,0:T(8,128)S(1)}, f32[1024,512]{1,0:T(8,128)}, u32[]{:S(2)}) copy-start(f32[1024,512]{1,0:T(8,128)} %leave.1) | copy-start | bytes 6291460
  (16 other events, 25.3 us)
Sparse Core Ops, SparseCore 0:
  10.8 84.7 all-gather.8
  112.6 203.5 all-gather.10
  318.5 110.4 all-gather.12
  431.6 58.3 all-gather.14
  492.2 135.5 reduce-scatter.4
  630.0 178.0 reduce-scatter.6
  813.0 67.9 reduce-scatter.8
  883.3 68.1 reduce-scatter.10

commit v3 on v2

--- a/solution.py
+++ b/solution.py
@@ -644,8 +644,7 @@
         inverse_ref[here, :] = jnp.broadcast_to(inverse, (128, 128))
         return carry
 
-    for t in range(rows // 128):
-        norm(t, 0)
+    lax.fori_loop(0, rows // 128, norm, 0)
     second.forward()
     second.receive()
     first.finish()
@@ -869,6 +868,14 @@
     )(unit_t, d_raw)
 
 
+def each_rows(start, size, step, visit):
+    def body(t, carry):
+        visit(pl.ds(pl.multiple_of(start + t * step, step), step))
+        return carry
+
+    lax.fori_loop(0, size // step, body, 0)
+
+
 def stats_of(values, unit):
     rows = values.shape[0]
     lane = lax.broadcasted_iota(jnp.int32, (rows, 128), 1)
@@ -916,12 +923,14 @@
 
 def split_rows(sum_ref, unit_ref, pieces_ref, stats_ref, start, size):
     count, _, width = pieces_ref.shape
-    for t in range(start, start + size, 128):
-        here = pl.ds(t, 128)
+
+    def part(here):
         values = sum_ref[here, :]
         stats_ref[:, here] = stats_of(values, unit_ref[here, :].astype(jnp.float32))
         for c in range(count):
             pieces_ref[c, here, :] = values[:, c * width : (c + 1) * width].astype(jnp.bfloat16)
+
+    each_rows(start, size, 128, part)
 
 
 def normed_grad(sum_ref, slots, stats_ref, stat_slots, own_ref, inverse_ref, here, width, col):
@@ -972,11 +981,13 @@
         moves[p].start()
     for p in range(parts):
         moves[p].receive()
-        for t in range(p * span, (p + 1) * span, 128):
-            here = pl.ds(t, 128)
+
+        def last_part(here):
             out_ref[here, :] = d_middle_ref[here, :] + normed_grad(
                 sum_ref, slots_ref, stats_ref, stat_slots_ref, own_ref, inverse_ref, here, width, col
             )
+
+        each_rows(p * span, span, 128, last_part)
     for one in moves:
         one.finish()
 
@@ -1045,21 +1056,15 @@
         )
 
 
-def feed_rear(unit_t_ref, cot_t_ref, down_weight, grad_ref, out_ref, act):
-    owners, _, _, depth, cols = grad_ref.shape
-    if out_ref is not None:
-        rows = out_ref.shape[0]
-        step = min(256, rows)
-        for t in range(0, rows, step):
-            here = pl.ds(t, step)
-            out_ref[here, :] += matmul_nt(act[0, here, :], down_weight)
+def feed_rear(unit_t_ref, cot_t_ref, grad_ref, act):
+    owners, _, depth, cols = grad_ref.shape
     hidden, d_gate, d_up = act[0], act[1], act[2]
     for owner in range(owners):
         here = pl.ds(owner * depth, depth)
         unit_t = unit_t_ref[here, :]
-        grad_ref[owner, 0, 0] = matmul(unit_t, d_gate).astype(jnp.bfloat16)
-        grad_ref[owner, 0, 1] = matmul(unit_t, d_up).astype(jnp.bfloat16)
-        grad_ref[owner, 0, 2] = matmul(cot_t_ref[here, :], hidden).astype(jnp.bfloat16)
+        grad_ref[owner, 0] = matmul(unit_t, d_gate).astype(jnp.bfloat16)
+        grad_ref[owner, 1] = matmul(unit_t, d_up).astype(jnp.bfloat16)
+        grad_ref[owner, 2] = matmul(cot_t_ref[here, :], hidden).astype(jnp.bfloat16)
 
 
 def feed_all_kernel(
@@ -1096,11 +1101,20 @@
         copies[0].start()
 
     down_weight = weight_ref[:, 0, 2].reshape(unit_ref.shape[1], weight_ref.shape[4])
-    feed_rear(unit_t_ref, cot_t_ref, down_weight, grad_ref, out_ref, act_ref)
+    rows = unit_ref.shape[0]
+    step = min(256, rows)
+    for t in range(0, rows, step):
+        here = pl.ds(t, step)
+        out_ref[here, :] += matmul_nt(act_ref[0, here, :], down_weight)
 
     @pl.when(final)
     def _():
         copies[1].start()
+
+    feed_rear(unit_t_ref, cot_t_ref, grad_ref, act_ref)
+
+    @pl.when(final)
+    def _():
         for copy in copies:
             copy.wait()
 
@@ -1113,20 +1127,20 @@
     )
 
 
-def feed_all(unit, unit_t, cot, cot_t, weights, old):
+def feed_all(unit, unit_t, cot, cot_t, weights, tiles, old, blocks):
     rows, width = unit.shape
-    owners, tiles, _, depth, cols = weights.shape
-    block = pl.BlockSpec((owners, 1, 3, depth, cols), lambda i: (0, i, 0, 0, 0))
+    owners, _, _, depth, cols = weights.shape
     hbm = pl.BlockSpec(memory_space=pl.ANY)
     return pl.pallas_call(
         feed_all_kernel,
         grid=(tiles,),
         in_specs=[
             resident((rows, width)), resident((width, rows)), resident(cot.shape),
-            resident((width, rows)), block,
+            resident((width, rows)),
+            pl.BlockSpec((owners, 1, 3, depth, cols), lambda i: (0, i, 0, 0, 0)),
         ] + [hbm] * len(old),
-        out_specs=[block, hbm, hbm],
-        out_shape=[jax.ShapeDtypeStruct(weights.shape, jnp.bfloat16)]
+        out_specs=[pl.BlockSpec((owners, 3, depth, cols), lambda i: (0, i, 0, 0)), hbm, hbm],
+        out_shape=[jax.ShapeDtypeStruct((owners, blocks, depth, cols), jnp.bfloat16)]
         + [jax.ShapeDtypeStruct((rows, width), jnp.float32)] * 2,
         scratch_shapes=[
             pltpu.VMEM((rows, width), jnp.float32),
@@ -1142,17 +1156,19 @@
 
 def feed_last_kernel(
     unit_hbm, unit_t_hbm, cots_hbm, cot_t_hbm, weight_hbm, old_two_hbm, old_out_hbm, own_ref,
-    inverse_ref, out_t_ref, back_ref,
-    grad_ref, ffn_ref, d_middle_ref, d_sent_ref, out_grad_ref,
-    unit_ref, turned_ref, cots_ref, weight_ref, two_ref, sum_ref, act_ref, pieces_ref, slots_ref,
+    inverse_ref, out_t_ref, back_ref, _,
+    late_ref, ffn_ref, d_middle_ref, d_sent_ref,
+    grad_ref, out_grad_ref, unit_ref, turned_ref, cots_ref, weight_ref, two_ref, sum_ref, act_ref, pieces_ref, slots_ref,
     stats_ref, stat_slots_ref, d_pieces_ref,
     load, sends, recvs, g_sends, g_recvs,
 ):
     col = lax.axis_index("col")
     rows, width = unit_ref.shape
     count, _, piece = pieces_ref.shape
-    owners, tiles, _, depth, cols = weight_ref.shape
+    owners, _, _, depth, cols = weight_ref.shape
     heads, _, size = back_ref.shape
+    tile = weight_hbm.shape[1] - 1
+    extra = late_ref.shape[1] - 3 - heads * size // cols
 
     def fetch(i, source, target):
         copy = pltpu.make_async_copy(source, target, load.at[i])
@@ -1160,15 +1176,14 @@
         return copy
 
     loads = [
-        fetch(0, unit_hbm, unit_ref), fetch(1, weight_hbm, weight_ref), fetch(2, cots_hbm, cots_ref),
+        fetch(0, unit_hbm, unit_ref), fetch(1, weight_hbm.at[:, pl.ds(tile, 1)], weight_ref), fetch(2, cots_hbm, cots_ref),
         fetch(3, old_two_hbm, two_ref), fetch(4, unit_t_hbm, turned_ref.at[0]),
-        fetch(5, cot_t_hbm, turned_ref.at[1]), fetch(6, old_out_hbm.at[: rows // 2], sum_ref),
+        fetch(5, cot_t_hbm, turned_ref.at[1]), fetch(6, old_out_hbm.at[: rows // 4], sum_ref),
     ]
     greet_cols(count)
     for i in range(4):
         loads[i].wait()
-    for tile in range(tiles):
-        feed_front(unit_ref, cots_ref, weight_ref.at[:, tile : tile + 1], two_ref, act_ref.at[tile])
+    feed_front(unit_ref, cots_ref, weight_ref, two_ref, act_ref)
     parts = 2
     span = rows // parts
     moves, gathers = [], []
@@ -1187,34 +1202,32 @@
                 g_sends.at[p], g_recvs.at[p], None,
             )
         )
-    for p in range(2):
+    quarter = rows // 4
+    down_weight = weight_ref[:, 0, 2].reshape(width, cols)
+    for p in range(4):
+        here = pl.ds(p * quarter, quarter)
         loads[6 + p].wait()
-        for tile in range(tiles):
-            down_weight = weight_ref[:, tile, 2].reshape(width, cols)
-            sum_ref[...] += matmul_nt(act_ref[tile, 0, pl.ds(p * span, span), :], down_weight)
+        sum_ref[...] += matmul_nt(act_ref[0, here, :], down_weight)
         for c in range(count):
-            ffn_ref[c, pl.ds(p * span, span), :] = sum_ref[
-                :, c * piece : (c + 1) * piece
-            ].astype(jnp.bfloat16)
-        if p == 0:
-            loads.append(fetch(7, old_out_hbm.at[rows // 2 :], sum_ref))
+            ffn_ref[c, here, :] = sum_ref[:, c * piece : (c + 1) * piece].astype(jnp.bfloat16)
+        if p < 3:
+            loads.append(fetch(7 + p, old_out_hbm.at[pl.ds((p + 1) * quarter, quarter)], sum_ref))
     for i in range(4, 6):
         loads[i].wait()
-    for tile in range(tiles):
-        feed_rear(
-            turned_ref.at[0], turned_ref.at[1], None, grad_ref.at[:, tile : tile + 1], None,
-            act_ref.at[tile],
-        )
+    feed_rear(turned_ref.at[0], turned_ref.at[1], grad_ref, act_ref)
+    stores = [fetch(10, grad_ref, late_ref.at[:, pl.ds(extra, 3)])]
     own_cot = cots_ref.at[col]
     for p in range(parts):
         moves[p].receive()
-        for t in range(p * span, (p + 1) * span, 128):
-            here = pl.ds(t, 128)
+
+        def middle_part(here):
             d_middle = own_cot[here, :].astype(jnp.float32) + normed_grad(
                 two_ref, slots_ref, stats_ref, stat_slots_ref, own_ref, inverse_ref, here, width, col
             )
             d_middle_ref[here, :] = d_middle
             d_pieces_ref[col, here, :] = d_middle.astype(jnp.bfloat16)
+
+        each_rows(p * span, span, 128, middle_part)
         gathers[p].start()
     for p in range(parts):
         gathers[p].forward()
@@ -1232,17 +1245,21 @@
         at = (owner % per_piece) * depth
         d_branch = d_pieces_ref[owner // per_piece, :, at : at + depth]
         for h in range(heads):
-            out_grad_ref[owner, h * size : (h + 1) * size, :] = lax.dot_general(
+            at = (h * size) % cols
+            out_grad_ref[owner, h * size // cols, at : at + size, :] = lax.dot_general(
                 back_ref[h], d_branch, (((0,), (0,)), ((), ())), preferred_element_type=jnp.float32
             ).astype(jnp.bfloat16)
+    stores.append(fetch(11, out_grad_ref, late_ref.at[:, pl.ds(extra + 3, heads * size // cols)]))
+    for one in stores:
+        one.wait()
     for one in moves + gathers:
         one.finish()
 
 
-def feed_last(unit, unit_t, cots, cot_t, weights, old, own, inverse, out_t, back):
+def feed_last(unit, unit_t, cots, cot_t, weights, old, own, inverse, out_t, back, late):
     rows, width = unit.shape
     count, _, piece = cots.shape
-    owners, tiles, _, depth, cols = weights.shape
+    owners, _, _, depth, cols = weights.shape
     heads, _, size = back.shape
     hbm = pl.BlockSpec(memory_space=pl.ANY)
     vmem = pl.BlockSpec(memory_space=pltpu.VMEM)
@@ -1250,39 +1267,41 @@
     shape = jax.ShapeDtypeStruct
     return pl.pallas_call(
         feed_last_kernel,
-        in_specs=[hbm] * 7 + [vmem] * 4,
-        out_specs=[vmem] * 5,
+        in_specs=[hbm] * 7 + [vmem] * 4 + [hbm],
+        out_specs=[hbm] + [vmem] * 3,
+        input_output_aliases={11: 0},
         out_shape=[
-            shape(weights.shape, jnp.bfloat16),
+            shape(late.shape, jnp.bfloat16),
             shape((count, rows, piece), jnp.bfloat16),
             shape((rows, piece), jnp.float32),
             shape((heads, rows, size), jnp.bfloat16),
-            shape((owners, heads * size, depth), jnp.bfloat16),
         ],
         scratch_shapes=[
+            pltpu.VMEM((owners, 3, depth, cols), jnp.bfloat16),
+            pltpu.VMEM((owners, heads * size // cols, cols, depth), jnp.bfloat16),
             pltpu.VMEM((rows, width), jnp.bfloat16),
             pltpu.VMEM((2, width, rows), jnp.bfloat16),
             pltpu.VMEM((count, rows, piece), jnp.bfloat16),
-            pltpu.VMEM(weights.shape, jnp.bfloat16),
+            pltpu.VMEM((owners, 1, 3, depth, cols), jnp.bfloat16),
             pltpu.VMEM((rows, width), jnp.float32),
-            pltpu.VMEM((rows // 2, width), jnp.float32),
-            pltpu.VMEM((tiles, 3, rows, cols), jnp.bfloat16),
+            pltpu.VMEM((rows // 4, width), jnp.float32),
+            pltpu.VMEM((3, rows, cols), jnp.bfloat16),
             pltpu.VMEM((count, rows, piece), jnp.bfloat16),
             pltpu.VMEM((count - 1, rows, piece), jnp.bfloat16),
             pltpu.VMEM((8, rows), jnp.float32),
             pltpu.VMEM((count - 1, 8, rows), jnp.float32),
             pltpu.VMEM((count, rows, piece), jnp.bfloat16),
-            dma((8,)), dma((2, 2, count - 1)), dma((2, 2, count - 1)), dma((2, 6)), dma((2, 6)),
+            dma((12,)), dma((2, 2, count - 1)), dma((2, 2, count - 1)), dma((2, 6)), dma((2, 6)),
         ],
         compiler_params=pltpu.CompilerParams(
             vmem_limit_bytes=63 * 2**20 + 2**19, collective_id=6, has_side_effects=True
         ),
         cost_estimate=pl.CostEstimate(
-            flops=18 * rows * width * tiles * cols, bytes_accessed=100 * rows * width,
+            flops=18 * rows * width * cols, bytes_accessed=100 * rows * width,
             transcendentals=rows * cols,
         ),
         name="feed_last",
-    )(unit, unit_t, cots, cot_t, weights, *old, own, inverse, out_t, back)
+    )(unit, unit_t, cots, cot_t, weights, *old, own, inverse, out_t, back, late)
 
 
 def group_tables(lengths, group):
@@ -1347,27 +1366,25 @@
     weights, _ = gather(mixed)
     packed = jnp.stack([gate_weight, up_weight, down_weight.T]).reshape(3, depth, tiles, tile)
     packed = packed.transpose(2, 0, 1, 3)
-    last = max(1, tiles // 8)
-    first = tiles // 2
+    first = max(1, tiles * 5 // 8)
+    pieces, cots, normed_one, unit_one_t, unit_one, inverse_one = enter(
+        inputs, cotangent, col_count
+    )
+    normed_one, weights, lengths = tied(normed_one, weights, lengths)
+    feed_one, weights = gather(packed[:first], weights)
     start_rows, cosine, sine = lax.optimization_barrier(group_tables(lengths, group))
     own_cos = lax.dynamic_slice_in_dim(
         cosine.reshape(span, tok_rows, HEAD), place, 1, 0
     )[0]
     own_sin = lax.dynamic_slice_in_dim(sine.reshape(span, tok_rows, HEAD), place, 1, 0)[0]
 
-    early_inputs, own_cos = tied(inputs, own_cos)
-    pieces, cots, normed_one, unit_one_t, unit_one, inverse_one = enter(
-        early_inputs, cotangent, col_count
-    )
-    normed_one, weights = tied(normed_one, weights)
-    feed_one, weights = gather(packed[:first], weights)
     sent = project(normed_one, weights, own_cos, own_sin)
     out_rows_t = weights[:, 3].reshape(-1, part_width)
     back, held, attended_head, lse, out_t = attend(
         sent, start_rows, out_rows_t, groups_here, col_count
     )
     back, feed_one = tied(back, feed_one)
-    feed_two, feed_one = gather(packed[first:-last], feed_one)
+    feed_two, feed_one = gather(packed[first:], feed_one)
     normed_two, unit_t, middle, unit_two, inverse_two = branch(back, out_t, pieces)
     cot_t = cots.transpose(0, 2, 1).reshape(-1, tok_rows)
     rows_two = (normed_two, unit_t, cots, cot_t)
@@ -1375,42 +1392,34 @@
     def owned(part):
         return lax.psum_scatter(part, "row", scatter_dimension=0, tiled=True)[0]
 
-    grads_one, *sums = feed_all(*rows_two, feed_one, ())
-    sums[0], feed_two = tied(sums[0], feed_two)
-    feed_three, feed_two = gather(packed[-last:], feed_two)
-    grads_two, *sums = feed_all(*rows_two, feed_two, sums)
-    sums[0], grads_one, feed_three = tied(sums[0], grads_one, feed_three)
+    grads_one, *sums = feed_all(*rows_two, feed_one, first, (), 3 * first)
+    sums[0], grads_one, feed_two = tied(sums[0], grads_one, feed_two)
     grads_one = owned(grads_one)
-    grads_three, ffn_pieces, d_middle, d_sent, out_part = feed_last(
-        *rows_two, feed_three, sums, unit_two, inverse_two, out_rows_t, back
+    rest = tiles - first - 1
+    blocks = 3 * (rest + 1) + part_width // tile
+    late, *sums = feed_all(*rows_two, feed_two, rest, sums, blocks)
+    late, ffn_pieces, d_middle, d_sent = feed_last(
+        *rows_two, feed_two, sums, unit_two, inverse_two, out_rows_t, back, late
     )
     d_sent, grads_one = tied(d_sent, grads_one)
-    grads_two, grads_one = tied(grads_two, grads_one)
-    grads_two = owned(grads_two)
+    late, grads_one = tied(late, grads_one)
+    late = owned(late)
     d_raw, ffn_others = attend_back(
         d_sent, held, attended_head, lse, start_rows, cosine, sine, ffn_pieces, groups_here
     )
     projection_part = project_grad(unit_one_t, d_raw, weights.shape[0])
-    projection_part, grads_two = tied(projection_part, grads_two)
-    blocks = out_part.reshape(out_part.shape[0], -1, tile, depth)
-    late = jnp.concatenate(
-        [grads_three.reshape(out_part.shape[0], -1, depth, tile), blocks], axis=1
-    )
-    late, grads_two = tied(late, grads_two)
-    late = owned(late)
+    projection_part, late, d_raw = tied(projection_part, late, d_raw)
+    own_grads = owned(projection_part)
     input_grad = leave(
         d_raw, weights, normed_one, unit_one, inverse_one, d_middle, col_count
     )
-    projection_part, late, input_grad = tied(projection_part, late, input_grad)
-    own_grads = owned(projection_part)
     own_ffn = lax.dynamic_slice_in_dim(ffn_pieces, col_index, 1, 0)[0]
     output = middle + own_ffn.astype(jnp.float32) + jnp.sum(ffn_others.astype(jnp.float32), axis=0)
     output = output.astype(jnp.bfloat16)
     qkv_grad = own_grads.astype(jnp.float32).transpose(1, 0, 2)
-    grads_three = late[: 3 * last].reshape(last, 3, depth, tile)
-    out_grad = late[3 * last :].reshape(part_width, depth).astype(jnp.float32)
-    grads = jnp.concatenate([grads_one, grads_two, grads_three]).astype(jnp.float32)
-    grads = grads.transpose(1, 2, 0, 3).reshape(3, depth, hidden_here)
+    out_grad = late[3 * (rest + 1) :].reshape(part_width, depth).astype(jnp.float32)
+    grads = jnp.concatenate([grads_one, late[: 3 * (rest + 1)]]).astype(jnp.float32)
+    grads = grads.reshape(tiles, 3, depth, tile).transpose(1, 2, 0, 3).reshape(3, depth, hidden_here)
     return (output, input_grad, qkv_grad, out_grad, grads[0], grads[1], grads[2].T)
 
 

time: 969 us -> 920 us (0.949)
  waiting for transfers between devices: 91.8 us -> 39.6 us
  Pallas kernels: 758 us -> 776 us
  starting transfers between devices: 13.1 us -> 0.77 us
    reduce_scatter x4 -> x3, waiting for transfers between devices: 79.6 us -> 22.5 us  [owned(): return lax.psum_scatter(part, 'row', scatter_dimension=0, tiled=True)[0]]
    pallas_call x1, Pallas kernels: 168 us -> 182 us  [attend(): pl.pallas_call(functools.partial(attend_kernel, groups_here), in_specs=[h...]
    all_gather x4 -> x3, starting transfers between devices: 12.5 us -> 0.65 us  [gather(): return (lax.all_gather(shard, 'row'), after)]
    pallas_call x1, Pallas kernels: 166 us -> 175 us  [attend_back(): pl.pallas_call(functools.partial(attend_back_kernel, groups_here), in_spe...]
    unnamed x66 -> x64, local copies, waits for them, and re-layouts: 32.4 us -> 38.7 us
  transfers between devices with their start and end apart: 8 -> 6, of which waited for: 4 -> 4; matrix products, arithmetic and copies ran while one was open for 5% -> 4% of each run, Pallas kernels for 79% -> 85%
where the time goes in v3:
time: 920 us; the launch traced here: 912 us
  Pallas kernels  776 us (84%)
  local copies, waits for them, and re-layouts  59.5 us (6%)
  waiting for transfers between devices  39.6 us (4%)
  other arithmetic  21.2 us (2%)
  between operations  14.8 us (2%)
    pallas_call x1, Pallas kernels, attend(): pl.pallas_call(functools.partial(attend_kernel, groups_here), in_specs=[h...  182 us
    pallas_call x1, Pallas kernels, attend_back(): pl.pallas_call(functools.partial(attend_back_kernel, groups_here), in_spe...  175 us
    pallas_call x1, Pallas kernels, feed_last(): pl.pallas_call(feed_last_kernel, in_specs=[hbm] * 7 + [vmem] * 4 + [hbm],...  109 us
    pallas_call x2, Pallas kernels, feed_all(): pl.pallas_call(feed_all_kernel, grid=(tiles,), in_specs=[resident((rows,...  99.7 us
    pallas_call x1, Pallas kernels, enter(): pl.pallas_call(enter_kernel, in_specs=[hbm, hbm], out_specs=[hbm, hbm, vm...  75.9 us
    pallas_call x1, Pallas kernels, leave(): pl.pallas_call(leave_kernel, in_specs=[vmem, hbm] + [vmem] * 4, out_specs...  58.2 us
    pallas_call x1, Pallas kernels, branch(): pl.pallas_call(branch_kernel, in_specs=[hbm, vmem, vmem], out_specs=[vmem...  55.7 us
    unnamed x64, local copies, waits for them, and re-layouts  38.7 us
  transfers between devices with their start and end apart: 6, of which 4 were waited for; matrix products, arithmetic and copies ran while one was open for 4% of the time, Pallas kernels for 85%

profile of v3, /device:TPU:0, one launch (start us, length us, event | category | flops | bytes accessed | tf_op | source)
XLA Modules:
  0.0 911.8 jit_solution(14379679655793502450)
XLA Ops:
  18.6 75.9 %enter.1 = (bf16[4,1024,512]{2,1,0:T(8,128)(2,1)S(1)}, bf16[4,1024,512]{2,1,0:T(8,128)(2,1)S(1)}, bf16[1024,2048]{1,0:T(8,128)(2,1)}, bf16[2048,1024]{1,0:T(8,12...) custom-call(bf16[1024,512]{1,0:T(8,128)(2,1)S(1)} %copy-done.6, bf16[1024,512]{1,0:T(8,128)(2,1)S(1)} %copy-done.7), custom_call_target="tpu_custom_call" | custom-call | flops 20971520 | bytes 209715200 | tf_op jit(solution)/shard_map/enter/pallas_call | solution.py:662
  100.6 4.0 copy.41
  107.3 7.5 multiply_sine_fusion
  118.6 12.1 %project.1.sent_ref = bf16[4,3,1024,128]{3,2,1,0:T(8,128)(2,1)S(1)} custom-call(bf16[1024,2048]{1,0:T(8,128)(2,1)S(1)} %copy-done.8, bf16[8,4,256,512]{3,2,1,0:T(8,128)(2,1)} %bitcast.86, f32[1024,128]{1,0:T(8,128)S(1)} %dynamic-slice_bitcast_fusion.1.cos_ref, f32[1024,128]{1,0:T(8,128)S(1)} %dynamic-slice_bitcast_fusion.sin_ref), custom_call_target="tpu_custom_call" | custom-call | flops 6442450944 | bytes 6291456 | tf_op jit(solution)/shard_map/project/pallas_call | solution.py:721
  130.7 182.4 %attend.1 = (bf16[4,1024,128]{2,1,0:T(8,128)(2,1)S(1)}, bf16[3,4096,128]{2,1,0:T(8,128)(2,1)S(1)}, bf16[4096,128]{1,0:T(8,128)(2,1)S(1)}, f32[8,1,512]{2,1,0:T(1,128)S(1)}, bf16[4,2048,512]{2,1,0:T(8,128)(2,1)S(1)}) custom-call(bf16[4,3,1024,128]{3,2,1,0:T(8,128)(2,1)S(1)} %project.1.sent_ref, s32[8,1,512]{2,1,0:T(1,128)S(1)} %compare_select_fusion.start_ref, ...), custom_call_target="tpu_custom_call" | custom-call | flops 4294967296 | bytes 104857600 | tf_op jit(solution)/shard_map/attend/pallas_call | solution.py:374
  314.1 3.3 copy-done.15
  320.1 17.0 %all-gather.9.cloned.1.call-done = bf16[40,3,256,256]{3,2,1,0:T(8,128)(2,1)} async-done(((bf16[5,3,256,256]{3,2,1,0:T(8,128)(2,1)}), bf16[40,3,256,256]{3,2,1,0:T(8,128)(2,1)}) %all-gather.9.cloned.1.call-update) | async-done | bytes 15728656 | tf_op jit(solution)/shard_map/all_gather | solution.py:1360
  338.7 6.5 copy.42
  345.1 55.7 %branch.1 = (bf16[1024,2048]{1,0:T(8,128)(2,1)}, bf16[2048,1024]{1,0:T(8,128)(2,1)}, f32[1024,512]{1,0:T(8,128)}, f32[1024,512]{1,0:T(8,128)}, f32[1024,128]{1,0:T(8,128)}) custom-call(bf16[4,1024,128]{2,1,0:T(8,128)(2,1)} %copy-done.5, bf16[4,2048,512]{2,1,0:T(8,128)(2,1)} %copy-done.15, bf16[4,1024,512]{2,1,0:T(8,128)(2,1)} %copy-done.10), custom_call_target="tpu_custom_call" | custom-call | flops 8589934592 | bytes 167772160 | tf_op jit(solution)/shard_map/branch/pallas_call | solution.py:810
  400.9 61.5 %feed_all.2 = (bf16[8,15,256,256]{3,2,1,0:T(8,128)(2,1)}, f32[1024,2048]{1,0:T(8,128)}, f32[1024,2048]{1,0:T(8,128)}) custom-call(bf16[1024,2048]{1,0:T(8,128)(2,1)} %get-tuple-element.71.unit_ref.unit_hbm, bf16[2048,1024]{1,0:T(8,128)(2,1)} %get-tuple-element.72.unit_t_ref.unit_t_hbm, bf16[4,1024,512]{2,1,0:T(8,128)(2,1)} %copy-done, ...), custom_call_target="tpu_custom_call" | custom-call | flops 48318382080 | bytes 31457280 | tf_op jit(solution)/shard_map/feed_all/pallas_call | solution.py:1134
  462.5 38.2 %feed_all.3 = (bf16[8,11,256,256]{3,2,1,0:T(8,128)(2,1)}, f32[1024,2048]{1,0:T(8,128)}, f32[1024,2048]{1,0:T(8,128)}) custom-call(bf16[1024,2048]{1,0:T(8,128)(2,1)} %get-tuple-element.71.unit_ref.unit_hbm, bf16[2048,1024]{1,0:T(8,128)(2,1)} %get-tuple-element.72.unit_t_ref.unit_t_hbm, bf16[4,1024,512]{2,1,0:T(8,128)(2,1)} %copy-done, ...), custom_call_target="tpu_custom_call" | custom-call | flops 19327352832 | bytes 12582912 | tf_op jit(solution)/shard_map/feed_all/pallas_call | solution.py:1134
  500.7 108.9 %feed_last.1 = (bf16[8,11,256,256]{3,2,1,0:T(8,128)(2,1)}, bf16[4,1024,512]{2,1,0:T(8,128)(2,1)}, f32[1024,512]{1,0:T(8,128)}, bf16[4,1024,128]{2,1,0:T(8,128)(2,1)}) custom-call(bf16[1024,2048]{1,0:T(8,128)(2,1)} %get-tuple-element.71.unit_ref.unit_hbm, ...), custom_call_target="tpu_custom_call", output_to_operand_aliasing={{0}: (11, {})} | custom-call | flops 9663676416 | bytes 209715200 | tf_op jit(solution)/shard_map/feed_last/pallas_call | solution.py:1268
  609.6 9.2 %reduce-scatter.4.cloned.1.call-done = bf16[1,15,256,256]{3,2,1,0:T(8,128)(2,1)} async-done(((bf16[8,15,256,256]{3,2,1,0:T(8,128)(2,1)}), bf16[1,15,256,256]{3,2,1,0:T(8,128)(2,1)}) %reduce-scatter.4.cloned.1.call-update) | async-done | bytes 1966096 | tf_op jit(solution)/shard_map/reduce_scatter | solution.py:1393
  622.8 175.3 %attend_back.1 = (bf16[4,3,1024,128]{3,2,1,0:T(8,128)(2,1)}, bf16[3,1024,512]{2,1,0:T(8,128)(2,1)}) custom-call(bf16[4,1024,128]{2,1,0:T(8,128)(2,1)S(1)} %copy-done.12, bf16[3,4096,128]{2,1,0:T(8,128)(2,1)} %copy-done.16, bf16[4096,128]{1,0:T(8,128)(2,1)S(1)} %copy-done.18, f32[8,1,512]{2,1,0:T(1,128)S(1)} %get-tuple-element.93.lse_ref, ...), custom_call_target="tpu_custom_call" | custom-call | flops 10737418240 | bytes 104857600 | tf_op jit(solution)/shard_map/attend_back/pallas_call | solution.py:567
  800.1 7.8 project_grad.1
  808.0 2.6 copy-done.2
  810.6 6.0 reduce-scatter.6.cloned.1.call-done
  820.0 2.9 fusion.1
  823.1 58.2 %leave.1 = f32[1024,512]{1,0:T(8,128)} custom-call(bf16[4,3,1024,128]{3,2,1,0:T(8,128)(2,1)} %get-tuple-element.100.d_raw_ref, bf16[8,4,256,512]{3,2,1,0:T(8,128)(2,1)} %bitcast.87, bf16[1024,2048]{1,0:T(8,128)(2,1)} %get-tuple-element.58.unit_ref, f32[1024,512]{1,0:T(8,128)} %copy-done.11, f32[1024,128]{1,0:T(8,128)} %copy-done.13, ...), custom_call_target="tpu_custom_call" | custom-call | flops 6442450944 | bytes 209715200 | tf_op jit(solution)/shard_map/leave/pallas_call | solution.py:1003
  882.3 2.6 fusion.5
  885.0 2.9 copy.46
  887.8 3.2 copy.48
  893.5 7.3 reduce-scatter.8.cloned.1.call-done
  900.8 2.5 convert_bitcast_fusion.1
  (99 shorter events, 43.6 us)
Async XLA Ops:
  7.2 3.5 copy-start.26
  7.2 93.4 %all-gather.7.cloned.1.call-start = ((), (), s32[]{:S(2)}) async-start(), calls=%async_computation.6 | async-start | bytes 9437184 | tf_op jit(solution)/shard_map/all_gather | solution.py:1360
  10.6 326.4 %all-gather.9.cloned.1.call-start = ((), (), s32[]{:S(2)}) async-start(), calls=%async_computation.7 | async-start | bytes 17694720 | tf_op jit(solution)/shard_map/all_gather | solution.py:1360
  15.5 89.6 %copy-start.19 = (bf16[8,3,256,256]{2,3,0,1:T(8,128)(2,1)}, bf16[8,3,256,256]{2,3,0,1:T(8,128)(2,1)S(1)}, u32[]{:S(2)}) copy-start(bf16[8,3,256,256]{2,3,0,1:T(8,128)(2,1)S(1)} %maximum_bitcast_fusion) | copy-start | bytes 9437188
  15.5 2.0 copy-start.6
  15.5 3.1 copy-start.7
  94.5 1.9 copy-start
  96.4 2.0 copy-start.10
  104.5 357.9 %all-gather.11.cloned.1.call-start = ((), (), s32[]{:S(2)}) async-start(), calls=%async_computation.8 | async-start | bytes 10616832 | tf_op jit(solution)/shard_map/all_gather | solution.py:1360
  107.1 23.6 %copy-start.1 = (bf16[8,1,256,512]{3,2,1,0:T(8,128)(2,1)}, bf16[8,1,256,512]{3,2,1,0:T(8,128)(2,1)S(1)}, u32[]{:S(2)}) copy-start(bf16[8,1,256,512]{3,2,1,0:T(8,128)(2,1)S(1)} %slice.28) | copy-start | bytes 6291460
  114.8 3.8 copy-start.8
  130.7 206.3 %slice-start = ((bf16[8,3,256,256]{2,3,0,1:T(8,128)(2,1)}), bf16[3,3,256,256]{2,3,0,1:T(8,128)(2,1)S(1)}, s32[]{:S(2)}) async-start(bf16[8,3,256,256]{2,3,0,1:T(8,128)(2,1)} %copy-done.19), calls=%async_computation.9 | async-start | bytes 2359296 | tf_op jit(solution)/shard_map/slice | solution.py:1387
  314.1 3.3 copy-start.15
  317.4 1.7 copy-start.16
  338.6 280.2 %reduce-scatter.4.cloned.1.call-start = ((), (), s32[]{:S(2)}) async-start(), calls=%async_computation.3 | async-start | bytes 17694720 | tf_op jit(solution)/shard_map/reduce_scatter | solution.py:1393
  462.4 354.1 %reduce-scatter.6.cloned.1.call-start = ((), (), s32[]{:S(2)}) async-start(), calls=%async_computation.4 | async-start | bytes 12976128 | tf_op jit(solution)/shard_map/reduce_scatter | solution.py:1393
  618.8 282.0 %reduce-scatter.8.cloned.1.call-start = ((), (), s32[]{:S(2)}) async-start(), calls=%async_computation.5 | async-start | bytes 7077888 | tf_op jit(solution)/shard_map/reduce_scatter | solution.py:1393
  622.8 175.3 %copy-start.9 = (bf16[2048,1024]{1,0:T(8,128)(2,1)S(1)}, bf16[2048,1024]{1,0:T(8,128)(2,1)}, u32[]{:S(2)}) copy-start(bf16[2048,1024]{1,0:T(8,128)(2,1)} %get-tuple-element.95.unit_t_ref) | copy-start | bytes 12582916
  798.1 2.0 copy-start.14
  808.0 2.6 copy-start.2
  816.5 1.9 copy-start.21
  820.0 2.9 copy-start.25
  823.1 58.2 %copy-start.24 = (bf16[1,15,256,256]{3,2,1,0:T(8,128)(2,1)S(1)}, bf16[1,15,256,256]{3,2,1,0:T(8,128)(2,1)}, u32[]{:S(2)}) copy-start(bf16[1,15,256,256]{3,2,1,0:T(8,128)(2,1)} %reduce-scatter.4.cloned.1.call-done) | copy-start | bytes 5898244
  892.7 10.7 %copy-start.23 = (f32[1024,512]{1,0:T(8,128)S(1)}, f32[1024,512]{1,0:T(8,128)}, u32[]{:S(2)}) copy-start(f32[1024,512]{1,0:T(8,128)} %leave.1) | copy-start | bytes 6291460
  (12 other events, 14.4 us)
Sparse Core Ops, SparseCore 0:
  10.7 84.7 all-gather.6
  104.7 232.3 all-gather.8
  339.3 88.8 all-gather.10
  462.6 156.1 reduce-scatter.3
  620.9 195.5 reduce-scatter.5
  818.7 82.0 reduce-scatter.7

commit v4 on v3

--- a/solution.py
+++ b/solution.py
@@ -208,7 +208,7 @@
     return ref.at[pl.ds(start, half)], ref.at[pl.ds(start + half, half)]
 
 
-def greet_all(me, span, groups_here, count):
+def greet_all(me, span, groups_here, count, others=0):
     barrier = pltpu.get_barrier_semaphore()
     for by in range(1, span):
         pl.semaphore_signal(
@@ -216,7 +216,7 @@
         )
     for by in range(1, count):
         pl.semaphore_signal(barrier, inc=1, device_id=col_device(by), device_id_type=MESH)
-    pl.semaphore_wait(barrier, span + count - 2)
+    pl.semaphore_wait(barrier, span + count - 2 + others)
 
 
 def attend_kernel(
@@ -230,9 +230,10 @@
     per_place = tokens // BLOCK
     scale = HEAD**-0.5 * log2e
     greet_all(me, span, groups_here, riders_ref.shape[0])
-    depth = rider_ref.shape[0]
+    half = rider_ref.shape[0] // 2
     ride = Gather(
-        halves(rider_ref, 0, depth), lambda c: halves(riders_ref.at[c], 0, depth),
+        (rider_ref.at[:half, 3], rider_ref.at[half:, 3]),
+        lambda c: (riders_ref.at[c, :half], riders_ref.at[c, half:]),
         ride_send, ride_recv, ride_local,
     )
 
@@ -380,7 +381,7 @@
             jax.ShapeDtypeStruct((3, length, size), jnp.bfloat16),
             jax.ShapeDtypeStruct((length, size), jnp.bfloat16),
             jax.ShapeDtypeStruct((blocks, 1, BLOCK), jnp.float32),
-            jax.ShapeDtypeStruct((count, *rider.shape), jnp.bfloat16),
+            jax.ShapeDtypeStruct((count, rider.shape[0], *rider.shape[2:]), jnp.bfloat16),
         ],
         scratch_shapes=[
             pltpu.VMEM((3, length, size), jnp.bfloat16),
@@ -403,8 +404,8 @@
 
 def attend_back_kernel(
     groups_here, d_sent_ref, qkv_ref, o_ref, lse_ref, start_ref, cos_ref, sin_ref, rider_ref,
-    d_raw_ref, riders_ref, do_ref, stage_ref, dq_sum, dk_sum, dv_sum,
-    in_send, in_recv, q_send, q_recv, kv_send, kv_recv, own_sem, ride_send, ride_recv,
+    middle_ref, d_raw_ref, output_ref, riders_ref, own_ride_ref, do_ref, stage_ref, dq_sum, dk_sum, dv_sum,
+    in_send, in_recv, q_send, q_recv, kv_send, kv_recv, own_sem, ride_send, ride_recv, ride_own,
 ):
     span, tokens, _ = d_sent_ref.shape
     me = lax.axis_index("row") // groups_here
@@ -430,6 +431,8 @@
     for by in range(1, span):
         do_copy(by).start()
     ride.start()
+    own_ride = pltpu.make_async_copy(rider_ref.at[lax.axis_index("col")], own_ride_ref, ride_own)
+    own_ride.start()
     dk_sum[...] = jnp.zeros_like(dk_sum)
     dv_sum[...] = jnp.zeros_like(dv_sum)
 
@@ -525,6 +528,15 @@
 
     lax.fori_loop(0, blocks, one_block, 0)
     ride.receive()
+    own_ride.wait()
+
+    def add_up(here):
+        total = middle_ref[here, :] + own_ride_ref[here, :].astype(jnp.float32)
+        for by in range(riders_ref.shape[0]):
+            total = total + riders_ref[by, here, :].astype(jnp.float32)
+        output_ref[here, :] = total.astype(jnp.bfloat16)
+
+    each_rows(0, tokens, 128, add_up)
     ride.finish()
     for by in range(1, span):
         do_copy(by).wait_send()
@@ -556,7 +568,7 @@
                 ).wait_recv()
 
 
-def attend_back(d_sent, held, out, lse, start_rows, cosine, sine, rider, groups_here):
+def attend_back(d_sent, held, out, lse, start_rows, cosine, sine, rider, middle, groups_here):
     span, tokens, size = d_sent.shape
     blocks = start_rows.shape[0]
     length = span * tokens
@@ -566,13 +578,15 @@
     dma = pltpu.SemaphoreType.DMA
     return pl.pallas_call(
         functools.partial(attend_back_kernel, groups_here),
-        in_specs=[hbm] + [vmem] * 6 + [hbm],
-        out_specs=[hbm, hbm],
+        in_specs=[hbm] + [vmem] * 6 + [hbm, vmem],
+        out_specs=[hbm, vmem],
         out_shape=[
             jax.ShapeDtypeStruct((span, 3, tokens, size), jnp.bfloat16),
-            jax.ShapeDtypeStruct((rider.shape[0] - 1, *rider.shape[1:]), jnp.bfloat16),
+            jax.ShapeDtypeStruct(rider.shape[1:], jnp.bfloat16),
         ],
         scratch_shapes=[
+            pltpu.VMEM((rider.shape[0] - 1, *rider.shape[1:]), jnp.bfloat16),
+            pltpu.VMEM(rider.shape[1:], jnp.bfloat16),
             pltpu.VMEM((length, size), jnp.bfloat16),
             pltpu.VMEM((3, length, size), jnp.bfloat16),
             pltpu.VMEM((size, BLOCK), jnp.float32),
@@ -580,7 +594,7 @@
             pltpu.VMEM((length, size), jnp.float32),
             dma((span,)), dma((span,)), dma((blocks,)), dma((span, per_place)), dma((blocks,)),
             dma((span, per_place)), dma((2, per_place)), dma((1, rider.shape[0] - 1)),
-            dma((1, rider.shape[0] - 1)),
+            dma((1, rider.shape[0] - 1)), dma,
         ],
         compiler_params=pltpu.CompilerParams(
             vmem_limit_bytes=48 * 2**20, collective_id=2, has_side_effects=True
@@ -590,7 +604,7 @@
             transcendentals=length * length // 2,
         ),
         name="attend_back",
-    )(d_sent, held, out, lse, start_rows, cosine, sine, rider)
+    )(d_sent, held, out, lse, start_rows, cosine, sine, rider, middle)
 
 
 def matmul(a, b):
@@ -835,39 +849,6 @@
     )(back, weight, pieces)
 
 
-def project_grad_kernel(unit_t_ref, d_raw_ref, grad_ref, rows_ref):
-    owners, _, depth, _ = grad_ref.shape
-    for h in range(d_raw_ref.shape[0]):
-        rows_ref[:, h * HEAD : (h + 1) * HEAD] = d_raw_ref[h, 0]
-    for owner in range(owners):
-        grad_ref[owner, 0] = matmul(
-            unit_t_ref[owner * depth : (owner + 1) * depth, :], rows_ref[...]
-        ).astype(jnp.bfloat16)
-
-
-def project_grad(unit_t, d_raw, owners):
-    width, rows = unit_t.shape
-    heads, kinds = d_raw.shape[:2]
-    columns, depth = heads * HEAD, width // owners
-    return pl.pallas_call(
-        project_grad_kernel,
-        grid=(kinds,),
-        in_specs=[
-            resident((width, rows)),
-            pl.BlockSpec((heads, 1, rows, HEAD), lambda k: (0, k, 0, 0)),
-        ],
-        out_specs=pl.BlockSpec((owners, 1, depth, columns), lambda k: (0, k, 0, 0)),
-        out_shape=jax.ShapeDtypeStruct((owners, kinds, depth, columns), jnp.bfloat16),
-        scratch_shapes=[pltpu.VMEM((rows, columns), jnp.bfloat16)],
-        compiler_params=pltpu.CompilerParams(vmem_limit_bytes=40 * 2**20),
-        cost_estimate=pl.CostEstimate(
-            flops=2 * rows * width * kinds * columns, bytes_accessed=2 * width * kinds * columns,
-            transcendentals=0,
-        ),
-        name="project_grad",
-    )(unit_t, d_raw)
-
-
 def each_rows(start, size, step, visit):
     def body(t, carry):
         visit(pl.ds(pl.multiple_of(start + t * step, step), step))
@@ -921,6 +902,53 @@
             one.wait_send()
 
 
+class Fold:
+    def __init__(self, pieces, slots, stats, stat_slots, start, size, sends, recvs):
+        me = lax.axis_index("col")
+        half = size // 2
+        self.pieces, self.slots = pieces, slots
+        self.firsts, self.sums, self.seconds, self.stats = [], [], [], []
+
+        def copy(i, source, target, by):
+            return send(source, target, sends.at[i], recvs.at[i], col_device(by))
+
+        for i, (by, then) in enumerate(((1, 2), (2, 1))):
+            here = pl.ds(pl.multiple_of(start + i * half, half), half)
+            self.firsts.append(
+                [
+                    copy(3 * i, pieces.at[me ^ by, here], slots.at[0, here], by),
+                    copy(3 * i + 1, pieces.at[me ^ 3, here], slots.at[1, here], by),
+                ]
+            )
+            self.sums.append((me ^ then, here))
+            self.seconds.append(copy(3 * i + 2, pieces.at[me ^ then, here], slots.at[2, here], then))
+        rows = pl.ds(pl.multiple_of(start, size), size)
+        for by in (1, 2, 3):
+            self.stats.append(copy(5 + by, stats.at[:, rows], stat_slots.at[by - 1, :, rows], by))
+
+    def start(self):
+        for one in self.firsts[0] + self.firsts[1] + self.stats:
+            one.start()
+
+    def forward(self):
+        for first, (to, here), second in zip(self.firsts, self.sums, self.seconds):
+            for one in first:
+                one.wait_recv()
+            total = self.pieces[to, here, :].astype(jnp.float32) + self.slots[1, here, :].astype(
+                jnp.float32
+            )
+            self.pieces[to, here, :] = total.astype(jnp.bfloat16)
+            second.start()
+
+    def receive(self):
+        for one in self.seconds + self.stats:
+            one.wait_recv()
+
+    def finish(self):
+        for one in self.firsts[0] + self.firsts[1] + self.seconds + self.stats:
+            one.wait_send()
+
+
 def split_rows(sum_ref, unit_ref, pieces_ref, stats_ref, start, size):
     count, _, width = pieces_ref.shape
 
@@ -936,50 +964,168 @@
 def normed_grad(sum_ref, slots, stats_ref, stat_slots, own_ref, inverse_ref, here, width, col):
     piece = slots.shape[2]
     grad = sum_ref[here, pl.ds(pl.multiple_of(col * piece, piece), piece)]
+    grad = grad + slots[0, here, :].astype(jnp.float32) + slots[2, here, :].astype(jnp.float32)
     stats = stats_ref[:, here]
-    for by in range(slots.shape[0]):
-        grad = grad + slots[by, here, :].astype(jnp.float32)
+    for by in range(stat_slots.shape[0]):
         stats = stats + stat_slots[by, :, here]
     sums, cross = columns_of(stats)
     return normalize_back(grad, sums, cross, own_ref[here, :], inverse_ref[here, :1], float(width))
 
 
+class LineSum:
+    def __init__(self, grads, cross, slots, groups_here, sems):
+        self.grads, self.cross, self.slots, self.groups = grads, cross, slots, groups_here
+        self.core_send, self.core_recv, self.hop_send, self.hop_recv = sems
+        self.span = grads.shape[0] // groups_here
+        row = lax.axis_index("row")
+        self.me, self.group = row // groups_here, lax.rem(row, groups_here)
+        self.partner = (row + 1 - 2 * self.group, lax.axis_index("col"))
+
+    def owner(self, place, other):
+        group = 1 - self.group if other else self.group
+        return jnp.clip(place, 0, self.span - 1) * self.groups + group
+
+    def across(self, place):
+        return send(
+            self.grads.at[self.owner(place, True)], self.cross.at[place], self.core_send.at[place],
+            self.core_recv.at[place], self.partner,
+        )
+
+    def join(self, place):
+        self.across(place).wait_recv()
+        owner = self.owner(place, False)
+        for k in range(self.grads.shape[1]):
+            total = self.grads[owner, k].astype(jnp.float32) + self.cross[place, k].astype(jnp.float32)
+            self.grads[owner, k] = total.astype(jnp.bfloat16)
+
+    def hop(self, way, r):
+        i = (1 - way) // 2
+        to = self.me + way * (self.span - r)
+        behind = self.me if way > 0 else self.span - 1 - self.me
+        copy = send(
+            self.grads.at[self.owner(to, False)], self.slots.at[i, r - 1], self.hop_send.at[i, r - 1],
+            self.hop_recv.at[i, r - 1],
+            place_of(jnp.clip(self.me + way, 0, self.span - 1), self.groups),
+        )
+        return behind <= r - 1, (behind >= 1) & (behind <= r), to, copy
+
+    def start(self, r):
+        for way in (1, -1):
+            i = (1 - way) // 2
+            sends, _, to, copy = self.hop(way, r)
+            if r > 1:
+                _, came, _, before = self.hop(way, r - 1)
+
+                @pl.when(came)
+                def _():
+                    before.wait_recv()
+
+                @pl.when(came & sends)
+                def _():
+                    owner = self.owner(to, False)
+                    for k in range(self.grads.shape[1]):
+                        total = self.grads[owner, k].astype(jnp.float32) + self.slots[
+                            i, r - 2, k
+                        ].astype(jnp.float32)
+                        self.grads[owner, k] = total.astype(jnp.bfloat16)
+
+            @pl.when(sends)
+            def _():
+                copy.start()
+
+    def result(self, out_ref):
+        last = self.span - 1
+        own = self.owner(self.me, False)
+        for k in range(self.grads.shape[1]):
+            out_ref[k] = self.grads[own, k].astype(jnp.float32)
+        for way in (1, -1):
+            _, came, _, copy = self.hop(way, last)
+
+            @pl.when(came)
+            def _():
+                copy.wait_recv()
+                for k in range(self.grads.shape[1]):
+                    out_ref[k] += self.slots[(1 - way) // 2, last - 1, k].astype(jnp.float32)
+
+    def finish(self):
+        for place in range(self.span):
+            self.across(place).wait_send()
+        for r in range(1, self.span):
+            for way in (1, -1):
+                sends, _, _, copy = self.hop(way, r)
+
+                @pl.when(sends)
+                def _():
+                    copy.wait_send()
+
+
 def leave_kernel(
-    d_raw_ref, weight_ref, unit_ref, own_ref, inverse_ref, d_middle_ref, out_ref,
-    rows_ref, sum_ref, pieces_ref, slots_ref, stats_ref, stat_slots_ref, weights_ref,
-    sends, recvs, load,
+    groups_here, d_raw_ref, weight_ref, unit_t_ref, unit_ref, own_ref, inverse_ref, d_middle_ref,
+    out_ref, grad_ref,
+    rows_ref, sum_ref, pieces_ref, slots_ref, stats_ref, stat_slots_ref, weights_ref, turned_ref,
+    parts_ref, cross_ref, line_ref,
+    sends, recvs, load, *line_sems,
 ):
     col = lax.axis_index("col")
     rows, width = unit_ref.shape
     heads, kinds = d_raw_ref.shape[:2]
     columns = heads * HEAD
+    depth = parts_ref.shape[2]
+    turned = pltpu.make_async_copy(unit_t_ref, turned_ref, load.at[kinds])
+    turned.start()
     loads = [
         pltpu.make_async_copy(weight_ref.at[:, k], weights_ref.at[k], load.at[k]) for k in range(kinds)
     ]
     for one in loads:
         one.start()
-    greet_cols(pieces_ref.shape[0])
+    line = LineSum(parts_ref, cross_ref, line_ref, groups_here, line_sems)
+    span = line.span
+    barrier = pltpu.get_barrier_semaphore()
+    pl.semaphore_signal(barrier, inc=1, device_id=line.partner, device_id_type=MESH)
+    greet_all(line.me, span, groups_here, pieces_ref.shape[0], 1)
     for k in range(kinds):
         for h in range(heads):
             rows_ref[k, :, h * HEAD : (h + 1) * HEAD] = d_raw_ref[h, k]
+    turned.wait()
+
+    def part_of(owner):
+        here = pl.ds(pl.multiple_of(owner * depth, depth), depth)
+        for k in range(kinds):
+            parts_ref[owner, k] = matmul(turned_ref[here, :], rows_ref[k]).astype(jnp.bfloat16)
+
+    for place in range(span):
+        part_of(line.owner(place, True))
+        line.across(place).start()
+    for place in range(span):
+        part_of(line.owner(place, False))
+    for place in (span - 1, 0):
+        line.join(place)
+    line.start(1)
+    for place in range(1, span - 1):
+        line.join(place)
     for one in loads:
         one.wait()
-    parts = 2
-    span = rows // parts
+    count = sends.shape[0]
+    size = rows // count
     moves = []
-    for p in range(parts):
-        here = pl.ds(p * span, span)
+    for p in range(count):
+        here = pl.ds(p * size, size)
         sum_ref[here, :] = matmul_nt(rows_ref[0, here, :], weights_ref[0].reshape(width, columns))
         for k in range(1, kinds):
             sum_ref[here, :] += matmul_nt(
                 rows_ref[k, here, :], weights_ref[k].reshape(width, columns)
             )
-        split_rows(sum_ref, unit_ref, pieces_ref, stats_ref, p * span, span)
+        split_rows(sum_ref, unit_ref, pieces_ref, stats_ref, p * size, size)
         moves.append(
-            Scatter(pieces_ref, slots_ref, stats_ref, stat_slots_ref, here, sends.at[p], recvs.at[p])
+            Fold(pieces_ref, slots_ref, stats_ref, stat_slots_ref, p * size, size, sends.at[p], recvs.at[p])
         )
         moves[p].start()
-    for p in range(parts):
+        if p == 0:
+            line.start(2)
+    moves[0].forward()
+    moves[1].forward()
+    line.start(3)
+    for p in range(count):
         moves[p].receive()
 
         def last_part(here):
@@ -987,24 +1133,30 @@
                 sum_ref, slots_ref, stats_ref, stat_slots_ref, own_ref, inverse_ref, here, width, col
             )
 
-        each_rows(p * span, span, 128, last_part)
+        each_rows(p * size, size, 128, last_part)
+    line.result(grad_ref)
     for one in moves:
         one.finish()
-
-
-def leave(d_raw, weight, unit, own, inverse, d_middle, count):
+    line.finish()
+
+
+def leave(d_raw, weight, unit_t, unit, own, inverse, d_middle, groups_here, count):
     rows, width = unit.shape
     heads, kinds = d_raw.shape[:2]
     owners, _, depth, columns = weight.shape
+    span = owners // groups_here
     piece = width // count
     hbm = pl.BlockSpec(memory_space=pl.ANY)
     vmem = pl.BlockSpec(memory_space=pltpu.VMEM)
     dma = pltpu.SemaphoreType.DMA
     return pl.pallas_call(
-        leave_kernel,
-        in_specs=[vmem, hbm] + [vmem] * 4,
-        out_specs=vmem,
-        out_shape=jax.ShapeDtypeStruct((rows, piece), jnp.float32),
+        functools.partial(leave_kernel, groups_here),
+        in_specs=[vmem, hbm, hbm] + [vmem] * 4,
+        out_specs=[vmem, vmem],
+        out_shape=[
+            jax.ShapeDtypeStruct((rows, piece), jnp.float32),
+            jax.ShapeDtypeStruct((kinds, depth, columns), jnp.float32),
+        ],
         scratch_shapes=[
             pltpu.VMEM((kinds, rows, columns), jnp.bfloat16),
             pltpu.VMEM((rows, width), jnp.float32),
@@ -1013,19 +1165,24 @@
             pltpu.VMEM((8, rows), jnp.float32),
             pltpu.VMEM((count - 1, 8, rows), jnp.float32),
             pltpu.VMEM((kinds, owners, depth, columns), jnp.bfloat16),
-            dma((2, 2, count - 1)), dma((2, 2, count - 1)), dma((kinds,)),
+            pltpu.VMEM((width, rows), jnp.bfloat16),
+            pltpu.VMEM((owners, kinds, depth, columns), jnp.bfloat16),
+            pltpu.VMEM((span, kinds, depth, columns), jnp.bfloat16),
+            pltpu.VMEM((2, span - 1, kinds, depth, columns), jnp.bfloat16),
+            dma((2, 9)), dma((2, 9)), dma((kinds + 1,)),
+            dma((span,)), dma((span,)), dma((2, span - 1)), dma((2, span - 1)),
         ],
         compiler_params=pltpu.CompilerParams(
-            vmem_limit_bytes=60 * 2**20, collective_id=5, has_side_effects=True
+            vmem_limit_bytes=63 * 2**20, collective_id=5, has_side_effects=True
         ),
         cost_estimate=pl.CostEstimate(
-            flops=2 * rows * width * kinds * columns, bytes_accessed=100 * rows * width, transcendentals=0
+            flops=4 * rows * width * kinds * columns, bytes_accessed=100 * rows * width, transcendentals=0
         ),
         name="leave",
-    )(d_raw, weight, unit, own, inverse, d_middle)
-
-
-def feed_front(unit_ref, cot_ref, weight_ref, two_ref, act):
+    )(d_raw, weight, unit_t, unit, own, inverse, d_middle)
+
+
+def feed_front(unit_ref, cot_ref, weight_ref, two_ref, act, before=None):
     owners, _, _, depth, cols = weight_ref.shape
     rows, width = unit_ref.shape
     count, _, piece = cot_ref.shape
@@ -1049,6 +1206,8 @@
             d_hidden * up_proj * sigmoid_gate * (1.0 + gate * (1.0 - sigmoid_gate))
         ).astype(jnp.bfloat16)
         act[2, here, :] = (d_hidden * silu_gate).astype(jnp.bfloat16)
+    if before is not None:
+        before()
     for t in range(0, rows, step):
         here = pl.ds(t, step)
         two_ref[here, :] += matmul_nt(act[1, here, :], gate_weight) + matmul_nt(
@@ -1074,22 +1233,28 @@
     grad_ref, new_two_ref, new_out_ref, two_ref, out_ref, act_ref, sem = refs[-7:]
     tile = pl.program_id(0)
 
+    loads = []
+    if old:
+        loads = [
+            pltpu.make_async_copy(old[0], two_ref, sem.at[0]),
+            pltpu.make_async_copy(old[1], out_ref, sem.at[1]),
+        ]
+
     @pl.when(tile == 0)
     def _():
-        if old:
-            loads = [
-                pltpu.make_async_copy(old[0], two_ref, sem.at[0]),
-                pltpu.make_async_copy(old[1], out_ref, sem.at[1]),
-            ]
-            for load in loads:
-                load.start()
+        for load in loads:
+            load.start()
+        if not old:
+            two_ref[...] = jnp.zeros_like(two_ref)
+            out_ref[...] = jnp.zeros_like(out_ref)
+
+    def arrive():
+        @pl.when(tile == 0)
+        def _():
             for load in loads:
                 load.wait()
-        else:
-            two_ref[...] = jnp.zeros_like(two_ref)
-            out_ref[...] = jnp.zeros_like(out_ref)
-
-    feed_front(unit_ref, cot_ref, weight_ref, two_ref, act_ref)
+
+    feed_front(unit_ref, cot_ref, weight_ref, two_ref, act_ref, arrive if old else None)
     final = tile == pl.num_programs(0) - 1
     copies = [
         pltpu.make_async_copy(two_ref, new_two_ref, sem.at[0]),
@@ -1156,9 +1321,9 @@
 
 def feed_last_kernel(
     unit_hbm, unit_t_hbm, cots_hbm, cot_t_hbm, weight_hbm, old_two_hbm, old_out_hbm, own_ref,
-    inverse_ref, out_t_ref, back_ref, _,
+    inverse_ref, out_t_hbm, back_ref, _,
     late_ref, ffn_ref, d_middle_ref, d_sent_ref,
-    grad_ref, out_grad_ref, unit_ref, turned_ref, cots_ref, weight_ref, two_ref, sum_ref, act_ref, pieces_ref, slots_ref,
+    grad_ref, out_grad_ref, out_t_ref, unit_ref, turned_ref, cots_ref, weight_ref, two_ref, sum_ref, act_ref, pieces_ref, slots_ref,
     stats_ref, stat_slots_ref, d_pieces_ref,
     load, sends, recvs, g_sends, g_recvs,
 ):
@@ -1181,17 +1346,19 @@
         fetch(5, cot_t_hbm, turned_ref.at[1]), fetch(6, old_out_hbm.at[: rows // 4], sum_ref),
     ]
     greet_cols(count)
-    for i in range(4):
+    for i in range(3):
         loads[i].wait()
-    feed_front(unit_ref, cots_ref, weight_ref, two_ref, act_ref)
-    parts = 2
+    feed_front(unit_ref, cots_ref, weight_ref, two_ref, act_ref, loads[3].wait)
+    turned_out = pltpu.make_async_copy(out_t_hbm.at[:, 3], out_t_ref, load.at[12])
+    turned_out.start()
+    parts = sends.shape[0]
     span = rows // parts
     moves, gathers = [], []
     for p in range(parts):
         split_rows(two_ref, unit_ref, pieces_ref, stats_ref, p * span, span)
         moves.append(
-            Scatter(pieces_ref, slots_ref, stats_ref, stat_slots_ref, pl.ds(p * span, span),
-                    sends.at[p], recvs.at[p])
+            Fold(pieces_ref, slots_ref, stats_ref, stat_slots_ref, p * span, span,
+                 sends.at[p], recvs.at[p])
         )
         moves[p].start()
         own = d_pieces_ref.at[col]
@@ -1212,11 +1379,15 @@
             ffn_ref[c, here, :] = sum_ref[:, c * piece : (c + 1) * piece].astype(jnp.bfloat16)
         if p < 3:
             loads.append(fetch(7 + p, old_out_hbm.at[pl.ds((p + 1) * quarter, quarter)], sum_ref))
+    moves[0].forward()
+    moves[1].forward()
     for i in range(4, 6):
         loads[i].wait()
     feed_rear(turned_ref.at[0], turned_ref.at[1], grad_ref, act_ref)
     stores = [fetch(10, grad_ref, late_ref.at[:, pl.ds(extra, 3)])]
     own_cot = cots_ref.at[col]
+    for p in range(2, parts):
+        moves[p].forward()
     for p in range(parts):
         moves[p].receive()
 
@@ -1229,30 +1400,36 @@
 
         each_rows(p * span, span, 128, middle_part)
         gathers[p].start()
+        if p:
+            gathers[p - 1].forward()
+    gathers[parts - 1].forward()
+    for one in moves:
+        one.finish()
+    for h in range(heads):
+        pieces_ref[0, :, h * size : (h + 1) * size] = back_ref[h]
+    turned_out.wait()
+    out_t = out_t_ref[...].reshape(width, heads * size)
     for p in range(parts):
-        gathers[p].forward()
         gathers[p].receive()
         here = pl.ds(p * span, span)
-        d_attended = matmul(d_pieces_ref[0, here, :], out_t_ref[:piece, :])
-        for c in range(1, count):
-            d_attended += matmul(
-                d_pieces_ref[c, here, :], out_t_ref[c * piece : (c + 1) * piece, :]
-            )
+        d_attended = sum(
+            matmul(d_pieces_ref[c, here, :], out_t[c * piece : (c + 1) * piece]) for c in range(count)
+        )
         for h in range(heads):
             d_sent_ref[h, here, :] = d_attended[:, h * size : (h + 1) * size].astype(jnp.bfloat16)
     per_piece = piece // depth
     for owner in range(owners):
         at = (owner % per_piece) * depth
-        d_branch = d_pieces_ref[owner // per_piece, :, at : at + depth]
-        for h in range(heads):
-            at = (h * size) % cols
-            out_grad_ref[owner, h * size // cols, at : at + size, :] = lax.dot_general(
-                back_ref[h], d_branch, (((0,), (0,)), ((), ())), preferred_element_type=jnp.float32
-            ).astype(jnp.bfloat16)
+        turned = lax.dot_general(
+            d_pieces_ref[owner // per_piece, :, at : at + depth], pieces_ref[0],
+            (((0,), (0,)), ((), ())), preferred_element_type=jnp.float32,
+        ).astype(jnp.bfloat16)
+        for j in range(heads * size // cols):
+            out_grad_ref[owner, j] = turned[:, j * cols : (j + 1) * cols]
     stores.append(fetch(11, out_grad_ref, late_ref.at[:, pl.ds(extra + 3, heads * size // cols)]))
     for one in stores:
         one.wait()
-    for one in moves + gathers:
+    for one in gathers:
         one.finish()
 
 
@@ -1267,7 +1444,7 @@
     shape = jax.ShapeDtypeStruct
     return pl.pallas_call(
         feed_last_kernel,
-        in_specs=[hbm] * 7 + [vmem] * 4 + [hbm],
+        in_specs=[hbm] * 7 + [vmem] * 2 + [hbm, vmem, hbm],
         out_specs=[hbm] + [vmem] * 3,
         input_output_aliases={11: 0},
         out_shape=[
@@ -1278,7 +1455,8 @@
         ],
         scratch_shapes=[
             pltpu.VMEM((owners, 3, depth, cols), jnp.bfloat16),
-            pltpu.VMEM((owners, heads * size // cols, cols, depth), jnp.bfloat16),
+            pltpu.VMEM((owners, heads * size // cols, depth, cols), jnp.bfloat16),
+            pltpu.VMEM((owners, depth, heads * size), jnp.bfloat16),
             pltpu.VMEM((rows, width), jnp.bfloat16),
             pltpu.VMEM((2, width, rows), jnp.bfloat16),
             pltpu.VMEM((count, rows, piece), jnp.bfloat16),
@@ -1291,7 +1469,7 @@
             pltpu.VMEM((8, rows), jnp.float32),
             pltpu.VMEM((count - 1, 8, rows), jnp.float32),
             pltpu.VMEM((count, rows, piece), jnp.bfloat16),
-            dma((12,)), dma((2, 2, count - 1)), dma((2, 2, count - 1)), dma((2, 6)), dma((2, 6)),
+            dma((13,)), dma((4, 9)), dma((4, 9)), dma((4, 6)), dma((4, 6)),
         ],
         compiler_params=pltpu.CompilerParams(
             vmem_limit_bytes=63 * 2**20 + 2**19, collective_id=6, has_side_effects=True
@@ -1304,9 +1482,32 @@
     )(unit, unit_t, cots, cot_t, weights, *old, own, inverse, out_t, back, late)
 
 
-def group_tables(lengths, group):
+def unpack_kernel(blocks_ref, *refs):
+    outs = refs[-3:]
+    outs[0][...] = blocks_ref[0].astype(jnp.float32)
+    outs[1][...] = blocks_ref[1].astype(jnp.float32)
+    outs[2][...] = blocks_ref[2].astype(jnp.float32).T
+
+
+def unpack(blocks, skip, count, hidden, old):
+    _, depth, cols = blocks.shape
+    shapes = [(depth, hidden), (depth, hidden), (hidden, depth)]
+    wide = pl.BlockSpec((depth, cols), lambda i: (0, skip + i))
+    return pl.pallas_call(
+        unpack_kernel,
+        grid=(count,),
+        in_specs=[pl.BlockSpec((3, depth, cols), lambda i: (i, 0, 0))]
+        + [pl.BlockSpec(memory_space=pl.ANY)] * len(old),
+        out_specs=[wide, wide, pl.BlockSpec((cols, depth), lambda i: (skip + i, 0))],
+        out_shape=[jax.ShapeDtypeStruct(one, jnp.float32) for one in shapes],
+        input_output_aliases={1 + i: i for i in range(len(old))},
+        name="unpack",
+    )(blocks, *old)
+
+
+def group_rows(lengths, group, begin, count):
     row_lengths = lax.dynamic_slice_in_dim(lengths, group, 1, 0)[0]
-    local_index = jnp.arange(GROUP_LEN, dtype=jnp.int32)
+    local_index = begin + jnp.arange(count, dtype=jnp.int32)
     seg_ends = jnp.cumsum(row_lengths)
     seg_starts = seg_ends - row_lengths
     after_prompt = local_index - PROMPT
@@ -1324,7 +1525,7 @@
     angles = position.astype(jnp.float32)[:, None] * frequency[None, :]
     cosine, sine = jnp.cos(angles), jnp.sin(angles)
     return (
-        start_row.reshape(GROUP_LEN // BLOCK, 1, BLOCK),
+        start_row,
         jnp.concatenate([cosine, cosine], axis=1),
         jnp.concatenate([sine, -sine], axis=1),
     )
@@ -1366,61 +1567,55 @@
     weights, _ = gather(mixed)
     packed = jnp.stack([gate_weight, up_weight, down_weight.T]).reshape(3, depth, tiles, tile)
     packed = packed.transpose(2, 0, 1, 3)
-    first = max(1, tiles * 5 // 8)
+    first = max(1, tiles // 2)
+    early, later = lax.optimization_barrier((packed[:first], packed[first:]))
     pieces, cots, normed_one, unit_one_t, unit_one, inverse_one = enter(
         inputs, cotangent, col_count
     )
     normed_one, weights, lengths = tied(normed_one, weights, lengths)
-    feed_one, weights = gather(packed[:first], weights)
-    start_rows, cosine, sine = lax.optimization_barrier(group_tables(lengths, group))
-    own_cos = lax.dynamic_slice_in_dim(
-        cosine.reshape(span, tok_rows, HEAD), place, 1, 0
-    )[0]
-    own_sin = lax.dynamic_slice_in_dim(sine.reshape(span, tok_rows, HEAD), place, 1, 0)[0]
-
+    feed_one, weights = gather(early, weights)
+    _, own_cos, own_sin = group_rows(lengths, group, place * tok_rows, tok_rows)
+    start_rows = group_rows(lengths, group, 0, GROUP_LEN)[0].reshape(-1, 1, BLOCK)
     sent = project(normed_one, weights, own_cos, own_sin)
-    out_rows_t = weights[:, 3].reshape(-1, part_width)
     back, held, attended_head, lse, out_t = attend(
-        sent, start_rows, out_rows_t, groups_here, col_count
-    )
+        sent, start_rows, weights, groups_here, col_count
+    )
+    out_t = out_t.reshape(col_count, -1, part_width)
     back, feed_one = tied(back, feed_one)
-    feed_two, feed_one = gather(packed[first:], feed_one)
+    feed_two, feed_one = gather(later, feed_one)
+    cots, back = tied(cots, back)
+    cot_t = cots.transpose(0, 2, 1).reshape(-1, tok_rows)
     normed_two, unit_t, middle, unit_two, inverse_two = branch(back, out_t, pieces)
-    cot_t = cots.transpose(0, 2, 1).reshape(-1, tok_rows)
     rows_two = (normed_two, unit_t, cots, cot_t)
 
     def owned(part):
         return lax.psum_scatter(part, "row", scatter_dimension=0, tiled=True)[0]
 
     grads_one, *sums = feed_all(*rows_two, feed_one, first, (), 3 * first)
-    sums[0], grads_one, feed_two = tied(sums[0], grads_one, feed_two)
+    lengths, sums[0] = tied(lengths, sums[0])
+    _, cosine, sine = lax.optimization_barrier(group_rows(lengths, group, 0, GROUP_LEN))
+    sums[0], grads_one, feed_two, cosine = tied(sums[0], grads_one, feed_two, cosine)
     grads_one = owned(grads_one)
     rest = tiles - first - 1
     blocks = 3 * (rest + 1) + part_width // tile
     late, *sums = feed_all(*rows_two, feed_two, rest, sums, blocks)
     late, ffn_pieces, d_middle, d_sent = feed_last(
-        *rows_two, feed_two, sums, unit_two, inverse_two, out_rows_t, back, late
-    )
-    d_sent, grads_one = tied(d_sent, grads_one)
+        *rows_two, feed_two, sums, unit_two, inverse_two, weights, back, late
+    )
     late, grads_one = tied(late, grads_one)
     late = owned(late)
-    d_raw, ffn_others = attend_back(
-        d_sent, held, attended_head, lse, start_rows, cosine, sine, ffn_pieces, groups_here
-    )
-    projection_part = project_grad(unit_one_t, d_raw, weights.shape[0])
-    projection_part, late, d_raw = tied(projection_part, late, d_raw)
-    own_grads = owned(projection_part)
-    input_grad = leave(
-        d_raw, weights, normed_one, unit_one, inverse_one, d_middle, col_count
-    )
-    own_ffn = lax.dynamic_slice_in_dim(ffn_pieces, col_index, 1, 0)[0]
-    output = middle + own_ffn.astype(jnp.float32) + jnp.sum(ffn_others.astype(jnp.float32), axis=0)
-    output = output.astype(jnp.bfloat16)
-    qkv_grad = own_grads.astype(jnp.float32).transpose(1, 0, 2)
-    out_grad = late[3 * (rest + 1) :].reshape(part_width, depth).astype(jnp.float32)
-    grads = jnp.concatenate([grads_one, late[: 3 * (rest + 1)]]).astype(jnp.float32)
-    grads = grads.reshape(tiles, 3, depth, tile).transpose(1, 2, 0, 3).reshape(3, depth, hidden_here)
-    return (output, input_grad, qkv_grad, out_grad, grads[0], grads[1], grads[2].T)
+    grads = unpack(grads_one, 0, first, hidden_here, ())
+    d_sent, *grads = tied(d_sent, *grads)
+    d_raw, output = attend_back(
+        d_sent, held, attended_head, lse, start_rows, cosine, sine, ffn_pieces, middle, groups_here
+    )
+    input_grad, own_grads = leave(
+        d_raw, weights, unit_one_t, normed_one, unit_one, inverse_one, d_middle, groups_here, col_count
+    )
+    qkv_grad = own_grads.transpose(1, 0, 2)
+    grads = unpack(late, first, tiles - first, hidden_here, grads)
+    out_grad = late[3 * (rest + 1) :].transpose(0, 2, 1).reshape(part_width, depth).astype(jnp.float32)
+    return (output, input_grad, qkv_grad, out_grad, *grads)
 
 
 def body(
@@ -1700,7 +1895,7 @@
 def step(inputs, *rest):
     span = GROUP_LEN // inputs.shape[0]
     heads_here = inputs.shape[1] // HEAD
-    fast = heads_here == span and lax.axis_size("col") == 4
+    fast = heads_here == span and lax.axis_size("col") == 4 and lax.axis_size("row") == 2 * span
     return (fast_body if fast else body)(inputs, *rest)
 
 

time: 920 us -> 879 us (0.955)
  waiting for transfers between devices: 39.6 us -> 12.2 us
  local copies, waits for them, and re-layouts: 59.5 us -> 37 us
  Pallas kernels: 776 us -> 787 us
    reduce_scatter x3 -> x2, waiting for transfers between devices: 22.5 us -> 0.04 us  [owned(): return lax.psum_scatter(part, 'row', scatter_dimension=0, tiled=True)[0]]
    pallas_call x3 -> x4, Pallas kernels: 175 us -> 190 us  [the longest x1 92.5 us: feed_last(): pl.pallas_call(feed_last_kernel, in_specs=[hbm] * 7 + [vmem] * 2 + [hbm,...]
    unnamed x64 -> x48, local copies, waits for them, and re-layouts: 38.7 us -> 26.1 us
  transfers between devices with their start and end apart: 6 -> 5, of which waited for: 4 -> 2; matrix products, arithmetic and copies ran while one was open for 4% -> 3% of each run, Pallas kernels for 85% -> 90%
where the time goes in v4:
time: 879 us; the launch traced here: 870 us
  Pallas kernels  787 us (90%)
  local copies, waits for them, and re-layouts  37 us (4%)
  other arithmetic  19.2 us (2%)
  between operations  14.4 us (2%)
  waiting for transfers between devices  12.2 us (1%)
    pallas_call x1, Pallas kernels, attend_back(): pl.pallas_call(functools.partial(attend_back_kernel, groups_here), in_spe...  183 us
    pallas_call x1, Pallas kernels, attend(): pl.pallas_call(functools.partial(attend_kernel, groups_here), in_specs=[h...  176 us
    pallas_call x2, Pallas kernels, feed_all(): pl.pallas_call(feed_all_kernel, grid=(tiles,), in_specs=[resident((rows,...  95.7 us
    pallas_call x1, Pallas kernels, feed_last(): pl.pallas_call(feed_last_kernel, in_specs=[hbm] * 7 + [vmem] * 2 + [hbm,...  92.5 us
    pallas_call x1, Pallas kernels, leave(): pl.pallas_call(functools.partial(leave_kernel, groups_here), in_specs=[vm...  89.6 us
    pallas_call x1, Pallas kernels, enter(): pl.pallas_call(enter_kernel, in_specs=[hbm, hbm], out_specs=[hbm, hbm, vm...  76 us
    pallas_call x1, Pallas kernels, branch(): pl.pallas_call(branch_kernel, in_specs=[hbm, vmem, vmem], out_specs=[vmem...  54.9 us
    unnamed x48, local copies, waits for them, and re-layouts  26.1 us
  transfers between devices with their start and end apart: 5, of which 2 were waited for; matrix products, arithmetic and copies ran while one was open for 3% of the time, Pallas kernels for 90%

profile of v4, /device:TPU:0, one launch (start us, length us, event | category | flops | bytes accessed | tf_op | source)
XLA Modules:
  0.0 870.4 jit_solution(3980578508979813662)
XLA Ops:
  8.4 2.2 pad_maximum_fusion.2
  12.3 1.6 maximum_bitcast_fusion
  15.5 76.0 %enter.1 = (bf16[4,1024,512]{2,1,0:T(8,128)(2,1)S(1)}, bf16[4,1024,512]{2,1,0:T(8,128)(2,1)S(1)}, bf16[1024,2048]{1,0:T(8,128)(2,1)}, bf16[2048,1024]{1,0:T(8,12...) custom-call(bf16[1024,512]{1,0:T(8,128)(2,1)S(1)} %copy-done.3, bf16[1024,512]{1,0:T(8,128)(2,1)S(1)} %copy-done.4), custom_call_target="tpu_custom_call" | custom-call | flops 20971520 | bytes 209715200 | tf_op jit(solution)/shard_map/enter/pallas_call | solution.py:676
  91.5 2.0 copy-done
  93.5 2.0 copy-done.8
  99.7 1.9 multiply_sine_fusion.1
  102.0 12.1 %project.1.sent_ref = bf16[4,3,1024,128]{3,2,1,0:T(8,128)(2,1)S(1)} custom-call(bf16[1024,2048]{1,0:T(8,128)(2,1)S(1)} %copy-done.7, bf16[8,4,256,512]{3,2,1,0:T(8,128)(2,1)} %bitcast.54, f32[1024,128]{1,0:T(8,128)S(1)} %get-tuple-element.141.cos_ref, f32[1024,128]{1,0:T(8,128)S(1)} %get-tuple-element.142.sin_ref), custom_call_target="tpu_custom_call" | custom-call | flops 6442450944 | bytes 6291456 | tf_op jit(solution)/shard_map/project/pallas_call | solution.py:735
  114.1 175.8 %attend.1 = (bf16[4,1024,128]{2,1,0:T(8,128)(2,1)S(1)}, bf16[3,4096,128]{2,1,0:T(8,128)(2,1)S(1)}, bf16[4096,128]{1,0:T(8,128)(2,1)S(1)}, f32[8,1,512]{2,1,0:T(1,128)S(1)}, bf16[4,8,256,512]{3,2,1,0:T(8,128)(2,1)S(1)}) custom-call(bf16[4,3,1024,128]{3,2,1,0:T(8,128)(2,1)S(1)} %project.1.sent_ref, s32[8,1,512]{2,1,0:T(1,128)S(1)} %compare_select_fusion.start_ref, ...), custom_call_target="tpu_custom_call" | custom-call | flops 4294967296 | bytes 104857600 | tf_op jit(solution)/shard_map/attend/pallas_call | solution.py:375
  290.9 3.3 copy-done.12
  294.2 1.7 copy-done.13
  296.8 8.9 %all-gather.9.cloned.1.call-done = bf16[32,3,256,256]{3,2,1,0:T(8,128)(2,1)} async-done(((bf16[4,3,256,256]{3,2,1,0:T(8,128)(2,1)}), bf16[32,3,256,256]{3,2,1,0:T(8,128)(2,1)}) %all-gather.9.cloned.1.call-update) | async-done | bytes 12582928 | tf_op jit(solution)/shard_map/all_gather | solution.py:1561
  307.3 6.5 copy.44
  313.9 54.9 %branch.1 = (bf16[1024,2048]{1,0:T(8,128)(2,1)}, bf16[2048,1024]{1,0:T(8,128)(2,1)}, f32[1024,512]{1,0:T(8,128)}, f32[1024,512]{1,0:T(8,128)}, f32[1024,128]{1,0:T(8,128)}) custom-call(bf16[4,1024,128]{2,1,0:T(8,128)(2,1)} %copy-done.2, bf16[4,2048,512]{2,1,0:T(8,128)(2,1)} %bitcast.48, bf16[4,1024,512]{2,1,0:T(8,128)(2,1)} %copy-done.8), custom_call_target="tpu_custom_call" | custom-call | flops 8589934592 | bytes 167772160 | tf_op jit(solution)/shard_map/branch/pallas_call | solution.py:824
  368.8 51.5 %feed_all.2 = (bf16[8,12,256,256]{3,2,1,0:T(8,128)(2,1)}, f32[1024,2048]{1,0:T(8,128)}, f32[1024,2048]{1,0:T(8,128)}) custom-call(bf16[1024,2048]{1,0:T(8,128)(2,1)} %get-tuple-element.83.unit_ref.unit_hbm, bf16[2048,1024]{1,0:T(8,128)(2,1)} %get-tuple-element.84.unit_t_ref.unit_t_hbm, bf16[4,1024,512]{2,1,0:T(8,128)(2,1)} %copy-done, ...), custom_call_target="tpu_custom_call" | custom-call | flops 38654705664 | bytes 25165824 | tf_op jit(solution)/shard_map/feed_all/pallas_call | solution.py:1299
  420.6 7.7 multiply_sine_fusion
  428.3 1.9 pad_maximum_fusion.cos_ref
  430.2 1.9 pad_maximum_fusion.1.sin_ref
  432.1 3.2 all-gather.11.cloned.1.call-done
  435.4 44.3 %feed_all.3 = (bf16[8,14,256,256]{3,2,1,0:T(8,128)(2,1)}, f32[1024,2048]{1,0:T(8,128)}, f32[1024,2048]{1,0:T(8,128)}) custom-call(bf16[1024,2048]{1,0:T(8,128)(2,1)} %get-tuple-element.83.unit_ref.unit_hbm, bf16[2048,1024]{1,0:T(8,128)(2,1)} %get-tuple-element.84.unit_t_ref.unit_t_hbm, bf16[4,1024,512]{2,1,0:T(8,128)(2,1)} %copy-done, ...), custom_call_target="tpu_custom_call" | custom-call | flops 28991029248 | bytes 18874368 | tf_op jit(solution)/shard_map/feed_all/pallas_call | solution.py:1299
  479.6 92.5 %feed_last.1 = (bf16[8,14,256,256]{3,2,1,0:T(8,128)(2,1)}, bf16[4,1024,512]{2,1,0:T(8,128)(2,1)}, f32[1024,512]{1,0:T(8,128)}, bf16[4,1024,128]{2,1,0:T(8,128)(2,1)}) custom-call(bf16[1024,2048]{1,0:T(8,128)(2,1)} %get-tuple-element.83.unit_ref.unit_hbm, ...), custom_call_target="tpu_custom_call", output_to_operand_aliasing={{0}: (11, {})} | custom-call | flops 9663676416 | bytes 209715200 | tf_op jit(solution)/shard_map/feed_last/pallas_call | solution.py:1445
  572.2 4.0 unpack.2
  579.0 182.9 %attend_back.1 = (bf16[4,3,1024,128]{3,2,1,0:T(8,128)(2,1)}, bf16[1024,512]{1,0:T(8,128)(2,1)S(1)}) custom-call(bf16[4,1024,128]{2,1,0:T(8,128)(2,1)S(1)} %copy-done.10, bf16[3,4096,128]{2,1,0:T(8,128)(2,1)} %copy-done.13, bf16[4096,128]{1,0:T(8,128)(2,1)S(1)} %copy-done.15, f32[8,1,512]{2,1,0:T(1,128)S(1)} %get-tuple-element.113.lse_ref, ...), custom_call_target="tpu_custom_call" | custom-call | flops 10737418240 | bytes 104857600 | tf_op jit(solution)/shard_map/attend_back/pallas_call | solution.py:579
  762.9 89.6 %leave.1 = (f32[1024,512]{1,0:T(8,128)}, f32[3,256,512]{2,1,0:T(8,128)}) custom-call(bf16[4,3,1024,128]{3,2,1,0:T(8,128)(2,1)} %get-tuple-element.119.d_raw_ref, bf16[8,4,256,512]{3,2,1,0:T(8,128)(2,1)} %bitcast.57, bf16[2048,1024]{1,0:T(8,128)(2,1)} %get-tuple-element.120.unit_t_ref, bf16[1024,2048]{1,0:T(8,128)(2,1)} %get-tuple-element.72.unit_ref, ...), custom_call_target="tpu_custom_call" | custom-call | flops 12884901888 | bytes 209715200 | tf_op jit(solution)/shard_map/leave/pallas_call | solution.py:1152
  854.5 3.9 unpack.3
  (79 shorter events, 24.0 us)
Async XLA Ops:
  7.2 3.5 copy-start.18
  7.2 90.4 %all-gather.7.cloned.1.call-start = ((), (), s32[]{:S(2)}) async-start(), calls=%async_computation.4 | async-start | bytes 9437184 | tf_op jit(solution)/shard_map/all_gather | solution.py:1561
  10.6 1.2 copy-start.19
  10.6 295.1 %all-gather.9.cloned.1.call-start = ((), (), s32[]{:S(2)}) async-start(), calls=%async_computation.5 | async-start | bytes 14155776 | tf_op jit(solution)/shard_map/all_gather | solution.py:1561
  13.9 1.2 copy-start.3
  13.9 1.5 copy-start.4
  91.5 2.0 copy-start
  93.5 2.0 copy-start.8
  95.5 1.3 copy-start.9
  97.5 1.7 copy-start.20
  99.1 336.2 %all-gather.11.cloned.1.call-start = ((), (), s32[]{:S(2)}) async-start(), calls=%async_computation.6 | async-start | bytes 14155776 | tf_op jit(solution)/shard_map/all_gather | solution.py:1561
  99.7 2.3 copy-start.7
  289.9 1.0 copy-start.2
  290.9 3.3 copy-start.12
  294.2 1.7 copy-start.13
  307.3 264.9 %reduce-scatter.3.cloned.1.call-start = ((), (), s32[]{:S(2)}) async-start(), calls=%async_computation.2 | async-start | bytes 14155776 | tf_op jit(solution)/shard_map/reduce_scatter | solution.py:1592
  435.3 417.2 %reduce-scatter.5.cloned.1.call-start = ((), (), s32[]{:S(2)}) async-start(), calls=%async_computation.3 | async-start | bytes 16515072 | tf_op jit(solution)/shard_map/reduce_scatter | solution.py:1592
  572.1 4.0 copy-start.1
  576.2 1.4 copy-start.10
  577.6 1.4 copy-start.15
  761.9 1.0 copy-start.5
  854.5 3.9 copy-start.6
  858.4 2.0 copy-start.16
  860.4 2.2 copy-start.17
  (2 other events, 1.8 us)
Sparse Core Ops, SparseCore 0:
  10.7 84.7 all-gather.6
  99.3 206.3 all-gather.8
  307.9 127.3 all-gather.10
  437.5 132.9 reduce-scatter.2
  572.6 226.8 reduce-scatter.4

commit v5 on v4

--- a/solution.py
+++ b/solution.py
@@ -402,9 +402,18 @@
     )(sent, start_rows, rider)
 
 
+def back_tables(position):
+    lane = lax.broadcasted_iota(jnp.int32, (1, HEAD), 1)
+    half = HEAD // 2
+    frequency = jnp.exp(-math.log(rope_base) * (2.0 * (lane % half).astype(jnp.float32) / HEAD))
+    angles = jnp.broadcast_to(position, (HEAD, BLOCK)).T * frequency
+    sine = jnp.sin(angles)
+    return jnp.cos(angles), jnp.where(lane < half, sine, -sine)
+
+
 def attend_back_kernel(
-    groups_here, d_sent_ref, qkv_ref, o_ref, lse_ref, start_ref, cos_ref, sin_ref, rider_ref,
-    middle_ref, d_raw_ref, output_ref, riders_ref, own_ride_ref, do_ref, stage_ref, dq_sum, dk_sum, dv_sum,
+    groups_here, d_sent_ref, qkv_ref, o_ref, lse_ref, start_ref, place_ref, rider_ref,
+    middle_ref, d_raw_ref, output_ref, cos_ref, sin_ref, riders_ref, own_ride_ref, do_ref, stage_ref, dq_sum, dk_sum, dv_sum,
     in_send, in_recv, q_send, q_recv, kv_send, kv_recv, own_sem, ride_send, ride_recv, ride_own,
 ):
     span, tokens, _ = d_sent_ref.shape
@@ -487,6 +496,7 @@
 
         dq_sum[...] = jnp.zeros_like(dq_sum)
         here = block_rows(block)
+        cos_ref[here, :], sin_ref[here, :] = back_tables(place_ref[block])
         queries = qkv_ref[0, here, :]
         d_out = do_ref[here, :]
         lse = lse_ref[block]
@@ -568,7 +578,7 @@
                 ).wait_recv()
 
 
-def attend_back(d_sent, held, out, lse, start_rows, cosine, sine, rider, middle, groups_here):
+def attend_back(d_sent, held, out, lse, start_rows, positions, rider, middle, groups_here):
     span, tokens, size = d_sent.shape
     blocks = start_rows.shape[0]
     length = span * tokens
@@ -578,13 +588,15 @@
     dma = pltpu.SemaphoreType.DMA
     return pl.pallas_call(
         functools.partial(attend_back_kernel, groups_here),
-        in_specs=[hbm] + [vmem] * 6 + [hbm, vmem],
+        in_specs=[hbm] + [vmem] * 5 + [hbm, vmem],
         out_specs=[hbm, vmem],
         out_shape=[
             jax.ShapeDtypeStruct((span, 3, tokens, size), jnp.bfloat16),
             jax.ShapeDtypeStruct(rider.shape[1:], jnp.bfloat16),
         ],
         scratch_shapes=[
+            pltpu.VMEM((length, size), jnp.float32),
+            pltpu.VMEM((length, size), jnp.float32),
             pltpu.VMEM((rider.shape[0] - 1, *rider.shape[1:]), jnp.bfloat16),
             pltpu.VMEM(rider.shape[1:], jnp.bfloat16),
             pltpu.VMEM((length, size), jnp.bfloat16),
@@ -604,7 +616,7 @@
             transcendentals=length * length // 2,
         ),
         name="attend_back",
-    )(d_sent, held, out, lse, start_rows, cosine, sine, rider, middle)
+    )(d_sent, held, out, lse, start_rows, positions, rider, middle)
 
 
 def matmul(a, b):
@@ -787,9 +799,14 @@
             for h in range(heads):
                 at = (c * heads + h) * size
                 flat_ref[:, at : at + size] = heads_ref[c, h, pl.ds(p * span, span), :]
-        terms_ref[...] = matmul_nt(flat_ref[:, :piece], weight_ref[0])
-        for c in range(1, count):
-            terms_ref[...] += matmul_nt(flat_ref[:, c * piece : (c + 1) * piece], weight_ref[c])
+        terms_ref[...] = jnp.zeros_like(terms_ref)
+
+        def add_col(c, carry):
+            part = flat_ref[:, pl.ds(pl.multiple_of(c * piece, piece), piece)]
+            terms_ref[...] += matmul_nt(part, weight_ref[c])
+            return carry
+
+        lax.fori_loop(0, count, add_col, 0)
 
         def finish(t, carry):
             inner = pl.ds(pl.multiple_of(t * 128, 128), 128)
@@ -807,8 +824,7 @@
             unit_t_ref[:, here] = unit.T
             return carry
 
-        for t in range(span // 128):
-            finish(t, 0)
+        lax.fori_loop(0, span // 128, finish, 0)
     for one in gathers:
         one.finish()
 
@@ -1093,11 +1109,17 @@
         for k in range(kinds):
             parts_ref[owner, k] = matmul(turned_ref[here, :], rows_ref[k]).astype(jnp.bfloat16)
 
-    for place in range(span):
+    def for_partner(place, carry):
         part_of(line.owner(place, True))
         line.across(place).start()
-    for place in range(span):
+        return carry
+
+    def for_own(place, carry):
         part_of(line.owner(place, False))
+        return carry
+
+    lax.fori_loop(0, span, for_partner, 0)
+    lax.fori_loop(0, span, for_own, 0)
     for place in (span - 1, 0):
         line.join(place)
     line.start(1)
@@ -1482,27 +1504,42 @@
     )(unit, unit_t, cots, cot_t, weights, *old, own, inverse, out_t, back, late)
 
 
-def unpack_kernel(blocks_ref, *refs):
-    outs = refs[-3:]
+def unpack_kernel(with_out, blocks_ref, *refs):
+    outs = refs[-4:] if with_out else refs[-3:]
     outs[0][...] = blocks_ref[0].astype(jnp.float32)
     outs[1][...] = blocks_ref[1].astype(jnp.float32)
     outs[2][...] = blocks_ref[2].astype(jnp.float32).T
-
-
-def unpack(blocks, skip, count, hidden, old):
+    if with_out:
+
+        @pl.when(pl.program_id(0) == 0)
+        def _():
+            extra, cols = refs[0].shape[0], refs[0].shape[2]
+            for j in range(extra):
+                outs[3][j * cols : (j + 1) * cols, :] = refs[0][j].astype(jnp.float32).T
+
+
+def unpack(blocks, skip, count, hidden, old, extra=0):
     _, depth, cols = blocks.shape
     shapes = [(depth, hidden), (depth, hidden), (hidden, depth)]
     wide = pl.BlockSpec((depth, cols), lambda i: (0, skip + i))
+    in_specs = [pl.BlockSpec((3, depth, cols), lambda i: (i, 0, 0))]
+    out_specs = [wide, wide, pl.BlockSpec((cols, depth), lambda i: (skip + i, 0))]
+    given = [blocks]
+    if extra:
+        assert 3 * count % extra == 0
+        in_specs.append(pl.BlockSpec((extra, depth, cols), lambda i: (3 * count // extra, 0, 0)))
+        out_specs.append(pl.BlockSpec((extra * cols, depth), lambda i: (0, 0)))
+        shapes.append((extra * cols, depth))
+        given.append(blocks)
     return pl.pallas_call(
-        unpack_kernel,
+        functools.partial(unpack_kernel, bool(extra)),
         grid=(count,),
-        in_specs=[pl.BlockSpec((3, depth, cols), lambda i: (i, 0, 0))]
-        + [pl.BlockSpec(memory_space=pl.ANY)] * len(old),
-        out_specs=[wide, wide, pl.BlockSpec((cols, depth), lambda i: (skip + i, 0))],
+        in_specs=in_specs + [pl.BlockSpec(memory_space=pl.ANY)] * len(old),
+        out_specs=out_specs,
         out_shape=[jax.ShapeDtypeStruct(one, jnp.float32) for one in shapes],
-        input_output_aliases={1 + i: i for i in range(len(old))},
+        input_output_aliases={len(given) + i: i for i in range(len(old))},
         name="unpack",
-    )(blocks, *old)
+    )(*given, *old)
 
 
 def group_rows(lengths, group, begin, count):
@@ -1518,17 +1555,17 @@
     in_prompt = local_index < PROMPT
     start_row = jnp.where(in_prompt, 0, PROMPT + start)
     position = jnp.where(in_prompt, local_index, PROMPT + after_prompt - start)
+    return start_row, position
+
+
+def rotary(position):
     half = HEAD // 2
     frequency = jnp.exp(
         -math.log(rope_base) * (2.0 * jnp.arange(half, dtype=jnp.float32) / HEAD)
     )
     angles = position.astype(jnp.float32)[:, None] * frequency[None, :]
     cosine, sine = jnp.cos(angles), jnp.sin(angles)
-    return (
-        start_row,
-        jnp.concatenate([cosine, cosine], axis=1),
-        jnp.concatenate([sine, -sine], axis=1),
-    )
+    return jnp.concatenate([cosine, cosine], axis=1), jnp.concatenate([sine, -sine], axis=1)
 
 
 def fast_body(
@@ -1574,8 +1611,10 @@
     )
     normed_one, weights, lengths = tied(normed_one, weights, lengths)
     feed_one, weights = gather(early, weights)
-    _, own_cos, own_sin = group_rows(lengths, group, place * tok_rows, tok_rows)
-    start_rows = group_rows(lengths, group, 0, GROUP_LEN)[0].reshape(-1, 1, BLOCK)
+    own_cos, own_sin = rotary(group_rows(lengths, group, place * tok_rows, tok_rows)[1])
+    start_rows, positions = group_rows(lengths, group, 0, GROUP_LEN)
+    start_rows = start_rows.reshape(-1, 1, BLOCK)
+    positions = positions.astype(jnp.float32).reshape(-1, 1, BLOCK)
     sent = project(normed_one, weights, own_cos, own_sin)
     back, held, attended_head, lse, out_t = attend(
         sent, start_rows, weights, groups_here, col_count
@@ -1592,9 +1631,7 @@
         return lax.psum_scatter(part, "row", scatter_dimension=0, tiled=True)[0]
 
     grads_one, *sums = feed_all(*rows_two, feed_one, first, (), 3 * first)
-    lengths, sums[0] = tied(lengths, sums[0])
-    _, cosine, sine = lax.optimization_barrier(group_rows(lengths, group, 0, GROUP_LEN))
-    sums[0], grads_one, feed_two, cosine = tied(sums[0], grads_one, feed_two, cosine)
+    sums[0], grads_one, feed_two = tied(sums[0], grads_one, feed_two)
     grads_one = owned(grads_one)
     rest = tiles - first - 1
     blocks = 3 * (rest + 1) + part_width // tile
@@ -1607,14 +1644,13 @@
     grads = unpack(grads_one, 0, first, hidden_here, ())
     d_sent, *grads = tied(d_sent, *grads)
     d_raw, output = attend_back(
-        d_sent, held, attended_head, lse, start_rows, cosine, sine, ffn_pieces, middle, groups_here
+        d_sent, held, attended_head, lse, start_rows, positions, ffn_pieces, middle, groups_here
     )
     input_grad, own_grads = leave(
         d_raw, weights, unit_one_t, normed_one, unit_one, inverse_one, d_middle, groups_here, col_count
     )
     qkv_grad = own_grads.transpose(1, 0, 2)
-    grads = unpack(late, first, tiles - first, hidden_here, grads)
-    out_grad = late[3 * (rest + 1) :].transpose(0, 2, 1).reshape(part_width, depth).astype(jnp.float32)
+    *grads, out_grad = unpack(late, first, rest + 1, hidden_here, grads, part_width // tile)
     return (output, input_grad, qkv_grad, out_grad, *grads)
 
 

time: 879 us -> 878 us (level)
  other arithmetic: 19.2 us -> 6.46 us
  waiting for transfers between devices: 12.2 us -> 22.9 us
    all_gather x3, waiting for transfers between devices: 12.1 us -> 22.8 us  [gather(): return (lax.all_gather(shard, 'row'), after)]
  transfers between devices with their start and end apart: 5 -> 5, of which waited for: 2 -> 2; matrix products, arithmetic and copies ran while one was open for 3% -> 1% of each run, Pallas kernels for 90% -> 91%
where the time goes in v5:
time: 878 us; the launch traced here: 870 us
  Pallas kernels  792 us (90%)
  local copies, waits for them, and re-layouts  33.5 us (4%)
  waiting for transfers between devices  22.9 us (3%)
  between operations  14.6 us (2%)
    pallas_call x1, Pallas kernels, attend_back(): pl.pallas_call(functools.partial(attend_back_kernel, groups_here), in_spe...  188 us
    pallas_call x1, Pallas kernels, attend(): pl.pallas_call(functools.partial(attend_kernel, groups_here), in_specs=[h...  176 us
    pallas_call x2, Pallas kernels, feed_all(): pl.pallas_call(feed_all_kernel, grid=(tiles,), in_specs=[resident((rows,...  96.3 us
    pallas_call x1, Pallas kernels, feed_last(): pl.pallas_call(feed_last_kernel, in_specs=[hbm] * 7 + [vmem] * 2 + [hbm,...  92.8 us
    pallas_call x1, Pallas kernels, leave(): pl.pallas_call(functools.partial(leave_kernel, groups_here), in_specs=[vm...  86.7 us
    pallas_call x1, Pallas kernels, enter(): pl.pallas_call(enter_kernel, in_specs=[hbm, hbm], out_specs=[hbm, hbm, vm...  76 us
    pallas_call x1, Pallas kernels, branch(): pl.pallas_call(branch_kernel, in_specs=[hbm, vmem, vmem], out_specs=[vmem...  56.1 us
    unnamed x48, local copies, waits for them, and re-layouts  23.9 us
  transfers between devices with their start and end apart: 5, of which 2 were waited for; matrix products, arithmetic and copies ran while one was open for 1% of the time, Pallas kernels for 91%

profile of v5, /device:TPU:0, one launch (start us, length us, event | category | flops | bytes accessed | tf_op | source)
XLA Modules:
  0.0 870.0 jit_solution(9694567949175679227)
XLA Ops:
  8.5 2.2 pad_maximum_fusion
  11.8 1.6 maximum_bitcast_fusion
  14.9 76.0 %enter.1 = (bf16[4,1024,512]{2,1,0:T(8,128)(2,1)S(1)}, bf16[4,1024,512]{2,1,0:T(8,128)(2,1)S(1)}, bf16[1024,2048]{1,0:T(8,128)(2,1)}, bf16[2048,1024]{1,0:T(8,12...) custom-call(bf16[1024,512]{1,0:T(8,128)(2,1)S(1)} %copy-done.2, bf16[1024,512]{1,0:T(8,128)(2,1)S(1)} %copy-done.3), custom_call_target="tpu_custom_call" | custom-call | flops 20971520 | bytes 209715200 | tf_op jit(solution)/shard_map/enter/pallas_call | solution.py:688
  90.9 2.0 copy-done
  92.9 2.0 copy-done.7
  97.0 1.6 copy.35
  99.2 1.9 multiply_sine_fusion
  101.5 12.1 %project.1.sent_ref = bf16[4,3,1024,128]{3,2,1,0:T(8,128)(2,1)S(1)} custom-call(bf16[1024,2048]{1,0:T(8,128)(2,1)S(1)} %copy-done.6, bf16[8,4,256,512]{3,2,1,0:T(8,128)(2,1)} %bitcast.37, f32[1024,128]{1,0:T(8,128)S(1)} %get-tuple-element.132.cos_ref, f32[1024,128]{1,0:T(8,128)S(1)} %get-tuple-element.133.sin_ref), custom_call_target="tpu_custom_call" | custom-call | flops 6442450944 | bytes 6291456 | tf_op jit(solution)/shard_map/project/pallas_call | solution.py:747
  113.6 175.8 %attend.1 = (bf16[4,1024,128]{2,1,0:T(8,128)(2,1)S(1)}, bf16[3,4096,128]{2,1,0:T(8,128)(2,1)S(1)}, bf16[4096,128]{1,0:T(8,128)(2,1)S(1)}, f32[8,1,512]{2,1,0:T(1,128)S(1)}, bf16[4,8,256,512]{3,2,1,0:T(8,128)(2,1)S(1)}) custom-call(bf16[4,3,1024,128]{3,2,1,0:T(8,128)(2,1)S(1)} %project.1.sent_ref, s32[8,1,512]{2,1,0:T(1,128)S(1)} %get-tuple-element.128.start_ref, ...), custom_call_target="tpu_custom_call" | custom-call | flops 4294967296 | bytes 104857600 | tf_op jit(solution)/shard_map/attend/pallas_call | solution.py:375
  290.4 3.3 copy-done.11
  293.6 1.7 copy-done.12
  296.3 8.9 %all-gather.9.cloned.1.call-done = bf16[32,3,256,256]{3,2,1,0:T(8,128)(2,1)} async-done(((bf16[4,3,256,256]{3,2,1,0:T(8,128)(2,1)}), bf16[32,3,256,256]{3,2,1,0:T(8,128)(2,1)}) %all-gather.9.cloned.1.call-update) | async-done | bytes 12582928 | tf_op jit(solution)/shard_map/all_gather | solution.py:1598
  305.2 1.6 copy.37
  307.0 6.3 copy.36
  313.4 56.1 %branch.1 = (bf16[1024,2048]{1,0:T(8,128)(2,1)}, bf16[2048,1024]{1,0:T(8,128)(2,1)}, f32[1024,512]{1,0:T(8,128)}, f32[1024,512]{1,0:T(8,128)}, f32[1024,128]{1,0:T(8,128)}) custom-call(bf16[4,1024,128]{2,1,0:T(8,128)(2,1)} %copy-done.1, bf16[4,2048,512]{2,1,0:T(8,128)(2,1)} %bitcast.31, bf16[4,1024,512]{2,1,0:T(8,128)(2,1)} %copy-done.7), custom_call_target="tpu_custom_call" | custom-call | flops 8589934592 | bytes 167772160 | tf_op jit(solution)/shard_map/branch/pallas_call | solution.py:840
  369.5 51.4 %feed_all.2 = (bf16[8,12,256,256]{3,2,1,0:T(8,128)(2,1)}, f32[1024,2048]{1,0:T(8,128)}, f32[1024,2048]{1,0:T(8,128)}) custom-call(bf16[1024,2048]{1,0:T(8,128)(2,1)} %get-tuple-element.79.unit_ref.unit_hbm, bf16[2048,1024]{1,0:T(8,128)(2,1)} %get-tuple-element.80.unit_t_ref.unit_t_hbm, bf16[4,1024,512]{2,1,0:T(8,128)(2,1)} %copy-done, ...), custom_call_target="tpu_custom_call" | custom-call | flops 38654705664 | bytes 25165824 | tf_op jit(solution)/shard_map/feed_all/pallas_call | solution.py:1321
  420.9 13.9 %all-gather.11.cloned.1.call-done = bf16[32,3,256,256]{3,2,1,0:T(8,128)(2,1)} async-done(((bf16[4,3,256,256]{3,2,1,0:T(8,128)(2,1)}), bf16[32,3,256,256]{3,2,1,0:T(8,128)(2,1)}) %all-gather.11.cloned.1.call-update) | async-done | bytes 12582928 | tf_op jit(solution)/shard_map/all_gather | solution.py:1598
  434.8 44.9 %feed_all.3 = (bf16[8,14,256,256]{3,2,1,0:T(8,128)(2,1)}, f32[1024,2048]{1,0:T(8,128)}, f32[1024,2048]{1,0:T(8,128)}) custom-call(bf16[1024,2048]{1,0:T(8,128)(2,1)} %get-tuple-element.79.unit_ref.unit_hbm, bf16[2048,1024]{1,0:T(8,128)(2,1)} %get-tuple-element.80.unit_t_ref.unit_t_hbm, bf16[4,1024,512]{2,1,0:T(8,128)(2,1)} %copy-done, ...), custom_call_target="tpu_custom_call" | custom-call | flops 28991029248 | bytes 18874368 | tf_op jit(solution)/shard_map/feed_all/pallas_call | solution.py:1321
  479.7 92.8 %feed_last.1 = (bf16[8,14,256,256]{3,2,1,0:T(8,128)(2,1)}, bf16[4,1024,512]{2,1,0:T(8,128)(2,1)}, f32[1024,512]{1,0:T(8,128)}, bf16[4,1024,128]{2,1,0:T(8,128)(2,1)}) custom-call(bf16[1024,2048]{1,0:T(8,128)(2,1)} %get-tuple-element.79.unit_ref.unit_hbm, ...), custom_call_target="tpu_custom_call", output_to_operand_aliasing={{0}: (11, {})} | custom-call | flops 9663676416 | bytes 209715200 | tf_op jit(solution)/shard_map/feed_last/pallas_call | solution.py:1467
  572.6 4.0 unpack.2
  576.6 1.9 copy-done.15
  578.5 187.9 %attend_back.1 = (bf16[4,3,1024,128]{3,2,1,0:T(8,128)(2,1)}, bf16[1024,512]{1,0:T(8,128)(2,1)S(1)}) custom-call(bf16[4,1024,128]{2,1,0:T(8,128)(2,1)S(1)} %copy-done.9, bf16[3,4096,128]{2,1,0:T(8,128)(2,1)} %copy-done.12, bf16[4096,128]{1,0:T(8,128)(2,1)S(1)} %copy-done.14, f32[8,1,512]{2,1,0:T(1,128)S(1)} %get-tuple-element.106.lse_ref, ...), custom_call_target="tpu_custom_call" | custom-call | flops 10737418240 | bytes 104857600 | tf_op jit(solution)/shard_map/attend_back/pallas_call | solution.py:589
  767.4 86.7 %leave.1 = (f32[1024,512]{1,0:T(8,128)}, f32[3,256,512]{2,1,0:T(8,128)}) custom-call(bf16[4,3,1024,128]{3,2,1,0:T(8,128)(2,1)} %get-tuple-element.110.d_raw_ref, bf16[8,4,256,512]{3,2,1,0:T(8,128)(2,1)} %bitcast.40, bf16[2048,1024]{1,0:T(8,128)(2,1)} %get-tuple-element.111.unit_t_ref, bf16[1024,2048]{1,0:T(8,128)(2,1)} %get-tuple-element.68.unit_ref, ...), custom_call_target="tpu_custom_call" | custom-call | flops 12884901888 | bytes 209715200 | tf_op jit(solution)/shard_map/leave/pallas_call | solution.py:1174
  854.1 4.5 unpack.3
  (68 shorter events, 14.6 us)
Async XLA Ops:
  7.2 3.6 copy-start.18
  7.2 4.1 copy-start.19
  7.2 89.8 %all-gather.7.cloned.1.call-start = ((), (), s32[]{:S(2)}) async-start(), calls=%async_computation.4 | async-start | bytes 9437184 | tf_op jit(solution)/shard_map/all_gather | solution.py:1598
  10.7 294.5 %all-gather.9.cloned.1.call-start = ((), (), s32[]{:S(2)}) async-start(), calls=%async_computation.5 | async-start | bytes 14155776 | tf_op jit(solution)/shard_map/all_gather | solution.py:1598
  13.4 1.2 copy-start.2
  13.4 1.5 copy-start.3
  14.9 83.8 %copy-start.20 = (s32[2,8]{1,0:T(2,128)S(1)}, s32[2,8]{1,0:T(2,128)}, u32[]{:S(2)}) copy-start(s32[2,8]{1,0:T(2,128)} %param.10) | copy-start | bytes 196
  90.9 2.0 copy-start
  92.9 2.0 copy-start.7
  94.9 1.3 copy-start.8
  98.6 336.2 %all-gather.11.cloned.1.call-start = ((), (), s32[]{:S(2)}) async-start(), calls=%async_computation.6 | async-start | bytes 14155776 | tf_op jit(solution)/shard_map/all_gather | solution.py:1598
  98.9 2.5 copy-start.6
  289.4 1.0 copy-start.1
  290.4 3.3 copy-start.11
  293.6 1.7 copy-start.12
  306.8 265.8 %reduce-scatter.3.cloned.1.call-start = ((), (), s32[]{:S(2)}) async-start(), calls=%async_computation.2 | async-start | bytes 14155776 | tf_op jit(solution)/shard_map/reduce_scatter | solution.py:1631
  434.8 419.3 %reduce-scatter.5.cloned.1.call-start = ((), (), s32[]{:S(2)}) async-start(), calls=%async_computation.3 | async-start | bytes 16515072 | tf_op jit(solution)/shard_map/reduce_scatter | solution.py:1631
  572.6 4.0 copy-start.9
  572.6 4.0 copy-start.14
  576.6 1.9 copy-start.15
  766.4 1.0 copy-start.4
  854.1 4.5 copy-start.5
  858.6 2.0 copy-start.16
  858.6 3.3 copy-start.17
  (2 other events, 1.7 us)
Sparse Core Ops, SparseCore 0:
  10.8 84.7 all-gather.6
  98.7 206.4 all-gather.8
  307.4 127.2 all-gather.10
  436.9 127.4 reduce-scatter.2
  572.7 225.3 reduce-scatter.4
